TPU v7x, 256 devices: a whole 4x4x8 slice. The times are simulated.
256 devices in a mesh: group: 16 (over z, x_hi), expert: 16 (over x_lo, y, core).
Axes of the slice: x: 4 (x_hi: 2, x_lo: 2; x = x_hi * 2 + x_lo), y: 4, z: 8, core: 2. Of those that a mesh axis runs over, the one named last changes fastest.
Arguments:
- hidden_in: bfloat16 [16384, 2048], P(('group', 'expert')), may hold values from -54 to 54
- norm_attention: float32 [2048], replicated, may hold values from 0.5 to 1.5
- norm_experts: float32 [2048], replicated, may hold values from 0.5 to 1.5
- query_master: float32 [2048, 4096], P('group', 'expert'), may hold values from -0.125 to 0.125
- trainer_key_value_weight: float32 [2, 2048, 512], P(None, 'group'), may hold values from -0.125 to 0.125
- output_master: float32 [4096, 2048], P('expert', 'group'), may hold values from -0.09375 to 0.09375
- query_gain: float32 [128], replicated, may hold values from 0.5 to 1.5
- key_gain: float32 [128], replicated, may hold values from 0.5 to 1.5
- lengths: int32 [8], replicated, may hold values from 1 to 2048, as said below
- router: bfloat16 [2048, 128], replicated, may hold values from -0.125 to 0.125
- expert_gateup: bfloat16 [16, 2048, 1536], P('expert'), may hold values from -0.125 to 0.125
- expert_down: bfloat16 [16, 768, 2048], P('expert'), may hold values from -0.21875 to 0.21875
- routes: int32 [16384, 8], P(('group', 'expert')), may hold values from 0 to 127, as said below
Outputs:
- hidden: bfloat16 [16384, 2048], P(('group', 'expert'))
- expert_mix: bfloat16 [16384, 2048], P(('group', 'expert'))
Inputs may be any that keep to these rules, and one draw needn't show every extreme that they name: `lengths`: one request has exactly 2048 valid tokens. `routes`: A row's 8 experts are different, and at most one of them is below 16. In the 64 rows of one device, each expert below 16 is named by at most 4 rows; in every such block some expert is named by exactly 4 rows, and one expert is named by exactly 4 rows in every block.
All inputs are finite; a program needn't handle non-finite values.
Results may differ from a plain program's by a relative error of at most 0.02.
Values may be sent and summed in bfloat16 or wider, within the bound.
A program may use at most 64 MiB of HBM per device.

v0:
```python
import math

import jax
import jax.numpy as jnp
from jax import lax
from jax.sharding import PartitionSpec as P

QUERY_HEADS = 32
KEY_VALUE_HEADS = 4
HEAD_DIMENSION = 128


epsilon = 1e-06
rope_theta = 1000000.0


def from_partner(block, axis, stride):
    count = lax.axis_size(axis)
    route = []
    for low in range(count):
        high = low | 1 << stride
        if high != low and high < count:
            route += [(low, high), (high, low)]
    return lax.ppermute(block, axis, route)


def norm_rows(values, gain_vector):
    widened = values.astype(jnp.float32)
    inverse_rms = lax.rsqrt(jnp.mean(widened * widened, axis=-1, keepdims=True) + epsilon)
    return widened * inverse_rms * gain_vector


def rotate(values, positions):
    half_width = values.shape[-1] // 2
    exponents = jnp.arange(half_width).astype(jnp.float32)
    inverse = jnp.exp(exponents * (-2.0 * math.log(rope_theta) / values.shape[-1]))
    angles = positions[:, None, None] * inverse[None, None, :]
    cosine_values = jnp.cos(angles)
    sine_values = jnp.sin(angles)
    first_half = values[..., :half_width]
    second = values[..., half_width:]
    return jnp.concatenate(
        [
            first_half * cosine_values - second * sine_values,
            second * cosine_values + first_half * sine_values,
        ],
        axis=-1,
    )


def local_positions(parity, row_count):
    indices = jnp.arange(row_count)
    quarter = row_count // 2
    offset = jnp.where(parity == 0, jnp.where(indices < quarter, 0, 2 * quarter), quarter)
    return indices + offset


def per_device(
    hidden_in,
    norm_attention,
    norm_experts,
    query_master,
    trainer_key_value_weight,
    output_master,
    query_gain,
    key_gain,
    lengths,
    router,
    expert_gateup,
    expert_down,
    routes,
):
    experts_axis = lax.axis_size("expert")
    group_member = lax.axis_index("expert")
    group_index = lax.axis_index("group")
    local_head_count = QUERY_HEADS // experts_axis
    width_here = local_head_count * HEAD_DIMENSION
    common_head = group_member * local_head_count // (QUERY_HEADS // KEY_VALUE_HEADS)
    keyvalue_slice = lax.dynamic_slice_in_dim(
        trainer_key_value_weight, common_head * HEAD_DIMENSION, HEAD_DIMENSION, 2
    ).astype(jnp.bfloat16)
    query_full, keyvalue_full, output_part = (
        lax.all_gather(query_master.astype(jnp.bfloat16), "group", axis=0, tiled=True),
        lax.all_gather(keyvalue_slice, "group", axis=1, tiled=True),
        lax.all_gather(output_master.astype(jnp.bfloat16), "group", axis=1, tiled=True),
    )
    joined_weights = jnp.concatenate([query_full, keyvalue_full[0], keyvalue_full[1]], axis=1)
    normed = norm_rows(hidden_in, norm_attention).astype(jnp.bfloat16)
    projected = jnp.dot(
        lax.all_gather(normed, "expert", axis=0, tiled=True),
        joined_weights,
        preferred_element_type=jnp.float32,
    ).astype(jnp.bfloat16)
    local_rows = projected.shape[0]
    query_rows_list = projected[:, :width_here].reshape(
        local_rows, local_head_count, HEAD_DIMENSION
    )
    key_rows = projected[:, width_here : width_here + HEAD_DIMENSION]
    value_rows = projected[:, width_here + HEAD_DIMENSION :]
    parity = group_index % 2
    own_places = local_positions(parity, local_rows)
    partner_places = local_positions(1 - parity, local_rows)
    query_rows_list = rotate(
        norm_rows(query_rows_list, query_gain), own_places.astype(jnp.float32)
    ).astype(jnp.bfloat16)
    key_rows = rotate(norm_rows(key_rows[:, None, :], key_gain), own_places.astype(jnp.float32))[
        :, 0, :
    ].astype(jnp.bfloat16)
    partner = from_partner(jnp.stack([key_rows, value_rows]), "group", 0)
    all_keys = jnp.concatenate([key_rows, partner[0]], axis=0)
    all_values = jnp.concatenate([value_rows, partner[1]], axis=0)
    key_places = jnp.concatenate([own_places, partner_places])
    valid_length = jnp.sum(jnp.where(jnp.arange(lengths.shape[0]) == group_index // 2, lengths, 0))
    block_rows = min(512, local_rows)
    block_count = local_rows // block_rows
    score_scale = HEAD_DIMENSION ** (-0.5)

    def attend(block_index):
        block_start = block_index * block_rows
        query_block = lax.dynamic_slice_in_dim(query_rows_list, block_start, block_rows, 0)
        query_places = lax.dynamic_slice_in_dim(own_places, block_start, block_rows, 0)
        scores = (
            jnp.einsum("qhd,kd->hqk", query_block, all_keys, preferred_element_type=jnp.float32)
            * score_scale
        )
        allowed = (key_places[None, :] <= query_places[:, None]) & (
            key_places[None, :] < valid_length
        )
        weights = jnp.where(allowed[None], jnp.exp(scores), 0.0)
        denominators = jnp.sum(weights, axis=-1)
        weighted = jnp.einsum(
            "hqk,kd->qhd",
            weights.astype(jnp.bfloat16),
            all_values,
            preferred_element_type=jnp.float32,
        )
        return (weighted / jnp.transpose(denominators)[:, :, None]).astype(jnp.bfloat16)

    attended = lax.map(attend, jnp.arange(block_count)).reshape(local_rows, width_here)
    summed = lax.psum_scatter(
        jnp.dot(attended, output_part, preferred_element_type=jnp.float32).astype(jnp.bfloat16),
        "expert",
        scatter_dimension=0,
        tiled=True,
    ).astype(jnp.float32)
    hidden = (hidden_in.astype(jnp.float32) + summed).astype(jnp.bfloat16)
    normed_second = norm_rows(hidden, norm_experts).astype(jnp.bfloat16)
    logits = jnp.dot(normed_second, router, preferred_element_type=jnp.float32)
    route_table = routes[:, :, None] == jnp.arange(logits.shape[1])[None, None, :]
    picked = jnp.sum(jnp.where(route_table, logits[:, None, :], 0.0), axis=-1)
    raised = jnp.exp(picked)
    gate_values = raised / jnp.sum(raised, axis=1, keepdims=True)
    inside = routes < experts_axis
    gate_window = jnp.sum(jnp.where(inside, gate_values, 0.0), axis=1)
    expert_window = jnp.sum(jnp.where(inside, routes, 0), axis=1)
    present = jnp.any(inside, axis=1)
    capacity = local_rows // (experts_axis * experts_axis)
    member_table = (
        present[:, None] & (expert_window[:, None] == jnp.arange(experts_axis)[None, :])
    ).astype(jnp.int32)
    ranking = jnp.sum(jnp.cumsum(member_table, axis=0) * member_table, axis=1) - 1
    slot_index = expert_window * capacity + ranking
    select = (
        (jnp.arange(experts_axis * capacity)[:, None] == slot_index[None, :]) & present[None, :]
    ).astype(jnp.bfloat16)
    model_width = normed_second.shape[1]
    outgoing = (
        jnp.dot(select, normed_second, preferred_element_type=jnp.float32)
        .astype(jnp.bfloat16)
        .reshape(experts_axis, capacity, model_width)
    )
    gateup_here = expert_gateup[0]
    down_here = expert_down[0]
    hidden_units = down_here.shape[0]
    slot_items = lax.all_to_all(outgoing, "expert", split_axis=0, concat_axis=0, tiled=True)
    flattened = slot_items.reshape(-1, slot_items.shape[-1])
    gate_up = jnp.dot(flattened, gateup_here, preferred_element_type=jnp.float32)
    active = (jax.nn.silu(gate_up[:, :hidden_units]) * gate_up[:, hidden_units:]).astype(
        jnp.bfloat16
    )
    result = (
        jnp.dot(active, down_here, preferred_element_type=jnp.float32)
        .astype(jnp.bfloat16)
        .reshape(slot_items.shape)
    )
    returned = lax.all_to_all(result, "expert", split_axis=0, concat_axis=0, tiled=True)
    combined = jnp.dot(
        jnp.transpose(select), returned.reshape(-1, model_width), preferred_element_type=jnp.float32
    )
    expert_mix = (gate_window[:, None] * combined).astype(jnp.bfloat16)
    return (hidden, expert_mix)


def solution(mesh):
    return jax.shard_map(
        per_device,
        mesh=mesh,
        in_specs=(
            P(("group", "expert"), None),
            P(),
            P(),
            P("group", "expert"),
            P(None, "group", None),
            P("expert", "group"),
            P(),
            P(),
            P(),
            P(),
            P("expert", None, None),
            P("expert", None, None),
            P(("group", "expert"), None),
        ),
        out_specs=(P(("group", "expert"), None), P(("group", "expert"), None)),
        check_vma=False,
    )
```

profile of v0, /device:TPU:1, one launch (start us, length us, event | category | flops | bytes accessed | tf_op | source)
XLA Modules:
  0.0 400.9 jit_solution(13658261090532443639)
XLA Ops:
  7.2 1.7 dynamic-slice_convert_fusion
  9.0 1.5 convert_element_type.103
  10.6 1.1 fusion.36
  11.7 1.8 fusion.38
  13.6 1.5 convert_element_type.114
  15.3 3.1 multiply_cosine_fusion
  18.4 1.4 fusion.68
  19.7 69.8 %all-gather.9.cloned.1.call-done = bf16[2,2048,128]{2,1,0:T(8,128)(2,1)} async-done(((bf16[2,128,128]{2,1,0:T(8,128)(2,1)}), bf16[2,2048,128]{2,1,0:T(8,128)(2,1)}) %all-gather.9.cloned.1.call-update) | async-done | bytes 1048592 | tf_op jit(solution)/shard_map/all_gather | solution.py:84
  89.6 2.3 slice_bitcast_fusion.1
  91.9 75.7 %all-gather.7.cloned.1.call-done = bf16[2048,256]{1,0:T(8,128)(2,1)} async-done(((bf16[128,256]{1,0:T(8,128)(2,1)}), bf16[2048,256]{1,0:T(8,128)(2,1)}) %all-gather.7.cloned.1.call-update) | async-done | bytes 1048592 | tf_op jit(solution)/shard_map/all_gather | solution.py:83
  167.6 43.1 %all-gather.5.cloned.1.call-done = bf16[1024,2048]{1,0:T(8,128)(2,1)} async-done(((bf16[64,2048]{1,0:T(8,128)(2,1)}), bf16[1024,2048]{1,0:T(8,128)(2,1)}) %all-gather.5.cloned.1.call-update) | async-done | bytes 4194320 | tf_op jit(solution)/shard_map/all_gather | solution.py:90
  210.7 5.2 %fusion.27 = bf16[1024,512]{0,1:T(8,128)(2,1)S(1)} fusion(bf16[1024,2048]{1,0:T(8,128)(2,1)} %all-gather.5.cloned.1.call-done, bf16[2048,128]{1,0:T(8,128)(2,1)} %get-tuple-element.104, bf16[2048,128]{1,0:T(8,128)(2,1)} %get-tuple-element.103, bf16[2048,256]{1,0:T(8,128)(2,1)} %all-gather.7.cloned.1.call-done), kind=kOutput, calls=%fused_computation.34 | convolution fusion | flops 2154299392 | bytes 7340032 | tf_op jit(solution)/shard_map/dot_general | solution.py:89
  216.0 0.8 slice.54
  216.8 0.1 multiply_reduce_fusion
  217.1 1.2 fusion.46
  218.2 0.7 fusion.55
  219.0 0.9 pad_maximum_fusion.1
  219.8 2.4 collective-permute-start
  222.3 2.2 copy.24
  224.5 1.6 multiply_multiply_fusion
  226.1 1.7 subtract_convert_fusion
  227.8 1.1 pad_maximum_fusion
  228.9 6.7 %collective-permute-done = bf16[2,1024,128]{1,2,0:T(8,128)(2,1)} collective-permute-done((bf16[2,1024,128]{1,2,0:T(8,128)(2,1)}, bf16[2,1024,128]{1,2,0:T(8,128)(2,1)}, u32[]{:S(2)}, u32[]{:S(2)}) %collective-permute-start) | collective-permute-done | bytes 524320 | tf_op jit(solution)/shard_map/ppermute | solution.py:24
  235.6 1.1 slice_bitcast_fusion.2
  236.7 1.1 pad_maximum_fusion.2
  237.8 2.1 copy.25
  239.8 2.1 copy.26
  241.9 19.4 %while.10 = (s32[]{:T(128)}, bf16[2,512,2,128]{3,2,1,0:T(2,128)(2,1)}, s32[2048]{0:T(1024)S(1)}, s32[2]{0:T(128)S(1)}, s32[1024]{0:T(1024)S(1)}, /*index=5*/s32[...) while((s32[]{:T(128)}, ...), condition=%wide.region_6.7_spmd, body=%wide.region_4.6_spmd.sunk | while | flops 1088685056 | bytes 24152800 | solution.py:139
  241.9 0.6 dynamic_slice.23
  243.2 0.7 broadcast_compare_fusion.3
  243.9 0.7 compare_and_fusion.2
  244.6 3.9 bitcast_reduce_fusion.2
  248.5 2.0 fusion.82
  250.6 1.0 copy_dynamic-update-slice_fusion.2
  251.6 0.6 dynamic_slice.23
  252.9 0.7 broadcast_compare_fusion.3
  253.6 0.7 compare_and_fusion.2
  254.3 3.9 bitcast_reduce_fusion.2
  258.2 2.0 fusion.82
  260.3 1.0 copy_dynamic-update-slice_fusion.2
  261.3 24.7 %all-gather.11.cloned.1.call-done = bf16[256,2048]{1,0:T(8,128)(2,1)} async-done(((bf16[256,128]{1,0:T(8,128)(2,1)}), bf16[256,2048]{1,0:T(8,128)(2,1)}) %all-gather.11.cloned.1.call-update) | async-done | bytes 1048592 | tf_op jit(solution)/shard_map/all_gather | solution.py:85
  286.0 4.6 %convolution_convert_fusion = bf16[1024,2048]{1,0:T(8,128)(2,1)} fusion(bf16[256,2048]{1,0:T(8,128)(2,1)} %all-gather.11.cloned.1.call-done, bf16[128,8,2,128]{3,2,1,0:T(2,128)(2,1)} %bitcast.20), kind=kOutput, calls=%fused_computation.21 | convolution fusion | flops 1075838976 | bytes 5767168 | tf_op jit(solution)/shard_map/dot_general | solution.py:141
  290.7 0.1 fusion.71
  290.8 0.1 select_reduce_fusion.2
  291.1 0.2 select_reduce_fusion.1
  291.3 64.7 %reduce-scatter.2.cloned.1.call-done = bf16[64,2048]{1,0:T(8,128)(2,1)} async-done(((bf16[1024,2048]{1,0:T(8,128)(2,1)}), bf16[64,2048]{1,0:T(8,128)(2,1)}) %reduce-scatter.2.cloned.1.call-update) | async-done | bytes 262160 | tf_op jit(solution)/shard_map/reduce_scatter | solution.py:140
  356.0 1.1 fusion.33
  357.2 0.7 copy-done.2
  357.9 0.3 convolution_convert_fusion.1
  358.2 0.8 reshape.264
  359.0 7.5 %all-to-all-start = ((bf16[16,4,2048]{2,1,0:T(4,128)(2,1)}), bf16[16,4,2048]{2,1,0:T(4,128)(2,1)S(1)}, u32[]{:S(2)}, u32[]{:S(2)}) async-start(bf16[16,4,2048]{2,1,0:T(4,128)(2,1)} %reshape.264), calls=%async_computation.1 | async-start | bytes 524288 | tf_op jit(solution)/shard_map/all_to_all | solution.py:175
  366.5 1.4 fusion.52
  367.9 5.8 %all-to-all-done = bf16[16,4,2048]{2,1,0:T(4,128)(2,1)S(1)} async-done(((bf16[16,4,2048]{2,1,0:T(4,128)(2,1)}), bf16[16,4,2048]{2,1,0:T(4,128)(2,1)S(1)}, u32[]{:S(2)}, u32[]{:S(2)}) %all-to-all-start) | async-done | bytes 262176 | tf_op jit(solution)/shard_map/all_to_all | solution.py:175
  373.8 0.8 reshape.265
  374.5 4.0 %fusion.13 = f32[64,1536]{1,0:T(8,128)S(1)} fusion(bf16[64,2048]{1,0:T(8,128)(2,1)} %reshape.265, bf16[1,2048,1536]{2,1,0:T(8,128)(2,1)} %param.25), kind=kOutput, calls=%fused_computation.19 | convolution fusion | flops 402653184 | bytes 6946816 | tf_op jit(solution)/shard_map/dot_general | solution.py:177
  378.6 0.7 fusion.18
  379.3 0.8 reshape.266
  380.1 4.9 %all-to-all-start.1 = ((bf16[16,4,2048]{2,1,0:T(4,128)(2,1)}), bf16[16,4,2048]{2,1,0:T(4,128)(2,1)}, u32[]{:S(2)}, u32[]{:S(2)}) async-start(bf16[16,4,2048]{2,1,0:T(4,128)(2,1)} %reshape.266), calls=%async_computation.2 | async-start | bytes 524288 | tf_op jit(solution)/shard_map/all_to_all | solution.py:186
  385.0 0.2 select_reduce_fusion
  385.2 0.1 exponential_reduce_fusion
  385.3 0.2 select_reduce_fusion.3
  385.5 6.8 %all-to-all-done.1 = bf16[16,4,2048]{2,1,0:T(4,128)(2,1)} async-done(((bf16[16,4,2048]{2,1,0:T(4,128)(2,1)}), bf16[16,4,2048]{2,1,0:T(4,128)(2,1)}, u32[]{:S(2)}, u32[]{:S(2)}) %all-to-all-start.1) | async-done | bytes 262176 | tf_op jit(solution)/shard_map/all_to_all | solution.py:186
  392.3 1.0 reshape.267
  393.4 1.0 fusion.17
  (48 shorter events, 1.0 us)
Async XLA Ops:
  7.2 371.4 %copy-start = (bf16[1,768,2048]{2,1,0:T(8,128)(2,1)S(1)}, bf16[1,768,2048]{2,1,0:T(8,128)(2,1)}, u32[]{:S(2)}) copy-start(bf16[1,768,2048]{2,1,0:T(8,128)(2,1)} %param.26) | copy-start | bytes 9437188
  7.2 82.4 %all-gather.9.cloned.1.call-start = ((), (), s32[]{:S(2)}) async-start(), calls=%async_computation.5 | async-start | bytes 1114112 | tf_op jit(solution)/shard_map/all_gather | solution.py:84
  9.0 158.6 %all-gather.7.cloned.1.call-start = ((), (), s32[]{:S(2)}) async-start(), calls=%async_computation.4 | async-start | bytes 1114112 | tf_op jit(solution)/shard_map/all_gather | solution.py:83
  10.6 200.1 %all-gather.5.cloned.1.call-start = ((), (), s32[]{:S(2)}) async-start(), calls=%async_computation.3 | async-start | bytes 4456448 | tf_op jit(solution)/shard_map/all_gather | solution.py:90
  13.5 272.4 %all-gather.11.cloned.1.call-start = ((), (), s32[]{:S(2)}) async-start(), calls=%async_computation.6 | async-start | bytes 1114112 | tf_op jit(solution)/shard_map/all_gather | solution.py:85
  15.2 340.9 %reduce-scatter.2.cloned.1.call-start = ((), (), s32[]{:S(2)}) async-start(), calls=%async_computation.7 | async-start | bytes 4456448 | tf_op jit(solution)/shard_map/reduce_scatter | solution.py:140
  210.6 6.3 %copy-start.8 = (f32[128]{0:T(128)S(1)}, f32[128]{0:T(128)}, u32[]{:S(2)}) copy-start(f32[128]{0:T(128)} %param.22) | copy-start | bytes 1540
  215.8 8.7 %copy-start.7 = (f32[128]{0:T(128)S(1)}, f32[128]{0:T(128)}, u32[]{:S(2)}) copy-start(f32[128]{0:T(128)} %param.21) | copy-start | bytes 1540
  219.8 15.8 %collective-permute-start = (bf16[2,1024,128]{1,2,0:T(8,128)(2,1)}, bf16[2,1024,128]{1,2,0:T(8,128)(2,1)}, u32[]{:S(2)}, u32[]{:S(2)}) collective-permute-start(bf16[2,1024,128]{1,2,0:T(8,128)(2,1)} %pad_maximum_fusion.1), channel_id=1, source_target_pairs={{0,16},{16,0},{32,48},{48,32},{64,80},{80,64},{96,112},{112,96},{1... | collective-permute-start | bytes 1572872 | tf_op jit(solution)/shard_map/ppermute | solution.py:24
  224.5 12.2 %copy-start.3 = (bf16[1024,128]{0,1:T(8,128)(2,1)S(1)}, bf16[1024,128]{0,1:T(8,128)(2,1)}, u32[]{:S(2)}) copy-start(bf16[1024,128]{0,1:T(8,128)(2,1)} %get-tuple-element.109) | copy-start | bytes 786436
  244.6 3.9 copy-start.4
  254.3 3.9 copy-start.4
  286.0 4.6 %copy-start.6 = (s32[64,8]{0,1:T(8,128)S(1)}, s32[64,8]{0,1:T(8,128)}, u32[]{:S(2)}) copy-start(s32[64,8]{0,1:T(8,128)} %param.27) | copy-start | bytes 6148
  290.6 65.5 %copy-start.1 = (bf16[64,2048]{1,0:T(8,128)(2,1)S(1)}, bf16[64,2048]{1,0:T(8,128)(2,1)}, u32[]{:S(2)}) copy-start(bf16[64,2048]{1,0:T(8,128)(2,1)} %param.15) | copy-start | bytes 786436
  290.6 67.3 %copy-start.5 = (f32[2048]{0:T(1024)S(1)}, f32[2048]{0:T(1024)}, u32[]{:S(2)}) copy-start(f32[2048]{0:T(1024)} %param.17) | copy-start | bytes 24580
  357.2 0.7 copy-start.2
  359.0 14.8 %all-to-all-start = ((bf16[16,4,2048]{2,1,0:T(4,128)(2,1)}), bf16[16,4,2048]{2,1,0:T(4,128)(2,1)S(1)}, u32[]{:S(2)}, u32[]{:S(2)}) async-start(bf16[16,4,2048]{2,1,0:T(4,128)(2,1)} %reshape.264), calls=%async_computation.1 | async-start | bytes 524288 | tf_op jit(solution)/shard_map/all_to_all | solution.py:175
  380.1 12.3 %all-to-all-start.1 = ((bf16[16,4,2048]{2,1,0:T(4,128)(2,1)}), bf16[16,4,2048]{2,1,0:T(4,128)(2,1)}, u32[]{:S(2)}, u32[]{:S(2)}) async-start(bf16[16,4,2048]{2,1,0:T(4,128)(2,1)} %reshape.266), calls=%async_computation.2 | async-start | bytes 524288 | tf_op jit(solution)/shard_map/all_to_all | solution.py:186
Sparse Core Ops, SparseCore 0:
  10.6 78.9 all-gather.8
  92.1 75.3 all-gather.6
  170.0 40.6 all-gather.4
  213.5 72.3 all-gather.10
  290.7 65.2 reduce-scatter.1
where the time goes:
time: 402 us; the launch traced here: 401 us
  waiting for transfers between devices  297 us (74%)
  matrix products  29 us (7%)
  other arithmetic  24.1 us (6%)
  local copies, waits for them, and re-layouts  19.8 us (5%)
  starting transfers between devices  15.1 us (4%)
  between operations  14.1 us (4%)
    all_gather x1, waiting for transfers between devices, per_device(): lax.all_gather(query_master.astype(jnp.bfloat16), 'group', axis=0, tiled=...  75.7 us
    all_gather x1, waiting for transfers between devices, per_device(): lax.all_gather(keyvalue_slice, 'group', axis=1, tiled=True)  69.8 us
    reduce_scatter x1, waiting for transfers between devices, per_device(): lax.psum_scatter(jnp.dot(attended, output_part, preferred_element_type=jn...  64.7 us
    all_gather x1, waiting for transfers between devices, per_device(): lax.all_gather(normed, 'expert', axis=0, tiled=True)  43.1 us
    all_gather x1, waiting for transfers between devices, per_device(): lax.all_gather(output_master.astype(jnp.bfloat16), 'group', axis=1, tiled...  24.7 us
  transfers between devices with their start and end apart: 8, of which 8 were waited for; matrix products, arithmetic and copies ran while one was open for 14% of the time, Pallas kernels for 0%

commit v1 on v0

--- a/solution.py
+++ b/solution.py
@@ -1,9 +1,14 @@
+import functools
 import math
 
 import jax
 import jax.numpy as jnp
 from jax import lax
+from jax.experimental import pallas as pl
+from jax.experimental.pallas import tpu as pltpu
 from jax.sharding import PartitionSpec as P
+
+MESH = pl.DeviceIdType.MESH
 
 QUERY_HEADS = 32
 KEY_VALUE_HEADS = 4
@@ -22,6 +27,112 @@
         if high != low and high < count:
             route += [(low, high), (high, low)]
     return lax.ppermute(block, axis, route)
+
+
+def gather_kernel(n_group, n_expert, wq, wk, wv, wo, xn, oq, ok, ov, oo, oxn, send, recv, local):
+    g = lax.axis_index("group")
+    e = lax.axis_index("expert")
+    barrier = pltpu.get_barrier_semaphore()
+    for j in range(1, n_group):
+        pl.semaphore_signal(barrier, 1, device_id=(lax.rem(g + j, n_group), e), device_id_type=MESH)
+    for j in range(1, n_expert):
+        pl.semaphore_signal(barrier, 1, device_id=(g, lax.rem(e + j, n_expert)), device_id_type=MESH)
+    pl.semaphore_wait(barrier, n_group - 1 + n_expert - 1)
+    copies = []
+    for j in range(1, n_expert):
+        copy = pltpu.make_async_remote_copy(
+            src_ref=xn,
+            dst_ref=oxn.at[e],
+            send_sem=send.at[4, j],
+            recv_sem=recv.at[4, j],
+            device_id=(g, lax.rem(e + j, n_expert)),
+            device_id_type=MESH,
+        )
+        copy.start()
+        copies.append(copy)
+    pieces = [(wq, oq), (wk, ok), (wv, ov), (wo, oo)]
+    for j in range(1, n_group):
+        for k, (src, dst) in enumerate(pieces):
+            copy = pltpu.make_async_remote_copy(
+                src_ref=src,
+                dst_ref=dst.at[g],
+                send_sem=send.at[k, j],
+                recv_sem=recv.at[k, j],
+                device_id=(lax.rem(g + j, n_group), e),
+                device_id_type=MESH,
+            )
+            copy.start()
+            copies.append(copy)
+    own = [pltpu.make_async_copy(xn, oxn.at[e], local.at[4])]
+    own += [pltpu.make_async_copy(src, dst.at[g], local.at[k]) for k, (src, dst) in enumerate(pieces)]
+    for copy in own:
+        copy.start()
+    for copy in copies:
+        copy.wait()
+    for copy in own:
+        copy.wait()
+
+
+def gather_all(wq, wk, wv, wo, xn, n_group, n_expert):
+    any_spec = pl.BlockSpec(memory_space=pl.ANY)
+    shapes = [
+        jax.ShapeDtypeStruct((n_group,) + a.shape, a.dtype) for a in (wq, wk, wv, wo)
+    ] + [jax.ShapeDtypeStruct((n_expert,) + xn.shape, xn.dtype)]
+    return pl.pallas_call(
+        functools.partial(gather_kernel, n_group, n_expert),
+        out_shape=tuple(shapes),
+        in_specs=[any_spec] * 5,
+        out_specs=tuple([any_spec] * 5),
+        scratch_shapes=[
+            pltpu.SemaphoreType.DMA((5, max(n_group, n_expert))),
+            pltpu.SemaphoreType.DMA((5, max(n_group, n_expert))),
+            pltpu.SemaphoreType.DMA((5,)),
+        ],
+        compiler_params=pltpu.CompilerParams(collective_id=0, has_side_effects=True),
+    )(wq, wk, wv, wo, xn)
+
+
+def scatter_kernel(n_expert, part, out, send, recv, local):
+    g = lax.axis_index("group")
+    e = lax.axis_index("expert")
+    barrier = pltpu.get_barrier_semaphore()
+    for j in range(1, n_expert):
+        pl.semaphore_signal(barrier, 1, device_id=(g, lax.rem(e + j, n_expert)), device_id_type=MESH)
+    pl.semaphore_wait(barrier, n_expert - 1)
+    copies = []
+    for j in range(1, n_expert):
+        peer = lax.rem(e + j, n_expert)
+        copy = pltpu.make_async_remote_copy(
+            src_ref=part.at[peer],
+            dst_ref=out.at[e],
+            send_sem=send.at[j],
+            recv_sem=recv.at[j],
+            device_id=(g, peer),
+            device_id_type=MESH,
+        )
+        copy.start()
+        copies.append(copy)
+    own = pltpu.make_async_copy(part.at[e], out.at[e], local.at[0])
+    own.start()
+    for copy in copies:
+        copy.wait()
+    own.wait()
+
+
+def scatter_blocks(part, n_expert):
+    any_spec = pl.BlockSpec(memory_space=pl.ANY)
+    return pl.pallas_call(
+        functools.partial(scatter_kernel, n_expert),
+        out_shape=jax.ShapeDtypeStruct(part.shape, part.dtype),
+        in_specs=[any_spec],
+        out_specs=any_spec,
+        scratch_shapes=[
+            pltpu.SemaphoreType.DMA((n_expert,)),
+            pltpu.SemaphoreType.DMA((n_expert,)),
+            pltpu.SemaphoreType.DMA((1,)),
+        ],
+        compiler_params=pltpu.CompilerParams(collective_id=1, has_side_effects=True),
+    )(part)
 
 
 def norm_rows(values, gain_vector):
@@ -76,18 +187,31 @@
     local_head_count = QUERY_HEADS // experts_axis
     width_here = local_head_count * HEAD_DIMENSION
     common_head = group_member * local_head_count // (QUERY_HEADS // KEY_VALUE_HEADS)
+    groups_axis = lax.axis_size("group")
     keyvalue_slice = lax.dynamic_slice_in_dim(
         trainer_key_value_weight, common_head * HEAD_DIMENSION, HEAD_DIMENSION, 2
     ).astype(jnp.bfloat16)
-    query_full, keyvalue_full, output_part = (
-        lax.all_gather(query_master.astype(jnp.bfloat16), "group", axis=0, tiled=True),
-        lax.all_gather(keyvalue_slice, "group", axis=1, tiled=True),
-        lax.all_gather(output_master.astype(jnp.bfloat16), "group", axis=1, tiled=True),
-    )
-    joined_weights = jnp.concatenate([query_full, keyvalue_full[0], keyvalue_full[1]], axis=1)
     normed = norm_rows(hidden_in, norm_attention).astype(jnp.bfloat16)
+    query_parts, key_parts, value_parts, output_parts, normed_parts = gather_all(
+        query_master.astype(jnp.bfloat16),
+        keyvalue_slice[0],
+        keyvalue_slice[1],
+        output_master.astype(jnp.bfloat16),
+        normed,
+        groups_axis,
+        experts_axis,
+    )
+    model_width = hidden_in.shape[1]
+    joined_weights = jnp.concatenate(
+        [
+            query_parts.reshape(model_width, -1),
+            key_parts.reshape(model_width, -1),
+            value_parts.reshape(model_width, -1),
+        ],
+        axis=1,
+    )
     projected = jnp.dot(
-        lax.all_gather(normed, "expert", axis=0, tiled=True),
+        normed_parts.reshape(-1, model_width),
         joined_weights,
         preferred_element_type=jnp.float32,
     ).astype(jnp.bfloat16)
@@ -137,12 +261,11 @@
         return (weighted / jnp.transpose(denominators)[:, :, None]).astype(jnp.bfloat16)
 
     attended = lax.map(attend, jnp.arange(block_count)).reshape(local_rows, width_here)
-    summed = lax.psum_scatter(
-        jnp.dot(attended, output_part, preferred_element_type=jnp.float32).astype(jnp.bfloat16),
-        "expert",
-        scatter_dimension=0,
-        tiled=True,
-    ).astype(jnp.float32)
+    head_partials = jnp.einsum(
+        "tk,gkn->tgn", attended, output_parts, preferred_element_type=jnp.float32
+    ).astype(jnp.bfloat16)
+    owned = scatter_blocks(head_partials.reshape(experts_axis, -1, model_width), experts_axis)
+    summed = jnp.sum(owned.astype(jnp.float32), axis=0)
     hidden = (hidden_in.astype(jnp.float32) + summed).astype(jnp.bfloat16)
     normed_second = norm_rows(hidden, norm_experts).astype(jnp.bfloat16)
     logits = jnp.dot(normed_second, router, preferred_element_type=jnp.float32)
@@ -163,7 +286,6 @@
     select = (
         (jnp.arange(experts_axis * capacity)[:, None] == slot_index[None, :]) & present[None, :]
     ).astype(jnp.bfloat16)
-    model_width = normed_second.shape[1]
     outgoing = (
         jnp.dot(select, normed_second, preferred_element_type=jnp.float32)
         .astype(jnp.bfloat16)

time: 402 us -> 295 us (0.73)
  waiting for transfers between devices: 297 us -> 13.4 us
  Pallas kernels: 0 us -> 166 us
  local copies, waits for them, and re-layouts: 19.8 us -> 37.2 us
  between operations: 14.1 us -> 0.96 us
  other arithmetic: 24.1 us -> 28.8 us
    all_gather x4 -> x0, waiting for transfers between devices: 213 us -> none  [the longest x1 75.7 us: per_device(): lax.all_gather(query_master.astype(jnp.bfloat16), 'group', axis=0, tiled=...]
    pallas_call x0 -> x2, Pallas kernels: none -> 166 us  [the longest x1 101 us: gather_all(): pl.pallas_call(functools.partial(gather_kernel, n_group, n_expert), out_s...]
    reduce_scatter x1 -> x0, waiting for transfers between devices: 64.7 us -> none  [per_device(): lax.psum_scatter(jnp.dot(attended, output_part, preferred_element_type=jn...]
    reshape x0 -> x2, local copies, waits for them, and re-layouts: none -> 9.48 us  [the longest x1 7.31 us: per_device(): head_partials.reshape(experts_axis, -1, model_width)]
    ppermute x1, waiting for transfers between devices: 6.69 us -> 0.62 us  [from_partner(): return lax.ppermute(block, axis, route)]
    convert_element_type x0 -> x1, local copies, waits for them, and re-layouts: none -> 4.67 us  [per_device(): head_partials = jnp.einsum('tk,gkn->tgn', attended, output_parts, preferr...]
  transfers between devices with their start and end apart: 8 -> 3, of which waited for: 8 -> 3; matrix products, arithmetic and copies ran while one was open for 14% -> 5% of each run, Pallas kernels for 0% -> 0%
where the time goes in v1:
time: 295 us; the launch traced here: 291 us
  Pallas kernels  166 us (56%)
  local copies, waits for them, and re-layouts  37.2 us (13%)
  other arithmetic  28.8 us (10%)
  matrix products  28.4 us (10%)
  starting transfers between devices  14.9 us (5%)
  waiting for transfers between devices  13.4 us (5%)
    pallas_call x1, Pallas kernels, gather_all(): pl.pallas_call(functools.partial(gather_kernel, n_group, n_expert), out_s...  101 us
    pallas_call x1, Pallas kernels, scatter_blocks(): pl.pallas_call(functools.partial(scatter_kernel, n_expert), out_shape=jax...  65.2 us
    all_to_all x1, starting transfers between devices, per_device(): lax.all_to_all(outgoing, 'expert', split_axis=0, concat_axis=0, tiled=True)  10 us
    dot_general x2, matrix products, attend(): jnp.einsum('qhd,kd->hqk', query_block, all_keys, preferred_element_type=j...  7.78 us
    reshape x1, local copies, waits for them, and re-layouts, per_device(): head_partials.reshape(experts_axis, -1, model_width)  7.31 us
    all_to_all x1, waiting for transfers between devices, per_device(): lax.all_to_all(result, 'expert', split_axis=0, concat_axis=0, tiled=True)  6.81 us
    all_to_all x1, waiting for transfers between devices, per_device(): lax.all_to_all(outgoing, 'expert', split_axis=0, concat_axis=0, tiled=True)  5.96 us
  transfers between devices with their start and end apart: 3, of which 3 were waited for; matrix products, arithmetic and copies ran while one was open for 5% of the time, Pallas kernels for 0%

profile of v1, /device:TPU:1, one launch (start us, length us, event | category | flops | bytes accessed | tf_op | source)
XLA Modules:
  0.0 290.9 jit_solution(16044121860371660046)
XLA Ops:
  0.7 1.1 dynamic-slice_convert_fusion
  1.8 0.6 slice_bitcast_fusion.2
  2.4 1.1 fusion.36
  3.5 1.6 convert_element_type.102.wq
  5.1 1.5 convert_element_type.104.wo
  6.6 1.8 fusion.38.xn
  8.4 100.5 %shard_map.140 = (bf16[16,128,256]{2,1,0:T(8,128)(2,1)}, bf16[16,128,128]{2,1,0:T(8,128)(2,1)}, bf16[16,128,128]{2,1,0:T(8,128)(2,1)}, bf16[16,256,128]{2,1,0:T(8,128)(2,1)}, bf16[16,64,2048]{2,1,0:T(8,128)(2,1)}) custom-call(bf16[128,256]{1,0:T(8,128)(2,1)} %convert_element_type.102.wq, bf16[128,128]{1,0:T(8,128)(2,1)} %get-tuple-element.120.wk, ...), custom_call_target="tpu_custom_call" | custom-call | tf_op jit(solution)/shard_map/pallas_call | solution.py:81
  108.9 5.2 %fusion.27 = bf16[1024,512]{0,1:T(8,128)(2,1)S(1)} fusion(bf16[1024,2048]{1,0:T(8,128)(2,1)} %bitcast.86, bf16[2048,128]{1,0:T(8,128)(2,1)} %bitcast.89, bf16[2048,128]{1,0:T(8,128)(2,1)} %bitcast.88, bf16[2048,256]{1,0:T(8,128)(2,1)} %bitcast.87), kind=kOutput, calls=%fused_computation.35 | convolution fusion | flops 2154299392 | bytes 7340032 | tf_op jit(solution)/shard_map/dot_general | solution.py:213
  114.2 0.9 copy-done.1
  115.1 0.8 fusion.71
  115.9 1.1 fusion.32
  117.0 1.2 fusion.44
  118.2 0.7 fusion.53
  118.9 1.8 pad_maximum_fusion.1
  120.8 1.9 slice.54
  122.6 0.1 multiply_reduce_fusion
  122.8 3.1 %multiply_cosine_fusion = (f32[1024,64]{1,0:T(8,128)}, f32[1024,64]{1,0:T(8,128)}) fusion(f32[64]{0:T(128)S(1)} %multiply_exponential_fusion, f32[1024]{0:T(1024)S(1)} %get-tuple-element.124), kind=kLoop, calls=%fused_computation.44 | loop fusion | flops 65536 | bytes 528640 | tf_op jit(solution)/shard_map/cos | solution.py:149
  126.2 2.2 copy.26
  128.7 1.6 multiply_multiply_fusion
  130.2 1.7 subtract_convert_fusion
  131.9 0.6 fusion.66
  132.5 0.2 select_reduce_fusion.1
  132.7 1.1 pad_maximum_fusion
  133.8 0.6 collective-permute-done
  134.4 1.8 slice_bitcast_fusion
  136.2 0.8 pad_maximum_fusion.3
  137.0 2.1 copy.28
  139.1 1.9 pad_maximum_fusion.2
  141.0 2.1 copy.27
  143.0 19.3 %while.10 = (s32[]{:T(128)}, bf16[2,512,2,128]{3,2,1,0:T(2,128)(2,1)}, s32[2048]{0:T(1024)S(1)}, s32[2]{0:T(128)S(1)}, s32[1024]{0:T(1024)S(1)}, /*index=5*/s32[...) while((s32[]{:T(128)}, ...), condition=%wide.region_6.7_spmd, body=%wide.region_4.6_spmd.sunk | while | flops 1088685056 | bytes 24152800 | solution.py:263
  143.0 0.6 dynamic_slice.23
  144.4 0.6 broadcast_compare_fusion.3
  145.0 0.7 compare_and_fusion.2
  145.7 3.9 %bitcast_reduce_fusion.2 = (f32[2,512]{1,0:T(2,128)S(1)}, f32[512,2,2048]{2,0,1:T(8,128)S(1)}) fusion(pred[512,2048]{1,0:T(8,128)(4,1)S(1)} %compare_and_fusion.2, bf16[2048,128]{1,0:T(8,128)(2,1)} %get-tuple-element.217, bf16[1024,2,128]{2,0,1:T(8,128)(2,1)} %get-tuple-element.216, s32[]{:T(128)S(6)} %select_n.131), kind=kOutput, calls=%fused_computation.clone.1 | convolution fusion | flops 543161344 | bytes 10227716 | tf_op jit(solution)/shard_map/while/body/eval_jaxpr/qhd,kd->hqk/dot_general | solution.py:247
  149.6 2.0 fusion.81
  151.7 1.0 copy_dynamic-update-slice_fusion.2
  152.7 0.6 dynamic_slice.23
  154.0 0.6 broadcast_compare_fusion.3
  154.6 0.7 compare_and_fusion.2
  155.4 3.9 %bitcast_reduce_fusion.2 = (f32[2,512]{1,0:T(2,128)S(1)}, f32[512,2,2048]{2,0,1:T(8,128)S(1)}) fusion(pred[512,2048]{1,0:T(8,128)(4,1)S(1)} %compare_and_fusion.2, bf16[2048,128]{1,0:T(8,128)(2,1)} %get-tuple-element.217, bf16[1024,2,128]{2,0,1:T(8,128)(2,1)} %get-tuple-element.216, s32[]{:T(128)S(6)} %select_n.131), kind=kOutput, calls=%fused_computation.clone.1 | convolution fusion | flops 543161344 | bytes 10227716 | tf_op jit(solution)/shard_map/while/body/eval_jaxpr/qhd,kd->hqk/dot_general | solution.py:247
  159.3 2.0 fusion.81
  161.4 1.0 copy_dynamic-update-slice_fusion.2
  162.4 2.2 reshape.291
  164.5 2.6 convolution_convert_fusion
  167.2 4.7 %copy.30 = bf16[1024,16,128]{2,1,0:T(8,128)(2,1)} copy(bf16[1024,16,128]{2,0,1:T(8,128)(2,1)S(1)} %convolution_convert_fusion) | data formatting | bytes 8388608 | tf_op jit(solution)/shard_map/convert_element_type | solution.py:266
  171.8 7.3 %reshape.283.part = bf16[16,64,2048]{2,1,0:T(8,128)(2,1)} reshape(bf16[1024,16,128]{2,1,0:T(8,128)(2,1)} %copy.30) | data formatting | bytes 8388608 | tf_op jit(solution)/shard_map/reshape | solution.py:267
  179.2 65.2 %shard_map.141 = bf16[16,64,2048]{2,1,0:T(8,128)(2,1)} custom-call(bf16[16,64,2048]{2,1,0:T(8,128)(2,1)} %reshape.283.part), custom_call_target="tpu_custom_call" | custom-call | tf_op jit(solution)/shard_map/pallas_call | solution.py:124
  244.4 3.0 %convert_reduce_fusion = f32[64,2048]{1,0:T(8,128)S(1)} fusion(bf16[16,64,2048]{2,1,0:T(8,128)(2,1)} %shard_map.141), kind=kLoop, calls=%fused_computation.19 | loop fusion | flops 4063232 | bytes 4718592 | tf_op jit(solution)/shard_map/reduce_sum | solution.py:268
  247.5 0.2 fusion.33
  247.7 1.0 convolution_convert_fusion.1
  248.7 1.8 reshape.284
  250.5 10.0 %all-to-all-start = ((bf16[16,4,2048]{2,1,0:T(4,128)(2,1)}), bf16[16,4,2048]{2,1,0:T(4,128)(2,1)}, u32[]{:S(2)}, u32[]{:S(2)}) async-start(bf16[16,4,2048]{2,1,0:T(4,128)(2,1)} %reshape.284), calls=%async_computation | async-start | bytes 524288 | tf_op jit(solution)/shard_map/all_to_all | solution.py:297
  260.5 1.3 fusion.50
  261.8 6.0 %all-to-all-done = bf16[16,4,2048]{2,1,0:T(4,128)(2,1)} async-done(((bf16[16,4,2048]{2,1,0:T(4,128)(2,1)}), bf16[16,4,2048]{2,1,0:T(4,128)(2,1)}, u32[]{:S(2)}, u32[]{:S(2)}) %all-to-all-start) | async-done | bytes 262176 | tf_op jit(solution)/shard_map/all_to_all | solution.py:297
  267.8 1.7 reshape.285
  269.5 4.0 %fusion.13 = f32[64,1536]{1,0:T(8,128)S(1)} fusion(bf16[64,2048]{1,0:T(8,128)(2,1)} %reshape.285, bf16[1,2048,1536]{2,1,0:T(8,128)(2,1)} %param.25), kind=kOutput, calls=%fused_computation.20 | convolution fusion | flops 402653184 | bytes 6946816 | tf_op jit(solution)/shard_map/dot_general | solution.py:299
  273.5 1.4 fusion.18
  274.9 1.8 reshape.286
  276.7 4.9 %all-to-all-start.1 = ((bf16[16,4,2048]{2,1,0:T(4,128)(2,1)}), bf16[16,4,2048]{2,1,0:T(4,128)(2,1)}, u32[]{:S(2)}, u32[]{:S(2)}) async-start(bf16[16,4,2048]{2,1,0:T(4,128)(2,1)} %reshape.286), calls=%async_computation.1 | async-start | bytes 524288 | tf_op jit(solution)/shard_map/all_to_all | solution.py:308
  281.6 0.2 select_reduce_fusion
  281.9 0.2 select_reduce_fusion.3
  282.1 6.8 %all-to-all-done.1 = bf16[16,4,2048]{2,1,0:T(4,128)(2,1)} async-done(((bf16[16,4,2048]{2,1,0:T(4,128)(2,1)}), bf16[16,4,2048]{2,1,0:T(4,128)(2,1)}, u32[]{:S(2)}, u32[]{:S(2)}) %all-to-all-start.1) | async-done | bytes 262176 | tf_op jit(solution)/shard_map/all_to_all | solution.py:308
  288.9 1.0 reshape.287
  289.9 1.0 fusion.17
  (44 shorter events, 0.9 us)
Async XLA Ops:
  0.6 272.9 %copy-start = (bf16[1,768,2048]{2,1,0:T(8,128)(2,1)S(1)}, bf16[1,768,2048]{2,1,0:T(8,128)(2,1)}, u32[]{:S(2)}) copy-start(bf16[1,768,2048]{2,1,0:T(8,128)(2,1)} %param.26) | copy-start | bytes 9437188
  108.9 7.0 %copy-start.9 = (f32[128]{0:T(128)S(1)}, f32[128]{0:T(128)}, u32[]{:S(2)}) copy-start(f32[128]{0:T(128)} %param.22) | copy-start | bytes 1540
  114.1 1.0 copy-start.1
  114.1 11.7 %copy-start.7 = (s32[64,8]{0,1:T(8,128)S(1)}, s32[64,8]{0,1:T(8,128)}, u32[]{:S(2)}) copy-start(s32[64,8]{0,1:T(8,128)} %param.27) | copy-start | bytes 6148
  115.1 13.5 %copy-start.8 = (f32[128]{0:T(128)S(1)}, f32[128]{0:T(128)}, u32[]{:S(2)}) copy-start(f32[128]{0:T(128)} %param.21) | copy-start | bytes 1540
  115.9 6.8 %copy-start.2 = (bf16[1024,512]{0,1:T(8,128)(2,1)S(1)}, bf16[1024,512]{0,1:T(8,128)(2,1)}, u32[]{:S(2)}) copy-start(bf16[1024,512]{0,1:T(8,128)(2,1)} %copy-done.1) | copy-start | bytes 3145732
  120.8 13.7 %collective-permute-start = (bf16[2,1024,128]{1,2,0:T(8,128)(2,1)}, bf16[2,1024,128]{1,2,0:T(8,128)(2,1)}, u32[]{:S(2)}, u32[]{:S(2)}) collective-permute-start(bf16[2,1024,128]{1,2,0:T(8,128)(2,1)} %pad_maximum_fusion.1), channel_id=1, source_target_pairs={{0,16},{16,0},{32,48},{48,32},{64,80},{80,64},{96,112},{112,96},{1... | collective-permute-start | bytes 1572872 | tf_op jit(solution)/shard_map/ppermute | solution.py:29
  125.8 6.0 %copy-start.10 = (s32[8]{0:T(128)S(1)}, s32[8]{0:T(128)}, u32[]{:S(2)}) copy-start(s32[8]{0:T(128)} %param.23) | copy-start | bytes 100
  145.7 3.9 %copy-start.5 = (bf16[2048,128]{1,0:T(8,128)(2,1)S(1)}, bf16[2048,128]{1,0:T(8,128)(2,1)}, u32[]{:S(2)}) copy-start(bf16[2048,128]{1,0:T(8,128)(2,1)} %get-tuple-element.218) | copy-start | bytes 1572868 | tf_op jit(solution)/shard_map/while
  155.4 3.9 %copy-start.5 = (bf16[2048,128]{1,0:T(8,128)(2,1)S(1)}, bf16[2048,128]{1,0:T(8,128)(2,1)}, u32[]{:S(2)}) copy-start(bf16[2048,128]{1,0:T(8,128)(2,1)} %get-tuple-element.218) | copy-start | bytes 1572868 | tf_op jit(solution)/shard_map/while
  244.4 3.1 %copy-start.3 = (bf16[64,2048]{1,0:T(8,128)(2,1)S(1)}, bf16[64,2048]{1,0:T(8,128)(2,1)}, u32[]{:S(2)}) copy-start(bf16[64,2048]{1,0:T(8,128)(2,1)} %param.15) | copy-start | bytes 786436
  244.4 3.3 %copy-start.6 = (f32[2048]{0:T(1024)S(1)}, f32[2048]{0:T(1024)}, u32[]{:S(2)}) copy-start(f32[2048]{0:T(1024)} %param.17) | copy-start | bytes 24580
  247.7 25.9 %copy-start.4 = (bf16[64,2048]{1,0:T(8,128)(2,1)}, bf16[64,2048]{1,0:T(8,128)(2,1)S(1)}, u32[]{:S(2)}) copy-start(bf16[64,2048]{1,0:T(8,128)(2,1)S(1)} %get-tuple-element.106) | copy-start | bytes 786436
  250.5 17.3 %all-to-all-start = ((bf16[16,4,2048]{2,1,0:T(4,128)(2,1)}), bf16[16,4,2048]{2,1,0:T(4,128)(2,1)}, u32[]{:S(2)}, u32[]{:S(2)}) async-start(bf16[16,4,2048]{2,1,0:T(4,128)(2,1)} %reshape.284), calls=%async_computation | async-start | bytes 524288 | tf_op jit(solution)/shard_map/all_to_all | solution.py:297
  276.7 12.2 %all-to-all-start.1 = ((bf16[16,4,2048]{2,1,0:T(4,128)(2,1)}), bf16[16,4,2048]{2,1,0:T(4,128)(2,1)}, u32[]{:S(2)}, u32[]{:S(2)}) async-start(bf16[16,4,2048]{2,1,0:T(4,128)(2,1)} %reshape.286), calls=%async_computation.1 | async-start | bytes 524288 | tf_op jit(solution)/shard_map/all_to_all | solution.py:308

commit v2 on v1

--- a/solution.py
+++ b/solution.py
@@ -51,11 +51,18 @@
         copy.start()
         copies.append(copy)
     pieces = [(wq, oq), (wk, ok), (wv, ov), (wo, oo)]
+    width = wo.shape[1]
+
+    def slot(dst, k):
+        if k == 3:
+            return dst.at[:, pl.ds(pl.multiple_of(g * width, width), width)]
+        return dst.at[g]
+
     for j in range(1, n_group):
         for k, (src, dst) in enumerate(pieces):
             copy = pltpu.make_async_remote_copy(
                 src_ref=src,
-                dst_ref=dst.at[g],
+                dst_ref=slot(dst, k),
                 send_sem=send.at[k, j],
                 recv_sem=recv.at[k, j],
                 device_id=(lax.rem(g + j, n_group), e),
@@ -64,7 +71,7 @@
             copy.start()
             copies.append(copy)
     own = [pltpu.make_async_copy(xn, oxn.at[e], local.at[4])]
-    own += [pltpu.make_async_copy(src, dst.at[g], local.at[k]) for k, (src, dst) in enumerate(pieces)]
+    own += [pltpu.make_async_copy(src, slot(dst, k), local.at[k]) for k, (src, dst) in enumerate(pieces)]
     for copy in own:
         copy.start()
     for copy in copies:
@@ -75,9 +82,9 @@
 
 def gather_all(wq, wk, wv, wo, xn, n_group, n_expert):
     any_spec = pl.BlockSpec(memory_space=pl.ANY)
-    shapes = [
-        jax.ShapeDtypeStruct((n_group,) + a.shape, a.dtype) for a in (wq, wk, wv, wo)
-    ] + [jax.ShapeDtypeStruct((n_expert,) + xn.shape, xn.dtype)]
+    shapes = [jax.ShapeDtypeStruct((n_group,) + a.shape, a.dtype) for a in (wq, wk, wv)]
+    shapes += [jax.ShapeDtypeStruct((wo.shape[0], n_group * wo.shape[1]), wo.dtype)]
+    shapes += [jax.ShapeDtypeStruct((n_expert,) + xn.shape, xn.dtype)]
     return pl.pallas_call(
         functools.partial(gather_kernel, n_group, n_expert),
         out_shape=tuple(shapes),
@@ -119,7 +126,7 @@
     own.wait()
 
 
-def scatter_blocks(part, n_expert):
+def scatter_blocks(part, n_expert, collective_id):
     any_spec = pl.BlockSpec(memory_space=pl.ANY)
     return pl.pallas_call(
         functools.partial(scatter_kernel, n_expert),
@@ -131,7 +138,7 @@
             pltpu.SemaphoreType.DMA((n_expert,)),
             pltpu.SemaphoreType.DMA((1,)),
         ],
-        compiler_params=pltpu.CompilerParams(collective_id=1, has_side_effects=True),
+        compiler_params=pltpu.CompilerParams(collective_id=collective_id, has_side_effects=True),
     )(part)
 
 
@@ -261,10 +268,10 @@
         return (weighted / jnp.transpose(denominators)[:, :, None]).astype(jnp.bfloat16)
 
     attended = lax.map(attend, jnp.arange(block_count)).reshape(local_rows, width_here)
-    head_partials = jnp.einsum(
-        "tk,gkn->tgn", attended, output_parts, preferred_element_type=jnp.float32
-    ).astype(jnp.bfloat16)
-    owned = scatter_blocks(head_partials.reshape(experts_axis, -1, model_width), experts_axis)
+    head_partials = jnp.dot(
+        attended, output_parts, preferred_element_type=jnp.float32
+    ).astype(jnp.bfloat16)
+    owned = scatter_blocks(head_partials.reshape(experts_axis, -1, model_width), experts_axis, 1)
     summed = jnp.sum(owned.astype(jnp.float32), axis=0)
     hidden = (hidden_in.astype(jnp.float32) + summed).astype(jnp.bfloat16)
     normed_second = norm_rows(hidden, norm_experts).astype(jnp.bfloat16)
@@ -294,7 +301,7 @@
     gateup_here = expert_gateup[0]
     down_here = expert_down[0]
     hidden_units = down_here.shape[0]
-    slot_items = lax.all_to_all(outgoing, "expert", split_axis=0, concat_axis=0, tiled=True)
+    slot_items = scatter_blocks(outgoing, experts_axis, 2)
     flattened = slot_items.reshape(-1, slot_items.shape[-1])
     gate_up = jnp.dot(flattened, gateup_here, preferred_element_type=jnp.float32)
     active = (jax.nn.silu(gate_up[:, :hidden_units]) * gate_up[:, hidden_units:]).astype(
@@ -305,7 +312,7 @@
         .astype(jnp.bfloat16)
         .reshape(slot_items.shape)
     )
-    returned = lax.all_to_all(result, "expert", split_axis=0, concat_axis=0, tiled=True)
+    returned = scatter_blocks(result, experts_axis, 3)
     combined = jnp.dot(
         jnp.transpose(select), returned.reshape(-1, model_width), preferred_element_type=jnp.float32
     )

time: 295 us -> 275 us (0.932)
  Pallas kernels: 166 us -> 188 us
  starting transfers between devices: 14.9 us -> 0.01 us
  local copies, waits for them, and re-layouts: 37.2 us -> 23 us
  waiting for transfers between devices: 13.4 us -> 0.65 us
    pallas_call x1 -> x3, Pallas kernels: 65.2 us -> 87.7 us  [scatter_blocks(): pl.pallas_call(functools.partial(scatter_kernel, n_expert), out_shape=jax...]
    all_to_all x2 -> x0, starting transfers between devices: 14.9 us -> none  [the longest x1 10 us: per_device(): lax.all_to_all(outgoing, 'expert', split_axis=0, concat_axis=0, tiled=True)]
    all_to_all x2 -> x0, waiting for transfers between devices: 12.8 us -> none  [the longest x1 6.81 us: per_device(): lax.all_to_all(result, 'expert', split_axis=0, concat_axis=0, tiled=True)]
    reshape x2 -> x0, local copies, waits for them, and re-layouts: 9.48 us -> none  [the longest x1 7.31 us: per_device(): head_partials.reshape(experts_axis, -1, model_width)]
    convert_element_type x1 -> x0, local copies, waits for them, and re-layouts: 4.67 us -> none  [per_device(): head_partials = jnp.einsum('tk,gkn->tgn', attended, output_parts, preferr...]
  transfers between devices with their start and end apart: 3 -> 1, of which waited for: 3 -> 1; matrix products, arithmetic and copies ran while one was open for 5% -> 5% of each run, Pallas kernels for 0% -> 0%
where the time goes in v2:
time: 275 us; the launch traced here: 273 us
  Pallas kernels  188 us (68%)
  matrix products  29.3 us (11%)
  other arithmetic  28.9 us (11%)
  local copies, waits for them, and re-layouts  23 us (8%)
    pallas_call x1, Pallas kernels, gather_all(): pl.pallas_call(functools.partial(gather_kernel, n_group, n_expert), out_s...  101 us
    pallas_call x3, Pallas kernels, scatter_blocks(): pl.pallas_call(functools.partial(scatter_kernel, n_expert), out_shape=jax...  87.7 us
    dot_general x2, matrix products, attend(): jnp.einsum('qhd,kd->hqk', query_block, all_keys, preferred_element_type=j...  7.79 us
  transfers between devices with their start and end apart: 1, of which 1 were waited for; matrix products, arithmetic and copies ran while one was open for 5% of the time, Pallas kernels for 0%

profile of v2, /device:TPU:1, one launch (start us, length us, event | category | flops | bytes accessed | tf_op | source)
XLA Modules:
  0.0 272.5 jit_solution(17957011255470621853)
XLA Ops:
  0.7 1.1 dynamic-slice_convert_fusion
  1.8 0.6 slice_bitcast_fusion.2
  2.4 1.1 fusion.36
  3.5 1.6 convert_element_type.102.wq
  5.1 1.5 convert_element_type.104.wo
  6.6 1.8 fusion.38.xn
  8.4 100.5 %shard_map.140 = (bf16[16,128,256]{2,1,0:T(8,128)(2,1)}, bf16[16,128,128]{2,1,0:T(8,128)(2,1)}, bf16[16,128,128]{2,1,0:T(8,128)(2,1)}, bf16[256,2048]{1,0:T(8,128)(2,1)}, bf16[16,64,2048]{2,1,0:T(8,128)(2,1)}) custom-call(bf16[128,256]{1,0:T(8,128)(2,1)} %convert_element_type.102.wq, bf16[128,128]{1,0:T(8,128)(2,1)} %get-tuple-element.120.wk, ...), custom_call_target="tpu_custom_call" | custom-call | tf_op jit(solution)/shard_map/pallas_call | solution.py:88
  108.9 5.2 %fusion.27 = bf16[1024,512]{0,1:T(8,128)(2,1)S(1)} fusion(bf16[1024,2048]{1,0:T(8,128)(2,1)} %bitcast.92, bf16[2048,128]{1,0:T(8,128)(2,1)} %bitcast.95, bf16[2048,128]{1,0:T(8,128)(2,1)} %bitcast.94, bf16[2048,256]{1,0:T(8,128)(2,1)} %bitcast.93), kind=kOutput, calls=%fused_computation.35 | convolution fusion | flops 2154299392 | bytes 7340032 | tf_op jit(solution)/shard_map/dot_general | solution.py:220
  114.2 0.9 copy-done.1
  115.1 0.8 fusion.73
  115.9 1.1 fusion.32
  117.0 1.2 fusion.46
  118.2 0.7 fusion.55
  118.9 1.8 pad_maximum_fusion.1
  120.8 1.9 slice.54
  122.6 0.1 multiply_reduce_fusion
  122.8 3.1 %multiply_cosine_fusion = (f32[1024,64]{1,0:T(8,128)}, f32[1024,64]{1,0:T(8,128)}) fusion(f32[64]{0:T(128)S(1)} %multiply_exponential_fusion, f32[1024]{0:T(1024)S(1)} %get-tuple-element.124), kind=kLoop, calls=%fused_computation.44 | loop fusion | flops 65536 | bytes 528640 | tf_op jit(solution)/shard_map/cos | solution.py:156
  125.8 0.1 copy.28
  125.9 0.1 fusion.71
  126.0 0.1 select_reduce_fusion.2
  126.1 2.2 copy.24
  128.5 0.1 reduce_window_sum.11
  128.6 1.6 multiply_multiply_fusion
  130.2 1.7 subtract_convert_fusion
  131.9 0.6 fusion.68
  132.5 0.2 select_reduce_fusion.1
  132.7 1.1 pad_maximum_fusion
  133.8 0.6 collective-permute-done
  134.4 1.8 slice_bitcast_fusion
  136.2 0.9 pad_maximum_fusion.3
  137.1 2.1 copy.26
  139.1 1.9 pad_maximum_fusion.2
  141.0 2.1 copy.25
  143.1 19.3 %while.10 = (s32[]{:T(128)}, bf16[2,512,2,128]{3,2,1,0:T(2,128)(2,1)}, s32[2048]{0:T(1024)S(1)}, s32[2]{0:T(128)S(1)}, s32[1024]{0:T(1024)S(1)}, /*index=5*/s32[...) while((s32[]{:T(128)}, ...), condition=%wide.region_6.7_spmd, body=%wide.region_4.6_spmd.sunk | while | flops 1088685056 | bytes 24152800 | solution.py:270
  143.1 0.6 dynamic_slice.23
  144.4 0.6 broadcast_compare_fusion.3
  145.0 0.7 compare_and_fusion.2
  145.8 3.9 %bitcast_reduce_fusion.2 = (f32[2,512]{1,0:T(2,128)S(1)}, f32[512,2,2048]{2,0,1:T(8,128)S(1)}) fusion(pred[512,2048]{1,0:T(8,128)(4,1)S(1)} %compare_and_fusion.2, bf16[2048,128]{1,0:T(8,128)(2,1)} %get-tuple-element.217, bf16[1024,2,128]{2,0,1:T(8,128)(2,1)} %get-tuple-element.216, s32[]{:T(128)S(6)} %select_n.131), kind=kOutput, calls=%fused_computation.clone.1 | convolution fusion | flops 543161344 | bytes 10227716 | tf_op jit(solution)/shard_map/while/body/eval_jaxpr/qhd,kd->hqk/dot_general | solution.py:254
  149.7 2.0 fusion.82
  151.7 1.0 copy_dynamic-update-slice_fusion.2
  152.7 0.6 dynamic_slice.23
  154.0 0.6 broadcast_compare_fusion.3
  154.7 0.7 compare_and_fusion.2
  155.4 3.9 %bitcast_reduce_fusion.2 = (f32[2,512]{1,0:T(2,128)S(1)}, f32[512,2,2048]{2,0,1:T(8,128)S(1)}) fusion(pred[512,2048]{1,0:T(8,128)(4,1)S(1)} %compare_and_fusion.2, bf16[2048,128]{1,0:T(8,128)(2,1)} %get-tuple-element.217, bf16[1024,2,128]{2,0,1:T(8,128)(2,1)} %get-tuple-element.216, s32[]{:T(128)S(6)} %select_n.131), kind=kOutput, calls=%fused_computation.clone.1 | convolution fusion | flops 543161344 | bytes 10227716 | tf_op jit(solution)/shard_map/while/body/eval_jaxpr/qhd,kd->hqk/dot_general | solution.py:254
  159.3 2.0 fusion.82
  161.4 1.0 copy_dynamic-update-slice_fusion.2
  162.4 4.6 %convolution_convert_fusion = bf16[1024,2048]{1,0:T(8,128)(2,1)} fusion(bf16[256,2048]{1,0:T(8,128)(2,1)} %get-tuple-element.59, bf16[128,8,2,128]{3,2,1,0:T(2,128)(2,1)} %bitcast.25), kind=kOutput, calls=%fused_computation.22 | convolution fusion | flops 1075838976 | bytes 5767168 | tf_op jit(solution)/shard_map/dot_general | solution.py:271
  167.0 65.2 %shard_map.141 = bf16[16,64,2048]{2,1,0:T(8,128)(2,1)} custom-call(bf16[16,64,2048]{2,1,0:T(8,128)(2,1)} %bitcast.90), custom_call_target="tpu_custom_call" | custom-call | tf_op jit(solution)/shard_map/pallas_call | solution.py:131
  232.2 3.1 %convert_reduce_fusion = f32[64,2048]{1,0:T(8,128)S(1)} fusion(bf16[16,64,2048]{2,1,0:T(8,128)(2,1)} %shard_map.141), kind=kLoop, calls=%fused_computation.19 | loop fusion | flops 4063232 | bytes 4718592 | tf_op jit(solution)/shard_map/reduce_sum | solution.py:275
  235.3 0.2 fusion.33
  235.5 0.3 fusion.52
  235.8 0.2 select_reduce_fusion
  236.1 0.1 exponential_reduce_fusion
  236.2 0.2 select_reduce_fusion.3
  236.4 1.0 convolution_convert_fusion.1
  237.4 1.7 reshape.284.part
  239.1 13.7 %shard_map.142 = bf16[16,4,2048]{2,1,0:T(4,128)(2,1)} custom-call(bf16[16,4,2048]{2,1,0:T(4,128)(2,1)} %reshape.284.part), custom_call_target="tpu_custom_call" | custom-call | tf_op jit(solution)/shard_map/pallas_call | solution.py:131
  252.8 1.7 reshape.285
  254.5 4.0 %fusion.13 = f32[64,1536]{1,0:T(8,128)S(1)} fusion(bf16[64,2048]{1,0:T(8,128)(2,1)} %reshape.285, bf16[1,2048,1536]{2,1,0:T(8,128)(2,1)} %param.25), kind=kOutput, calls=%fused_computation.20 | convolution fusion | flops 402653184 | bytes 6946816 | tf_op jit(solution)/shard_map/dot_general | solution.py:306
  258.6 1.4 fusion.18
  259.9 1.7 reshape.286.part
  261.7 8.8 %shard_map.143 = bf16[16,4,2048]{2,1,0:T(4,128)(2,1)} custom-call(bf16[16,4,2048]{2,1,0:T(4,128)(2,1)} %reshape.286.part), custom_call_target="tpu_custom_call" | custom-call | tf_op jit(solution)/shard_map/pallas_call | solution.py:131
  270.5 1.0 reshape.287
  271.5 1.0 fusion.17
  (41 shorter events, 0.4 us)
Async XLA Ops:
  0.6 257.9 %copy-start = (bf16[1,768,2048]{2,1,0:T(8,128)(2,1)S(1)}, bf16[1,768,2048]{2,1,0:T(8,128)(2,1)}, u32[]{:S(2)}) copy-start(bf16[1,768,2048]{2,1,0:T(8,128)(2,1)} %param.26) | copy-start | bytes 9437188
  108.9 7.0 %copy-start.10 = (f32[128]{0:T(128)S(1)}, f32[128]{0:T(128)}, u32[]{:S(2)}) copy-start(f32[128]{0:T(128)} %param.22) | copy-start | bytes 1540
  114.1 1.0 copy-start.1
  114.1 11.7 %copy-start.8 = (s32[64,8]{0,1:T(8,128)S(1)}, s32[64,8]{0,1:T(8,128)}, u32[]{:S(2)}) copy-start(s32[64,8]{0,1:T(8,128)} %param.27) | copy-start | bytes 6148
  115.1 13.5 %copy-start.9 = (f32[128]{0:T(128)S(1)}, f32[128]{0:T(128)}, u32[]{:S(2)}) copy-start(f32[128]{0:T(128)} %param.21) | copy-start | bytes 1540
  115.9 6.8 %copy-start.2 = (bf16[1024,512]{0,1:T(8,128)(2,1)S(1)}, bf16[1024,512]{0,1:T(8,128)(2,1)}, u32[]{:S(2)}) copy-start(bf16[1024,512]{0,1:T(8,128)(2,1)} %copy-done.1) | copy-start | bytes 3145732
  120.8 13.7 %collective-permute-start = (bf16[2,1024,128]{1,2,0:T(8,128)(2,1)}, bf16[2,1024,128]{1,2,0:T(8,128)(2,1)}, u32[]{:S(2)}, u32[]{:S(2)}) collective-permute-start(bf16[2,1024,128]{1,2,0:T(8,128)(2,1)} %pad_maximum_fusion.1), channel_id=1, source_target_pairs={{0,16},{16,0},{32,48},{48,32},{64,80},{80,64},{96,112},{112,96},{1... | collective-permute-start | bytes 1572872 | tf_op jit(solution)/shard_map/ppermute | solution.py:29
  125.8 6.0 %copy-start.11 = (s32[8]{0:T(128)S(1)}, s32[8]{0:T(128)}, u32[]{:S(2)}) copy-start(s32[8]{0:T(128)} %param.23) | copy-start | bytes 100
  145.8 3.9 %copy-start.6 = (bf16[2048,128]{1,0:T(8,128)(2,1)S(1)}, bf16[2048,128]{1,0:T(8,128)(2,1)}, u32[]{:S(2)}) copy-start(bf16[2048,128]{1,0:T(8,128)(2,1)} %get-tuple-element.218) | copy-start | bytes 1572868 | tf_op jit(solution)/shard_map/while
  155.4 3.9 %copy-start.6 = (bf16[2048,128]{1,0:T(8,128)(2,1)S(1)}, bf16[2048,128]{1,0:T(8,128)(2,1)}, u32[]{:S(2)}) copy-start(bf16[2048,128]{1,0:T(8,128)(2,1)} %get-tuple-element.218) | copy-start | bytes 1572868 | tf_op jit(solution)/shard_map/while
  232.2 3.1 %copy-start.3 = (bf16[64,2048]{1,0:T(8,128)(2,1)S(1)}, bf16[64,2048]{1,0:T(8,128)(2,1)}, u32[]{:S(2)}) copy-start(bf16[64,2048]{1,0:T(8,128)(2,1)} %param.15) | copy-start | bytes 786436
  232.2 3.3 %copy-start.5 = (bf16[2048,128]{1,0:T(8,128)(2,1)S(1)}, bf16[2048,128]{1,0:T(8,128)(2,1)}, u32[]{:S(2)}) copy-start(bf16[2048,128]{1,0:T(8,128)(2,1)} %param.24) | copy-start | bytes 1572868
  232.2 3.3 %copy-start.7 = (f32[2048]{0:T(1024)S(1)}, f32[2048]{0:T(1024)}, u32[]{:S(2)}) copy-start(f32[2048]{0:T(1024)} %param.17) | copy-start | bytes 24580
  235.5 23.0 %copy-start.4 = (bf16[64,2048]{1,0:T(8,128)(2,1)}, bf16[64,2048]{1,0:T(8,128)(2,1)S(1)}, u32[]{:S(2)}) copy-start(bf16[64,2048]{1,0:T(8,128)(2,1)S(1)} %get-tuple-element.106) | copy-start | bytes 786436

commit v3 on v2

--- a/solution.py
+++ b/solution.py
@@ -29,53 +29,128 @@
     return lax.ppermute(block, axis, route)
 
 
-def gather_kernel(n_group, n_expert, wq, wk, wv, wo, xn, oq, ok, ov, oo, oxn, send, recv, local):
+def gather_kernel(n_group, n_expert, wq, wk, wv, wo, xn, oq, ok, ov, oo, oxn, send, recv, xsend, xrecv, local):
     g = lax.axis_index("group")
     e = lax.axis_index("expert")
+    columns = n_group // 2
+    z = lax.div(g, 2)
+    xh = lax.rem(g, 2)
+    zp = lax.rem(z + 1, columns)
+    zm = lax.rem(z + columns - 1, columns)
+    plus_dev = (2 * zp + xh, e)
+    minus_dev = (2 * zm + xh, e)
+    pair_dev = (g + 1 - 2 * xh, e)
+    core = lax.rem(e, 2)
+    chip = lax.div(e, 2)
+    chips = n_expert // 2
+    mate_dev = (g, e + 1 - 2 * core)
+    chip_devs = [(g, 2 * lax.rem(chip + j, chips) + core) for j in range(1, chips)]
     barrier = pltpu.get_barrier_semaphore()
-    for j in range(1, n_group):
-        pl.semaphore_signal(barrier, 1, device_id=(lax.rem(g + j, n_group), e), device_id_type=MESH)
-    for j in range(1, n_expert):
-        pl.semaphore_signal(barrier, 1, device_id=(g, lax.rem(e + j, n_expert)), device_id_type=MESH)
-    pl.semaphore_wait(barrier, n_group - 1 + n_expert - 1)
-    copies = []
-    for j in range(1, n_expert):
+    peers = [plus_dev, minus_dev, pair_dev, mate_dev] + chip_devs
+    for dev in peers:
+        pl.semaphore_signal(barrier, 1, device_id=dev, device_id_type=MESH)
+    pl.semaphore_wait(barrier, len(peers))
+
+    width = wo.shape[1]
+
+    def slot(k, origin):
+        if k == 3:
+            return oo.at[:, pl.ds(pl.multiple_of(origin * width, width), width)]
+        return (oq, ok, ov)[k].at[origin]
+
+    sends = []
+
+    def push(k, origin, src, dev):
         copy = pltpu.make_async_remote_copy(
-            src_ref=xn,
-            dst_ref=oxn.at[e],
-            send_sem=send.at[4, j],
-            recv_sem=recv.at[4, j],
-            device_id=(g, lax.rem(e + j, n_expert)),
+            src_ref=src,
+            dst_ref=slot(k, origin),
+            send_sem=send.at[len(sends)],
+            recv_sem=recv.at[k, origin],
+            device_id=dev,
             device_id_type=MESH,
         )
         copy.start()
-        copies.append(copy)
-    pieces = [(wq, oq), (wk, ok), (wv, ov), (wo, oo)]
-    width = wo.shape[1]
-
-    def slot(dst, k):
-        if k == 3:
-            return dst.at[:, pl.ds(pl.multiple_of(g * width, width), width)]
-        return dst.at[g]
-
-    for j in range(1, n_group):
-        for k, (src, dst) in enumerate(pieces):
-            copy = pltpu.make_async_remote_copy(
-                src_ref=src,
-                dst_ref=slot(dst, k),
-                send_sem=send.at[k, j],
-                recv_sem=recv.at[k, j],
-                device_id=(lax.rem(g + j, n_group), e),
+        sends.append(copy)
+
+    def forward(origin, dev):
+        for k in range(4):
+            push(k, origin, slot(k, origin), dev)
+
+    def arrive(origin):
+        for k in range(4):
+            pltpu.make_async_remote_copy(
+                src_ref=slot(k, origin),
+                dst_ref=slot(k, origin),
+                send_sem=send.at[0],
+                recv_sem=recv.at[k, origin],
+                device_id=pair_dev,
                 device_id_type=MESH,
-            )
-            copy.start()
-            copies.append(copy)
+            ).wait_recv()
+
+    xsends = []
+
+    def xpush(src, origin, dev):
+        copy = pltpu.make_async_remote_copy(
+            src_ref=src,
+            dst_ref=oxn.at[origin],
+            send_sem=xsend.at[len(xsends)],
+            recv_sem=xrecv.at[origin],
+            device_id=dev,
+            device_id_type=MESH,
+        )
+        copy.start()
+        xsends.append(copy)
+
+    def xarrive(origin):
+        pltpu.make_async_remote_copy(
+            src_ref=oxn.at[origin],
+            dst_ref=oxn.at[origin],
+            send_sem=xsend.at[0],
+            recv_sem=xrecv.at[origin],
+            device_id=mate_dev,
+            device_id_type=MESH,
+        ).wait_recv()
+
+    inputs = (wq, wk, wv, wo)
     own = [pltpu.make_async_copy(xn, oxn.at[e], local.at[4])]
-    own += [pltpu.make_async_copy(src, slot(dst, k), local.at[k]) for k, (src, dst) in enumerate(pieces)]
+    own += [pltpu.make_async_copy(inputs[k], slot(k, g), local.at[k]) for k in range(4)]
     for copy in own:
         copy.start()
-    for copy in copies:
-        copy.wait()
+    xpush(xn, e, mate_dev)
+    for dev in chip_devs:
+        xpush(xn, e, dev)
+    for dev in (pair_dev, plus_dev, minus_dev):
+        for k in range(4):
+            push(k, g, inputs[k], dev)
+    partner = g + 1 - 2 * xh
+    arrive(partner)
+    forward(partner, plus_dev)
+    forward(partner, minus_dev)
+    chip_origins = [2 * lax.rem(chip + j, chips) + core for j in range(1, chips)]
+    normed_order = [chip_origins[0:2], chip_origins[2:5], chip_origins[5:]]
+    for step in range(1, 4):
+        behind = lax.rem(z - step + columns, columns)
+        ahead = lax.rem(z + step, columns)
+        for origin in (2 * behind, 2 * behind + 1):
+            arrive(origin)
+        for origin in ((2 * behind, 2 * behind + 1) if step < 3 else (2 * behind,)):
+            forward(origin, plus_dev)
+        for origin in (2 * ahead, 2 * ahead + 1):
+            arrive(origin)
+        for origin in ((2 * ahead, 2 * ahead + 1) if step < 3 else (2 * ahead + 1,)):
+            forward(origin, minus_dev)
+        for origin in normed_order[step - 1]:
+            xarrive(origin)
+            xpush(oxn.at[origin], origin, mate_dev)
+    across = lax.rem(z + columns // 2, columns)
+    arrive(2 * across)
+    arrive(2 * across + 1)
+    mate_core = 1 - core
+    xarrive(e + 1 - 2 * core)
+    for j in range(1, chips):
+        xarrive(2 * lax.rem(chip + j, chips) + mate_core)
+    for copy in sends + xsends:
+        copy.wait_send()
     for copy in own:
         copy.wait()
 
@@ -91,12 +166,93 @@
         in_specs=[any_spec] * 5,
         out_specs=tuple([any_spec] * 5),
         scratch_shapes=[
-            pltpu.SemaphoreType.DMA((5, max(n_group, n_expert))),
-            pltpu.SemaphoreType.DMA((5, max(n_group, n_expert))),
+            pltpu.SemaphoreType.DMA((64,)),
+            pltpu.SemaphoreType.DMA((4, n_group)),
+            pltpu.SemaphoreType.DMA((n_expert,)),
+            pltpu.SemaphoreType.DMA((n_expert,)),
             pltpu.SemaphoreType.DMA((5,)),
         ],
         compiler_params=pltpu.CompilerParams(collective_id=0, has_side_effects=True),
     )(wq, wk, wv, wo, xn)
+
+
+def mate_kernel(part, out, send, recv):
+    g = lax.axis_index("group")
+    e = lax.axis_index("expert")
+    core = lax.rem(e, 2)
+    mate_dev = (g, e + 1 - 2 * core)
+    barrier = pltpu.get_barrier_semaphore()
+    pl.semaphore_signal(barrier, 1, device_id=mate_dev, device_id_type=MESH)
+    pl.semaphore_wait(barrier, 1)
+    copy = pltpu.make_async_remote_copy(
+        src_ref=part.at[:, 1 - core],
+        dst_ref=out,
+        send_sem=send.at[0],
+        recv_sem=recv.at[0],
+        device_id=mate_dev,
+        device_id_type=MESH,
+    )
+    copy.start()
+    copy.wait()
+
+
+def exchange_with_mate(part):
+    any_spec = pl.BlockSpec(memory_space=pl.ANY)
+    shape = (part.shape[0],) + part.shape[2:]
+    return pl.pallas_call(
+        mate_kernel,
+        out_shape=jax.ShapeDtypeStruct(shape, part.dtype),
+        in_specs=[any_spec],
+        out_specs=any_spec,
+        scratch_shapes=[pltpu.SemaphoreType.DMA((1,)), pltpu.SemaphoreType.DMA((1,))],
+        compiler_params=pltpu.CompilerParams(collective_id=4, has_side_effects=True),
+    )(part)
+
+
+def chip_scatter_kernel(chips, part, out, send, recv, local):
+    g = lax.axis_index("group")
+    e = lax.axis_index("expert")
+    core = lax.rem(e, 2)
+    chip = lax.div(e, 2)
+    devs = [(g, 2 * lax.rem(chip + j, chips) + core) for j in range(1, chips)]
+    barrier = pltpu.get_barrier_semaphore()
+    for dev in devs:
+        pl.semaphore_signal(barrier, 1, device_id=dev, device_id_type=MESH)
+    pl.semaphore_wait(barrier, len(devs))
+    copies = []
+    for j in range(1, chips):
+        copy = pltpu.make_async_remote_copy(
+            src_ref=part.at[lax.rem(chip + j, chips)],
+            dst_ref=out.at[chip],
+            send_sem=send.at[j],
+            recv_sem=recv.at[j],
+            device_id=devs[j - 1],
+            device_id_type=MESH,
+        )
+        copy.start()
+        copies.append(copy)
+    own = pltpu.make_async_copy(part.at[chip], out.at[chip], local.at[0])
+    own.start()
+    for copy in copies:
+        copy.wait()
+    own.wait()
+
+
+def scatter_to_chips(part):
+    chips = part.shape[0]
+    any_spec = pl.BlockSpec(memory_space=pl.ANY)
+    return pl.pallas_call(
+        functools.partial(chip_scatter_kernel, chips),
+        out_shape=jax.ShapeDtypeStruct(part.shape, part.dtype),
+        in_specs=[any_spec],
+        out_specs=any_spec,
+        scratch_shapes=[
+            pltpu.SemaphoreType.DMA((chips,)),
+            pltpu.SemaphoreType.DMA((chips,)),
+            pltpu.SemaphoreType.DMA((1,)),
+        ],
+        compiler_params=pltpu.CompilerParams(collective_id=5, has_side_effects=True),
+    )(part)
 
 
 def scatter_kernel(n_expert, part, out, send, recv, local):
@@ -271,7 +427,11 @@
     head_partials = jnp.dot(
         attended, output_parts, preferred_element_type=jnp.float32
     ).astype(jnp.bfloat16)
-    owned = scatter_blocks(head_partials.reshape(experts_axis, -1, model_width), experts_axis, 1)
+    paired = head_partials.reshape(experts_axis // 2, 2, -1, model_width)
+    from_mate = exchange_with_mate(paired)
+    own_parity = lax.dynamic_index_in_dim(paired, group_member % 2, 1, keepdims=False)
+    chip_sums = (own_parity.astype(jnp.float32) + from_mate.astype(jnp.float32)).astype(jnp.bfloat16)
+    owned = scatter_to_chips(chip_sums)
     summed = jnp.sum(owned.astype(jnp.float32), axis=0)
     hidden = (hidden_in.astype(jnp.float32) + summed).astype(jnp.bfloat16)
     normed_second = norm_rows(hidden, norm_experts).astype(jnp.bfloat16)

time: 275 us -> 219 us (0.80)
  Pallas kernels: 188 us -> 133 us
  other arithmetic: 28.9 us -> 32.3 us
    pallas_call x3 -> x2, Pallas kernels: 87.7 us -> 22.1 us  [scatter_blocks(): pl.pallas_call(functools.partial(scatter_kernel, n_expert), out_shape=jax...]
    pallas_call x0 -> x2, Pallas kernels: none -> 39.3 us  [the longest x1 31.8 us: scatter_to_chips(): pl.pallas_call(functools.partial(chip_scatter_kernel, chips), out_shape=j...]
    pallas_call x1, Pallas kernels: 101 us -> 71.5 us  [gather_all(): pl.pallas_call(functools.partial(gather_kernel, n_group, n_expert), out_s...]
    convert_element_type x0 -> x1, other arithmetic: none -> 4.46 us  [per_device(): (own_parity.astype(jnp.float32) + from_mate.astype(jnp.float32)).astype(j...]
  transfers between devices with their start and end apart: 1 -> 1, of which waited for: 1 -> 0; matrix products, arithmetic and copies ran while one was open for 5% -> 6% of each run, Pallas kernels for 0% -> 0%
where the time goes in v3:
time: 219 us; the launch traced here: 218 us
  Pallas kernels  133 us (61%)
  other arithmetic  32.3 us (15%)
  matrix products  28.9 us (13%)
  local copies, waits for them, and re-layouts  20.4 us (9%)
    pallas_call x1, Pallas kernels, gather_all(): pl.pallas_call(functools.partial(gather_kernel, n_group, n_expert), out_s...  71.5 us
    pallas_call x1, Pallas kernels, scatter_to_chips(): pl.pallas_call(functools.partial(chip_scatter_kernel, chips), out_shape=j...  31.8 us
    pallas_call x2, Pallas kernels, scatter_blocks(): pl.pallas_call(functools.partial(scatter_kernel, n_expert), out_shape=jax...  22.1 us
    dot_general x2, matrix products, attend(): jnp.einsum('qhd,kd->hqk', query_block, all_keys, preferred_element_type=j...  7.79 us
    pallas_call x1, Pallas kernels, exchange_with_mate(): pl.pallas_call(mate_kernel, out_shape=jax.ShapeDtypeStruct(shape, part.dt...  7.54 us
    dot_general x1, matrix products, per_device(): jnp.dot(normed_parts.reshape(-1, model_width), joined_weights, preferred_...  5.18 us
    dot_general x1, matrix products, per_device(): jnp.dot(attended, output_parts, preferred_element_type=jnp.float32)  4.57 us
    convert_element_type x1, other arithmetic, per_device(): (own_parity.astype(jnp.float32) + from_mate.astype(jnp.float32)).astype(j...  4.46 us
  transfers between devices with their start and end apart: 1, of which 0 were waited for; matrix products, arithmetic and copies ran while one was open for 6% of the time, Pallas kernels for 0%

profile of v3, /device:TPU:1, one launch (start us, length us, event | category | flops | bytes accessed | tf_op | source)
XLA Modules:
  0.0 217.8 jit_solution(9031638292398873981)
XLA Ops:
  0.7 1.1 dynamic-slice_convert_fusion
  1.8 0.6 slice_bitcast_fusion.2
  2.4 1.1 fusion.37
  3.5 1.6 convert_element_type.114.wq
  5.1 1.5 convert_element_type.116.wo
  6.6 1.8 fusion.39.xn
  8.4 71.5 %shard_map.140 = (bf16[16,128,256]{2,1,0:T(8,128)(2,1)}, bf16[16,128,128]{2,1,0:T(8,128)(2,1)}, bf16[16,128,128]{2,1,0:T(8,128)(2,1)}, bf16[256,2048]{1,0:T(8,128)(2,1)}, bf16[16,64,2048]{2,1,0:T(8,128)(2,1)}) custom-call(bf16[128,256]{1,0:T(8,128)(2,1)} %convert_element_type.114.wq, bf16[128,128]{1,0:T(8,128)(2,1)} %get-tuple-element.120.wk, ...), custom_call_target="tpu_custom_call" | custom-call | tf_op jit(solution)/shard_map/pallas_call | solution.py:163
  79.9 5.2 %fusion.28 = bf16[1024,512]{0,1:T(8,128)(2,1)S(1)} fusion(bf16[1024,2048]{1,0:T(8,128)(2,1)} %bitcast.98, bf16[2048,128]{1,0:T(8,128)(2,1)} %bitcast.101, bf16[2048,128]{1,0:T(8,128)(2,1)} %bitcast.100, bf16[2048,256]{1,0:T(8,128)(2,1)} %bitcast.99), kind=kOutput, calls=%fused_computation.37 | convolution fusion | flops 2154299392 | bytes 7340032 | tf_op jit(solution)/shard_map/dot_general | solution.py:376
  85.2 0.9 copy-done.1
  86.1 0.8 fusion.74
  86.9 1.1 fusion.33
  88.0 1.2 fusion.47
  89.2 0.7 fusion.56
  89.9 1.8 pad_maximum_fusion.1
  91.8 0.8 collective-permute-start
  92.6 1.9 slice.54
  94.5 0.1 multiply_reduce_fusion
  94.6 3.1 %multiply_cosine_fusion = (f32[1024,64]{1,0:T(8,128)}, f32[1024,64]{1,0:T(8,128)}) fusion(f32[64]{0:T(128)S(1)} %multiply_exponential_fusion, f32[1024]{0:T(1024)S(1)} %get-tuple-element.124), kind=kLoop, calls=%fused_computation.46 | loop fusion | flops 65536 | bytes 528640 | tf_op jit(solution)/shard_map/cos | solution.py:312
  97.7 0.1 fusion.72
  97.9 0.1 select_reduce_fusion.2
  98.0 2.2 %copy.26 = f32[1024,2,128]{2,0,1:T(8,128)} copy(bf16[1024,2,128]{0,2,1:T(8,128)(2,1)} %bitcast.97) | data formatting | bytes 1572864 | tf_op jit(solution)/shard_map/convert_element_type | solution.py:302
  100.5 1.6 multiply_multiply_fusion
  102.0 1.7 subtract_convert_fusion
  103.7 0.6 fusion.69
  104.4 0.2 select_reduce_fusion.1
  104.5 1.1 pad_maximum_fusion
  105.6 1.8 slice_bitcast_fusion
  107.4 0.9 pad_maximum_fusion.3
  108.2 2.1 copy.28
  110.3 1.9 pad_maximum_fusion.2
  112.2 2.1 copy.27
  114.3 19.3 %while.10 = (s32[]{:T(128)}, bf16[2,512,2,128]{3,2,1,0:T(2,128)(2,1)}, s32[2048]{0:T(1024)S(1)}, s32[2]{0:T(128)S(1)}, s32[1024]{0:T(1024)S(1)}, /*index=5*/s32[...) while((s32[]{:T(128)}, ...), condition=%wide.region_6.7_spmd, body=%wide.region_4.6_spmd.sunk | while | flops 1088685056 | bytes 24152800 | solution.py:426
  114.3 0.6 dynamic_slice.29
  115.6 0.6 broadcast_compare_fusion.3
  116.2 0.7 compare_and_fusion.2
  117.0 3.9 %bitcast_reduce_fusion.2 = (f32[2,512]{1,0:T(2,128)S(1)}, f32[512,2,2048]{2,0,1:T(8,128)S(1)}) fusion(pred[512,2048]{1,0:T(8,128)(4,1)S(1)} %compare_and_fusion.2, bf16[2048,128]{1,0:T(8,128)(2,1)} %get-tuple-element.217, bf16[1024,2,128]{2,0,1:T(8,128)(2,1)} %get-tuple-element.216, s32[]{:T(128)S(6)} %select_n.141), kind=kOutput, calls=%fused_computation.clone.1 | convolution fusion | flops 543161344 | bytes 10227716 | tf_op jit(solution)/shard_map/while/body/eval_jaxpr/qhd,kd->hqk/dot_general | solution.py:410
  120.9 2.0 fusion.83
  122.9 1.0 copy_dynamic-update-slice_fusion.2
  123.9 0.6 dynamic_slice.29
  125.2 0.6 broadcast_compare_fusion.3
  125.9 0.7 compare_and_fusion.2
  126.6 3.9 %bitcast_reduce_fusion.2 = (f32[2,512]{1,0:T(2,128)S(1)}, f32[512,2,2048]{2,0,1:T(8,128)S(1)}) fusion(pred[512,2048]{1,0:T(8,128)(4,1)S(1)} %compare_and_fusion.2, bf16[2048,128]{1,0:T(8,128)(2,1)} %get-tuple-element.217, bf16[1024,2,128]{2,0,1:T(8,128)(2,1)} %get-tuple-element.216, s32[]{:T(128)S(6)} %select_n.141), kind=kOutput, calls=%fused_computation.clone.1 | convolution fusion | flops 543161344 | bytes 10227716 | tf_op jit(solution)/shard_map/while/body/eval_jaxpr/qhd,kd->hqk/dot_general | solution.py:410
  130.5 2.0 fusion.83
  132.6 1.0 copy_dynamic-update-slice_fusion.2
  133.6 4.6 %convolution_convert_fusion = bf16[1024,2048]{1,0:T(8,128)(2,1)} fusion(bf16[256,2048]{1,0:T(8,128)(2,1)} %get-tuple-element.59, bf16[128,8,2,128]{3,2,1,0:T(2,128)(2,1)} %bitcast.29), kind=kOutput, calls=%fused_computation.24 | convolution fusion | flops 1075838976 | bytes 5767168 | tf_op jit(solution)/shard_map/dot_general | solution.py:427
  138.1 7.5 %shard_map.141 = bf16[8,64,2048]{2,1,0:T(8,128)(2,1)} custom-call(bf16[8,2,64,2048]{3,2,1,0:T(8,128)(2,1)} %bitcast.95), custom_call_target="tpu_custom_call" | custom-call | tf_op jit(solution)/shard_map/pallas_call | solution.py:202
  145.7 4.5 %fusion.15.part = bf16[8,64,2048]{2,1,0:T(8,128)(2,1)} fusion(bf16[8,64,2048]{2,1,0:T(8,128)(2,1)} %shard_map.141, bf16[8,2,64,2048]{3,2,1,0:T(8,128)(2,1)} %bitcast.96, s32[]{:T(128)S(6)} %select_n.92), kind=kLoop, calls=%fused_computation.22 | loop fusion | flops 4194304 | bytes 6291460 | tf_op jit(solution)/shard_map/convert_element_type | solution.py:433
  150.2 31.8 %shard_map.142 = bf16[8,64,2048]{2,1,0:T(8,128)(2,1)} custom-call(bf16[8,64,2048]{2,1,0:T(8,128)(2,1)} %fusion.15.part), custom_call_target="tpu_custom_call" | custom-call | tf_op jit(solution)/shard_map/pallas_call | solution.py:244
  181.9 2.0 convert_reduce_fusion
  184.0 0.2 fusion.34
  184.2 1.4 fusion.53
  185.6 0.2 select_reduce_fusion
  185.8 0.1 exponential_reduce_fusion
  185.9 0.2 select_reduce_fusion.3
  186.1 0.3 convolution_convert_fusion.1
  186.4 0.8 reshape.286.part
  187.2 13.3 %shard_map.143 = bf16[16,4,2048]{2,1,0:T(4,128)(2,1)} custom-call(bf16[16,4,2048]{2,1,0:T(4,128)(2,1)} %reshape.286.part), custom_call_target="tpu_custom_call" | custom-call | tf_op jit(solution)/shard_map/pallas_call | solution.py:287
  200.5 1.0 reshape.287
  201.5 4.0 %fusion.13 = f32[64,1536]{1,0:T(8,128)S(1)} fusion(bf16[64,2048]{1,0:T(8,128)(2,1)S(1)} %reshape.287, bf16[1,2048,1536]{2,1,0:T(8,128)(2,1)} %param.25), kind=kOutput, calls=%fused_computation.19 | convolution fusion | flops 402653184 | bytes 6946816 | tf_op jit(solution)/shard_map/dot_general | solution.py:466
  205.5 0.7 fusion.19
  206.2 0.8 reshape.288.part
  207.0 8.8 %shard_map.144 = bf16[16,4,2048]{2,1,0:T(4,128)(2,1)} custom-call(bf16[16,4,2048]{2,1,0:T(4,128)(2,1)} %reshape.288.part), custom_call_target="tpu_custom_call" | custom-call | tf_op jit(solution)/shard_map/pallas_call | solution.py:287
  215.8 1.0 reshape.289
  216.9 1.0 fusion.18
  (41 shorter events, 0.6 us)
Async XLA Ops:
  0.6 204.9 %copy-start = (bf16[1,768,2048]{2,1,0:T(8,128)(2,1)S(1)}, bf16[1,768,2048]{2,1,0:T(8,128)(2,1)}, u32[]{:S(2)}) copy-start(bf16[1,768,2048]{2,1,0:T(8,128)(2,1)} %param.26) | copy-start | bytes 9437188
  79.9 7.0 %copy-start.9 = (f32[128]{0:T(128)S(1)}, f32[128]{0:T(128)}, u32[]{:S(2)}) copy-start(f32[128]{0:T(128)} %param.22) | copy-start | bytes 1540
  85.1 1.0 copy-start.1
  85.1 12.5 %copy-start.7 = (s32[64,8]{0,1:T(8,128)S(1)}, s32[64,8]{0,1:T(8,128)}, u32[]{:S(2)}) copy-start(s32[64,8]{0,1:T(8,128)} %param.27) | copy-start | bytes 6148
  86.1 14.4 %copy-start.8 = (f32[128]{0:T(128)S(1)}, f32[128]{0:T(128)}, u32[]{:S(2)}) copy-start(f32[128]{0:T(128)} %param.21) | copy-start | bytes 1540
  86.9 7.6 %copy-start.2 = (bf16[1024,512]{0,1:T(8,128)(2,1)S(1)}, bf16[1024,512]{0,1:T(8,128)(2,1)}, u32[]{:S(2)}) copy-start(bf16[1024,512]{0,1:T(8,128)(2,1)} %copy-done.1) | copy-start | bytes 3145732
  91.8 13.9 %collective-permute-start = (bf16[2,1024,128]{1,2,0:T(8,128)(2,1)}, bf16[2,1024,128]{1,2,0:T(8,128)(2,1)}, u32[]{:S(2)}, u32[]{:S(2)}) collective-permute-start(bf16[2,1024,128]{1,2,0:T(8,128)(2,1)} %pad_maximum_fusion.1), channel_id=1, source_target_pairs={{0,16},{16,0},{32,48},{48,32},{64,80},{80,64},{96,112},{112,96},{1... | collective-permute-start | bytes 1572872 | tf_op jit(solution)/shard_map/ppermute | solution.py:29
  97.7 6.1 %copy-start.10 = (s32[8]{0:T(128)S(1)}, s32[8]{0:T(128)}, u32[]{:S(2)}) copy-start(s32[8]{0:T(128)} %param.23) | copy-start | bytes 100
  117.0 3.9 %copy-start.5 = (bf16[2048,128]{1,0:T(8,128)(2,1)S(1)}, bf16[2048,128]{1,0:T(8,128)(2,1)}, u32[]{:S(2)}) copy-start(bf16[2048,128]{1,0:T(8,128)(2,1)} %get-tuple-element.218) | copy-start | bytes 1572868 | tf_op jit(solution)/shard_map/while
  126.6 3.9 %copy-start.5 = (bf16[2048,128]{1,0:T(8,128)(2,1)S(1)}, bf16[2048,128]{1,0:T(8,128)(2,1)}, u32[]{:S(2)}) copy-start(bf16[2048,128]{1,0:T(8,128)(2,1)} %get-tuple-element.218) | copy-start | bytes 1572868 | tf_op jit(solution)/shard_map/while
  150.2 33.8 %copy-start.3 = (bf16[64,2048]{1,0:T(8,128)(2,1)S(1)}, bf16[64,2048]{1,0:T(8,128)(2,1)}, u32[]{:S(2)}) copy-start(bf16[64,2048]{1,0:T(8,128)(2,1)} %param.15) | copy-start | bytes 786436
  150.2 34.0 %copy-start.6 = (f32[2048]{0:T(1024)S(1)}, f32[2048]{0:T(1024)}, u32[]{:S(2)}) copy-start(f32[2048]{0:T(1024)} %param.17) | copy-start | bytes 24580
  184.2 2.0 copy-start.4

commit v4 on v3

--- a/solution.py
+++ b/solution.py
@@ -298,6 +298,51 @@
     )(part)
 
 
+def attention_kernel(scale, heads, q_ref, k_ref, v_ref, qpos_ref, kpos_ref, o_ref):
+    allowed = kpos_ref[...] <= qpos_ref[...]
+    keys = k_ref[...]
+    values = v_ref[...]
+    depth = keys.shape[1]
+    for h in range(heads):
+        query = q_ref[:, h * depth : (h + 1) * depth]
+        scores = (
+            lax.dot_general(
+                query, keys, (((1,), (1,)), ((), ())), preferred_element_type=jnp.float32
+            )
+            * scale
+        )
+        weights = jnp.where(allowed, jnp.exp(scores), 0.0)
+        denominators = jnp.sum(weights, axis=-1, keepdims=True)
+        weighted = jnp.dot(
+            weights.astype(jnp.bfloat16), values, preferred_element_type=jnp.float32
+        )
+        o_ref[:, h * depth : (h + 1) * depth] = (weighted / denominators).astype(o_ref.dtype)
+
+
+def attention(queries, keys, values, query_places, key_places, scale):
+    rows, width = queries.shape
+    key_rows, depth = keys.shape
+    block = min(256, rows)
+    return pl.pallas_call(
+        functools.partial(attention_kernel, scale, width // depth),
+        out_shape=jax.ShapeDtypeStruct((rows, width), jnp.bfloat16),
+        grid=(rows // block,),
+        in_specs=[
+            pl.BlockSpec((block, width), lambda i: (i, 0)),
+            pl.BlockSpec((key_rows, depth), lambda i: (0, 0)),
+            pl.BlockSpec((key_rows, depth), lambda i: (0, 0)),
+            pl.BlockSpec((block, 1), lambda i: (i, 0)),
+            pl.BlockSpec((1, key_rows), lambda i: (0, 0)),
+        ],
+        out_specs=pl.BlockSpec((block, width), lambda i: (i, 0)),
+        cost_estimate=pl.CostEstimate(
+            flops=4 * rows * key_rows * width,
+            transcendentals=rows * key_rows * (width // depth),
+            bytes_accessed=2 * (2 * rows * width + 2 * key_rows * depth),
+        ),
+    )(queries, keys, values, query_places.reshape(rows, 1), key_places.reshape(1, key_rows))
+
+
 def norm_rows(values, gain_vector):
     widened = values.astype(jnp.float32)
     inverse_rms = lax.rsqrt(jnp.mean(widened * widened, axis=-1, keepdims=True) + epsilon)
@@ -398,32 +443,16 @@
     all_values = jnp.concatenate([value_rows, partner[1]], axis=0)
     key_places = jnp.concatenate([own_places, partner_places])
     valid_length = jnp.sum(jnp.where(jnp.arange(lengths.shape[0]) == group_index // 2, lengths, 0))
-    block_rows = min(512, local_rows)
-    block_count = local_rows // block_rows
-    score_scale = HEAD_DIMENSION ** (-0.5)
-
-    def attend(block_index):
-        block_start = block_index * block_rows
-        query_block = lax.dynamic_slice_in_dim(query_rows_list, block_start, block_rows, 0)
-        query_places = lax.dynamic_slice_in_dim(own_places, block_start, block_rows, 0)
-        scores = (
-            jnp.einsum("qhd,kd->hqk", query_block, all_keys, preferred_element_type=jnp.float32)
-            * score_scale
-        )
-        allowed = (key_places[None, :] <= query_places[:, None]) & (
-            key_places[None, :] < valid_length
-        )
-        weights = jnp.where(allowed[None], jnp.exp(scores), 0.0)
-        denominators = jnp.sum(weights, axis=-1)
-        weighted = jnp.einsum(
-            "hqk,kd->qhd",
-            weights.astype(jnp.bfloat16),
-            all_values,
-            preferred_element_type=jnp.float32,
-        )
-        return (weighted / jnp.transpose(denominators)[:, :, None]).astype(jnp.bfloat16)
-
-    attended = lax.map(attend, jnp.arange(block_count)).reshape(local_rows, width_here)
+    past_end = jnp.full_like(key_places, 4 * key_places.shape[0])
+    key_limits = jnp.where(key_places < valid_length, key_places, past_end)
+    attended = attention(
+        query_rows_list.reshape(local_rows, width_here),
+        all_keys,
+        all_values,
+        own_places,
+        key_limits,
+        HEAD_DIMENSION ** (-0.5),
+    )
     head_partials = jnp.dot(
         attended, output_parts, preferred_element_type=jnp.float32
     ).astype(jnp.bfloat16)

time: 219 us -> 212 us (0.968)
  matrix products: 28.9 us -> 17 us
  Pallas kernels: 133 us -> 142 us
  local copies, waits for them, and re-layouts: 20.4 us -> 11.7 us
  other arithmetic: 32.3 us -> 39.2 us
    dot_general x4 -> x0, matrix products: 11.9 us -> none  [the longest x2 7.79 us: attend(): jnp.einsum('qhd,kd->hqk', query_block, all_keys, preferred_element_type=j...]
    pallas_call x0 -> x1, Pallas kernels: none -> 9.01 us  [attention(): pl.pallas_call(functools.partial(attention_kernel, scale, width // depth)...]
    while x6 -> x0, local copies, waits for them, and re-layouts: 4.13 us -> none  [the longest x2 4.12 us: per_device(): lax.map(attend, jnp.arange(block_count)).reshape(local_rows, width_here)]
    reduce_sum x4, other arithmetic: 1.49 us -> 3.99 us  [norm_rows(): jnp.mean(widened * widened, axis=-1, keepdims=True) + epsilon]
  transfers between devices with their start and end apart: 1 -> 1, of which waited for: 0 -> 0; matrix products, arithmetic and copies ran while one was open for 6% -> 10% of each run, Pallas kernels for 0% -> 0%
where the time goes in v4:
time: 212 us
  Pallas kernels  142 us (67%)
  other arithmetic  39.2 us (18%)
  matrix products  17 us (8%)
  local copies, waits for them, and re-layouts  11.7 us (6%)
    pallas_call x1, Pallas kernels, gather_all(): pl.pallas_call(functools.partial(gather_kernel, n_group, n_expert), out_s...  71.5 us
    pallas_call x1, Pallas kernels, scatter_to_chips(): pl.pallas_call(functools.partial(chip_scatter_kernel, chips), out_shape=j...  31.8 us
    pallas_call x2, Pallas kernels, scatter_blocks(): pl.pallas_call(functools.partial(scatter_kernel, n_expert), out_shape=jax...  22.1 us
    pallas_call x1, Pallas kernels, attention(): pl.pallas_call(functools.partial(attention_kernel, scale, width // depth)...  9.01 us
    pallas_call x1, Pallas kernels, exchange_with_mate(): pl.pallas_call(mate_kernel, out_shape=jax.ShapeDtypeStruct(shape, part.dt...  7.53 us
    dot_general x1, matrix products, per_device(): jnp.dot(normed_parts.reshape(-1, model_width), joined_weights, preferred_...  5.14 us
    mul x2, other arithmetic, norm_rows(): return widened * inverse_rms * gain_vector  4.81 us
    dot_general x1, matrix products, per_device(): jnp.dot(attended, output_parts, preferred_element_type=jnp.float32)  4.57 us
  transfers between devices with their start and end apart: 1, of which 0 were waited for; matrix products, arithmetic and copies ran while one was open for 10% of the time, Pallas kernels for 0%

profile of v4, /device:TPU:1, one launch (start us, length us, event | category | flops | bytes accessed | tf_op | source)
XLA Modules:
  0.0 211.8 jit_solution(13310485327223128533)
XLA Ops:
  0.6 0.0 copy-start
  0.7 1.1 dynamic-slice_convert_fusion
  1.8 0.6 slice_bitcast_fusion.2
  2.4 1.1 fusion.30
  3.5 1.6 convert_element_type.112.wq
  5.1 1.5 convert_element_type.114.wo
  6.6 1.8 fusion.32.xn
  8.4 71.5 %shard_map.140 = (bf16[16,128,256]{2,1,0:T(8,128)(2,1)}, bf16[16,128,128]{2,1,0:T(8,128)(2,1)}, bf16[16,128,128]{2,1,0:T(8,128)(2,1)}, bf16[256,2048]{1,0:T(8,128)(2,1)}, bf16[16,64,2048]{2,1,0:T(8,128)(2,1)}) custom-call(bf16[128,256]{1,0:T(8,128)(2,1)} %convert_element_type.112.wq, bf16[128,128]{1,0:T(8,128)(2,1)} %get-tuple-element.23.wk, ...), custom_call_target="tpu_custom_call" | custom-call | tf_op jit(solution)/shard_map/pallas_call | solution.py:163
  79.9 0.0 copy-start.9
  79.9 5.1 %fusion.15 = bf16[1024,512]{1,0:T(8,128)(2,1)S(1)} fusion(bf16[1024,2048]{1,0:T(8,128)(2,1)} %bitcast.52, bf16[2048,128]{1,0:T(8,128)(2,1)} %bitcast.55, bf16[2048,128]{1,0:T(8,128)(2,1)} %bitcast.54, bf16[2048,256]{1,0:T(8,128)(2,1)} %bitcast.53), kind=kOutput, calls=%fused_computation.18 | convolution fusion | flops 2154299392 | bytes 7340032 | tf_op jit(solution)/shard_map/dot_general | solution.py:421
  85.1 0.2 fusion.22
  85.3 0.8 copy-done.5
  86.1 0.7 fusion.57
  86.8 1.2 fusion.24
  88.1 2.4 %fusion.28 = (bf16[1024,1,64]{2,0,1:T(8,128)(2,1)S(1)}, bf16[1024,1,64]{2,0,1:T(8,128)(2,1)S(1)}) fusion(f32[1024,1,128]{2,0,1:T(8,128)S(1)} %fusion.24, f32[64]{0:T(128)S(1)} %multiply_exponential_fusion, f32[1024]{0:T(1024)S(1)} %get-tuple-element.27), kind=kLoop, calls=%fused_computation.44 | loop fusion | flops 589824 | bytes 790784 | tf_op jit(solution)/shard_map/sub | solution.py:363
  90.5 0.1 fusion.58
  90.7 1.8 pad_maximum_fusion.1
  92.5 0.8 collective-permute-start
  93.3 0.8 fusion.59
  94.1 0.0 copy-done.6
  94.1 1.1 slice_convert_fusion
  95.2 3.0 %multiply_cosine_fusion.1 = (f32[1024,64]{1,0:T(8,128)}, f32[1024,64]{1,0:T(8,128)}) fusion(f32[64]{0:T(128)S(1)} %multiply_exponential_fusion, f32[1024]{0:T(1024)S(1)} %get-tuple-element.27), kind=kLoop, calls=%fused_computation.29 | loop fusion | flops 65536 | bytes 528640 | tf_op jit(solution)/shard_map/cos | solution.py:357
  98.2 0.8 select_add_fusion.qpos_ref
  99.1 0.1 copy.36
  99.2 0.1 fusion.55
  99.3 0.1 select_reduce_fusion.2
  99.4 2.8 %reshape.302 = f32[1024,2,128]{2,1,0:T(2,128)} reshape(f32[1024,256]{1,0:T(8,128)} %slice_convert_fusion) | data formatting | bytes 2097152 | tf_op jit(solution)/shard_map/convert_element_type | solution.py:347
  102.2 2.5 %multiply_reduce_fusion = f32[1024,2]{1,0:T(8,128)S(1)} fusion(f32[1024,2,128]{2,1,0:T(2,128)} %reshape.302), kind=kLoop, calls=%fused_computation.22 | loop fusion | flops 522240 | bytes 1056768 | tf_op jit(solution)/shard_map/reduce_sum | solution.py:348
  104.7 0.1 add_rsqrt_fusion
  104.8 0.0 copy-start.11
  104.8 3.6 %multiply_multiply_fusion = f32[1024,2,128]{2,1,0:T(2,128)S(1)} fusion(f32[1024,2,128]{2,1,0:T(2,128)} %reshape.302, f32[128]{0:T(128)S(1)} %copy-done.10, f32[1024,2]{1,0:T(8,128)S(1)} %add_rsqrt_fusion), kind=kLoop, calls=%fused_computation.21 | loop fusion | flops 524288 | bytes 2105856 | tf_op jit(solution)/shard_map/mul | solution.py:349
  108.4 1.7 subtract_convert_fusion
  110.1 1.4 pad_maximum_fusion
  111.5 0.9 copy.44
  112.4 0.1 fusion.44
  112.5 0.1 reduce_window_sum.11
  112.6 0.2 select_reduce_fusion.1
  112.8 0.7 fusion.52
  113.5 1.3 compare_select_fusion.kpos_ref
  114.8 0.0 collective-permute-done
  114.8 1.1 slice_bitcast_fusion
  115.9 0.8 pad_maximum_fusion.3.v_ref
  116.7 1.8 pad_maximum_fusion.2.k_ref
  118.5 9.0 %shard_map.141 = bf16[1024,256]{1,0:T(8,128)(2,1)} custom-call(bf16[1024,256]{1,0:T(8,128)(2,1)} %bitcast.49, bf16[2048,128]{1,0:T(8,128)(2,1)} %pad_maximum_fusion.2.k_ref, bf16[2048,128]{1,0:T(8,128)(2,1)} %pad_maximum_fusion.3.v_ref, s32[1024,1]{1,0:T(8,128)} %select_add_fusion.qpos_ref, s32[1,2048]{1,0:T(1,128)} %compare_select_fusion.kpos_ref), custom_call_target="tpu_custom_call" | custom-call | flops 2147483648 | bytes 2097152 | tf_op jit(solution)/shard_map/pallas_call | solution.py:326
  127.5 4.6 %convolution_convert_fusion = bf16[1024,2048]{1,0:T(8,128)(2,1)} fusion(bf16[1024,256]{1,0:T(8,128)(2,1)} %shard_map.141, bf16[256,2048]{1,0:T(8,128)(2,1)} %get-tuple-element.11), kind=kOutput, calls=%fused_computation.5 | convolution fusion | flops 1075838976 | bytes 5767168 | tf_op jit(solution)/shard_map/dot_general | solution.py:456
  132.1 7.5 %shard_map.142 = bf16[8,64,2048]{2,1,0:T(8,128)(2,1)} custom-call(bf16[8,2,64,2048]{3,2,1,0:T(8,128)(2,1)} %bitcast.46), custom_call_target="tpu_custom_call" | custom-call | tf_op jit(solution)/shard_map/pallas_call | solution.py:202
  139.6 4.5 %fusion.2.part = bf16[8,64,2048]{2,1,0:T(8,128)(2,1)} fusion(bf16[8,64,2048]{2,1,0:T(8,128)(2,1)} %shard_map.142, bf16[8,2,64,2048]{3,2,1,0:T(8,128)(2,1)} %bitcast.47, s32[]{:T(128)S(6)} %select_n.152), kind=kLoop, calls=%fused_computation.3 | loop fusion | flops 4194304 | bytes 6291460 | tf_op jit(solution)/shard_map/convert_element_type | solution.py:462
  144.1 31.8 %shard_map.143 = bf16[8,64,2048]{2,1,0:T(8,128)(2,1)} custom-call(bf16[8,64,2048]{2,1,0:T(8,128)(2,1)} %fusion.2.part), custom_call_target="tpu_custom_call" | custom-call | tf_op jit(solution)/shard_map/pallas_call | solution.py:244
  175.9 2.0 convert_reduce_fusion
  177.9 0.2 fusion.25
  178.1 1.4 fusion.38
  179.5 0.2 select_reduce_fusion
  179.8 0.1 exponential_reduce_fusion
  179.9 0.2 select_reduce_fusion.3
  180.1 0.3 convolution_convert_fusion.1
  180.4 0.8 reshape.298.part
  181.2 13.3 %shard_map.144 = bf16[16,4,2048]{2,1,0:T(4,128)(2,1)} custom-call(bf16[16,4,2048]{2,1,0:T(4,128)(2,1)} %reshape.298.part), custom_call_target="tpu_custom_call" | custom-call | tf_op jit(solution)/shard_map/pallas_call | solution.py:287
  194.4 1.0 reshape.299
  195.5 4.0 %fusion = f32[64,1536]{1,0:T(8,128)S(1)} fusion(bf16[64,2048]{1,0:T(8,128)(2,1)S(1)} %reshape.299, bf16[1,2048,1536]{2,1,0:T(8,128)(2,1)} %param.23), kind=kOutput, calls=%fused_computation | convolution fusion | flops 402653184 | bytes 6946816 | tf_op jit(solution)/shard_map/dot_general | solution.py:495
  199.4 0.7 fusion.6
  200.1 0.8 reshape.300.part
  200.9 8.8 %shard_map.145 = bf16[16,4,2048]{2,1,0:T(4,128)(2,1)} custom-call(bf16[16,4,2048]{2,1,0:T(4,128)(2,1)} %reshape.300.part), custom_call_target="tpu_custom_call" | custom-call | tf_op jit(solution)/shard_map/pallas_call | solution.py:287
  209.8 1.0 reshape.301
  210.8 1.0 fusion.5
  (26 shorter events, 0.1 us)
Async XLA Ops:
  0.6 198.8 %copy-start = (bf16[1,768,2048]{2,1,0:T(8,128)(2,1)S(1)}, bf16[1,768,2048]{2,1,0:T(8,128)(2,1)}, u32[]{:S(2)}) copy-start(bf16[1,768,2048]{2,1,0:T(8,128)(2,1)} %param.24) | copy-start | bytes 9437188
  79.9 6.9 %copy-start.9 = (f32[128]{0:T(128)S(1)}, f32[128]{0:T(128)}, u32[]{:S(2)}) copy-start(f32[128]{0:T(128)} %param.20) | copy-start | bytes 1540
  85.1 1.0 copy-start.5
  86.8 12.3 %copy-start.8 = (s32[64,8]{0,1:T(8,128)S(1)}, s32[64,8]{0,1:T(8,128)}, u32[]{:S(2)}) copy-start(s32[64,8]{0,1:T(8,128)} %param.25) | copy-start | bytes 6148
  86.8 7.3 %copy-start.6 = (bf16[1024,512]{1,0:T(8,128)(2,1)S(1)}, bf16[1024,512]{1,0:T(8,128)(2,1)}, u32[]{:S(2)}) copy-start(bf16[1024,512]{1,0:T(8,128)(2,1)} %copy-done.5) | copy-start | bytes 3145732
  92.5 22.4 %collective-permute-start = (bf16[2,1024,128]{2,1,0:T(8,128)(2,1)}, bf16[2,1024,128]{2,1,0:T(8,128)(2,1)}, u32[]{:S(2)}, u32[]{:S(2)}) collective-permute-start(bf16[2,1024,128]{2,1,0:T(8,128)(2,1)} %pad_maximum_fusion.1), channel_id=1, source_target_pairs={{0,16},{16,0},{32,48},{48,32},{64,80},{80,64},{96,112},{112,96},{1... | collective-permute-start | bytes 1572872 | tf_op jit(solution)/shard_map/ppermute | solution.py:29
  94.1 10.6 %copy-start.10 = (f32[128]{0:T(128)S(1)}, f32[128]{0:T(128)}, u32[]{:S(2)}) copy-start(f32[128]{0:T(128)} %param.19) | copy-start | bytes 1540
  102.2 6.2 %copy-start.3 = (f32[1024,64]{1,0:T(8,128)S(1)}, f32[1024,64]{1,0:T(8,128)}, u32[]{:S(2)}) copy-start(f32[1024,64]{1,0:T(8,128)} %get-tuple-element.24) | copy-start | bytes 786436
  102.2 6.2 %copy-start.4 = (f32[1024,64]{1,0:T(8,128)S(1)}, f32[1024,64]{1,0:T(8,128)}, u32[]{:S(2)}) copy-start(f32[1024,64]{1,0:T(8,128)} %get-tuple-element.25) | copy-start | bytes 786436
  104.8 8.0 %copy-start.11 = (s32[8]{0:T(128)S(1)}, s32[8]{0:T(128)}, u32[]{:S(2)}) copy-start(s32[8]{0:T(128)} %param.21) | copy-start | bytes 100
  144.1 33.8 %copy-start.1 = (bf16[64,2048]{1,0:T(8,128)(2,1)S(1)}, bf16[64,2048]{1,0:T(8,128)(2,1)}, u32[]{:S(2)}) copy-start(bf16[64,2048]{1,0:T(8,128)(2,1)} %param.13) | copy-start | bytes 786436
  144.1 34.0 %copy-start.7 = (f32[2048]{0:T(1024)S(1)}, f32[2048]{0:T(1024)}, u32[]{:S(2)}) copy-start(f32[2048]{0:T(1024)} %param.15) | copy-start | bytes 24580
  178.1 2.0 copy-start.2

commit v5 on v4

--- a/solution.py
+++ b/solution.py
@@ -2,6 +2,7 @@
 import math
 
 import jax
+import numpy as np
 import jax.numpy as jnp
 from jax import lax
 from jax.experimental import pallas as pl
@@ -374,6 +375,80 @@
     return indices + offset
 
 
+def prep_kernel(x_ref, wq_ref, wk_ref, wv_ref, cos_ref, sin_ref, qg_ref, kg_ref, q_out, k_out, v_out):
+    x = x_ref[...]
+    cosines = cos_ref[...]
+    sines = sin_ref[...]
+    depth = cosines.shape[1]
+
+    def project(w_ref):
+        return jnp.dot(x, w_ref[...], preferred_element_type=jnp.float32).astype(jnp.bfloat16)
+
+    def norm_rope(values, gain):
+        values = values.astype(jnp.float32)
+        inverse_rms = lax.rsqrt(jnp.mean(values * values, axis=-1, keepdims=True) + epsilon)
+        normed = values * inverse_rms * gain
+        return (normed * cosines + pltpu.roll(normed, depth // 2, 1) * sines).astype(jnp.bfloat16)
+
+    queries = project(wq_ref)
+    for h in range(queries.shape[1] // depth):
+        q_out[:, h * depth : (h + 1) * depth] = norm_rope(
+            queries[:, h * depth : (h + 1) * depth], qg_ref[...]
+        )
+    k_out[...] = norm_rope(project(wk_ref), kg_ref[...])
+    v_out[...] = project(wv_ref)
+
+
+def prep(normed_rows, wq, wk, wv, cosines, sines, query_gain, key_gain):
+    rows, width = normed_rows.shape
+    depth = wk.shape[1]
+    block = min(256, rows)
+    whole = lambda shape: pl.BlockSpec(shape, lambda i: (0, 0))
+    per_row = lambda cols: pl.BlockSpec((block, cols), lambda i: (i, 0))
+    return pl.pallas_call(
+        prep_kernel,
+        out_shape=(
+            jax.ShapeDtypeStruct((rows, wq.shape[1]), jnp.bfloat16),
+            jax.ShapeDtypeStruct((rows, depth), jnp.bfloat16),
+            jax.ShapeDtypeStruct((rows, depth), jnp.bfloat16),
+        ),
+        grid=(rows // block,),
+        in_specs=[
+            per_row(width),
+            whole(wq.shape),
+            whole(wk.shape),
+            whole(wv.shape),
+            per_row(depth),
+            per_row(depth),
+            whole((1, depth)),
+            whole((1, depth)),
+        ],
+        out_specs=(per_row(wq.shape[1]), per_row(depth), per_row(depth)),
+        cost_estimate=pl.CostEstimate(
+            flops=2 * rows * width * (wq.shape[1] + 2 * depth),
+            transcendentals=rows * (wq.shape[1] // depth + 1),
+            bytes_accessed=2 * (rows * width + width * (wq.shape[1] + 2 * depth) + rows * (wq.shape[1] + 2 * depth)),
+        ),
+    )(normed_rows, wq, wk, wv, cosines, sines, query_gain.reshape(1, depth), key_gain.reshape(1, depth))
+
+
+def rope_tables(parity, row_count, depth):
+    half = depth // 2
+    frequencies = rope_theta ** (-2.0 * np.arange(half) / depth)
+    indices = np.arange(row_count)
+    quarter = row_count // 2
+    places = np.concatenate([np.where(indices < quarter, indices, indices + 2 * quarter), indices + quarter])
+    angles = places[:, None].astype(np.float64) * frequencies[None, :]
+    cosines = jnp.asarray(np.cos(angles), jnp.float32)
+    sines = jnp.asarray(np.sin(angles), jnp.float32)
+    cosines = lax.dynamic_slice_in_dim(cosines, parity * row_count, row_count, 0)
+    sines = lax.dynamic_slice_in_dim(sines, parity * row_count, row_count, 0)
+    return (
+        jnp.concatenate([cosines, cosines], axis=1),
+        jnp.concatenate([-sines, sines], axis=1),
+    )
+
+
 def per_device(
     hidden_in,
     norm_attention,
@@ -410,34 +485,21 @@
         experts_axis,
     )
     model_width = hidden_in.shape[1]
-    joined_weights = jnp.concatenate(
-        [
-            query_parts.reshape(model_width, -1),
-            key_parts.reshape(model_width, -1),
-            value_parts.reshape(model_width, -1),
-        ],
-        axis=1,
-    )
-    projected = jnp.dot(
-        normed_parts.reshape(-1, model_width),
-        joined_weights,
-        preferred_element_type=jnp.float32,
-    ).astype(jnp.bfloat16)
-    local_rows = projected.shape[0]
-    query_rows_list = projected[:, :width_here].reshape(
-        local_rows, local_head_count, HEAD_DIMENSION
-    )
-    key_rows = projected[:, width_here : width_here + HEAD_DIMENSION]
-    value_rows = projected[:, width_here + HEAD_DIMENSION :]
+    local_rows = normed_parts.shape[0] * normed_parts.shape[1]
     parity = group_index % 2
     own_places = local_positions(parity, local_rows)
     partner_places = local_positions(1 - parity, local_rows)
-    query_rows_list = rotate(
-        norm_rows(query_rows_list, query_gain), own_places.astype(jnp.float32)
-    ).astype(jnp.bfloat16)
-    key_rows = rotate(norm_rows(key_rows[:, None, :], key_gain), own_places.astype(jnp.float32))[
-        :, 0, :
-    ].astype(jnp.bfloat16)
+    cosines, sines = rope_tables(parity, local_rows, HEAD_DIMENSION)
+    query_rows_list, key_rows, value_rows = prep(
+        normed_parts.reshape(local_rows, model_width),
+        query_parts.reshape(model_width, -1),
+        key_parts.reshape(model_width, -1),
+        value_parts.reshape(model_width, -1),
+        cosines,
+        sines,
+        query_gain,
+        key_gain,
+    )
     partner = from_partner(jnp.stack([key_rows, value_rows]), "group", 0)
     all_keys = jnp.concatenate([key_rows, partner[0]], axis=0)
     all_values = jnp.concatenate([value_rows, partner[1]], axis=0)
@@ -446,7 +508,7 @@
     past_end = jnp.full_like(key_places, 4 * key_places.shape[0])
     key_limits = jnp.where(key_places < valid_length, key_places, past_end)
     attended = attention(
-        query_rows_list.reshape(local_rows, width_here),
+        query_rows_list,
         all_keys,
         all_values,
         own_places,

time: 212 us -> 203 us (0.958)
  other arithmetic: 39.2 us -> 24.5 us
  Pallas kernels: 142 us -> 150 us
  waiting for transfers between devices: 0.01 us -> 7.15 us
  local copies, waits for them, and re-layouts: 11.7 us -> 6.53 us
  matrix products: 17 us -> 11.9 us
    ppermute x1, waiting for transfers between devices: 0.01 us -> 7.15 us  [from_partner(): return lax.ppermute(block, axis, route)]
    pallas_call x0 -> x1, Pallas kernels: none -> 7.04 us  [prep(): pl.pallas_call(prep_kernel, out_shape=(jax.ShapeDtypeStruct((rows, wq.sha...]
    dot_general x1 -> x0, matrix products: 5.14 us -> none  [per_device(): jnp.dot(normed_parts.reshape(-1, model_width), joined_weights, preferred_...]
    mul x2 -> x0, other arithmetic: 4.81 us -> none  [norm_rows(): return widened * inverse_rms * gain_vector]
    cos x1 -> x0, other arithmetic: 3.04 us -> none  [rotate(): cosine_values = jnp.cos(angles)]
    convert_element_type x1 -> x0, local copies, waits for them, and re-layouts: 2.78 us -> none  [norm_rows(): widened = values.astype(jnp.float32)]
    reduce_sum x4 -> x2, other arithmetic: 3.99 us -> 1.29 us  [norm_rows(): jnp.mean(widened * widened, axis=-1, keepdims=True) + epsilon]
    sub x1 -> x0, other arithmetic: 2.42 us -> none  [rotate(): first_half * cosine_values - second * sine_values]
  transfers between devices with their start and end apart: 1 -> 1, of which waited for: 0 -> 1; matrix products, arithmetic and copies ran while one was open for 10% -> 2% of each run, Pallas kernels for 0% -> 0%
where the time goes in v5:
time: 203 us; the launch traced here: 202 us
  Pallas kernels  150 us (74%)
  other arithmetic  24.5 us (12%)
  matrix products  11.9 us (6%)
  waiting for transfers between devices  7.15 us (4%)
  local copies, waits for them, and re-layouts  6.53 us (3%)
    pallas_call x1, Pallas kernels, gather_all(): pl.pallas_call(functools.partial(gather_kernel, n_group, n_expert), out_s...  71.5 us
    pallas_call x1, Pallas kernels, scatter_to_chips(): pl.pallas_call(functools.partial(chip_scatter_kernel, chips), out_shape=j...  31.8 us
    pallas_call x2, Pallas kernels, scatter_blocks(): pl.pallas_call(functools.partial(scatter_kernel, n_expert), out_shape=jax...  22.1 us
    pallas_call x1, Pallas kernels, attention(): pl.pallas_call(functools.partial(attention_kernel, scale, width // depth)...  9 us
    pallas_call x1, Pallas kernels, exchange_with_mate(): pl.pallas_call(mate_kernel, out_shape=jax.ShapeDtypeStruct(shape, part.dt...  8.75 us
    ppermute x1, waiting for transfers between devices, from_partner(): return lax.ppermute(block, axis, route)  7.15 us
    pallas_call x1, Pallas kernels, prep(): pl.pallas_call(prep_kernel, out_shape=(jax.ShapeDtypeStruct((rows, wq.sha...  7.04 us
    dot_general x1, matrix products, per_device(): jnp.dot(attended, output_parts, preferred_element_type=jnp.float32)  4.57 us
  transfers between devices with their start and end apart: 1, of which 1 were waited for; matrix products, arithmetic and copies ran while one was open for 2% of the time, Pallas kernels for 0%

profile of v5, /device:TPU:1, one launch (start us, length us, event | category | flops | bytes accessed | tf_op | source)
XLA Modules:
  0.0 202.0 jit_solution(551062011647485864)
XLA Ops:
  0.6 0.0 copy-start
  0.6 0.0 copy-start.1
  0.7 0.0 copy-start.4
  0.7 1.1 dynamic-slice_convert_fusion
  1.8 0.6 slice_bitcast_fusion.2
  2.4 1.1 fusion.12
  3.5 1.6 convert_element_type.60.wq
  5.1 1.5 convert_element_type.62.wo
  6.6 1.3 dynamic-slice_negate_fusion
  7.9 1.0 pad_maximum_fusion.cos_ref
  8.9 0.0 copy-done.1
  8.9 0.0 copy-done.4
  8.9 0.8 fusion.14.xn
  9.7 1.1 pad_maximum_fusion.1.sin_ref
  10.8 71.5 %shard_map.158 = (bf16[16,128,256]{2,1,0:T(8,128)(2,1)}, bf16[16,128,128]{2,1,0:T(8,128)(2,1)}, bf16[16,128,128]{2,1,0:T(8,128)(2,1)}, bf16[256,2048]{1,0:T(8,128)(2,1)}, bf16[16,64,2048]{2,1,0:T(8,128)(2,1)}) custom-call(bf16[128,256]{1,0:T(8,128)(2,1)} %convert_element_type.60.wq, bf16[128,128]{1,0:T(8,128)(2,1)} %get-tuple-element.25.wk, ...), custom_call_target="tpu_custom_call" | custom-call | tf_op jit(solution)/shard_map/pallas_call | solution.py:164
  82.3 0.0 copy-start.5
  82.4 0.0 copy-start.6
  82.4 7.0 %shard_map.159 = (bf16[1024,256]{1,0:T(8,128)(2,1)}, bf16[1024,128]{1,0:T(8,128)(2,1)}, bf16[1024,128]{1,0:T(8,128)(2,1)}) custom-call(bf16[1024,2048]{1,0:T(8,128)(2,1)} %bitcast.43, bf16[2048,256]{1,0:T(8,128)(2,1)} %bitcast.44, bf16[2048,128]{1,0:T(8,128)(2,1)} %bitcast.45, bf16[2048,128]{1,0:T(8,128)(2,1)} %bitcast.46, ...), custom_call_target="tpu_custom_call" | custom-call | flops 2147483648 | bytes 7340032 | tf_op jit(solution)/shard_map/pallas_call | solution.py:408
  89.4 1.9 pad_maximum_fusion.2
  91.3 0.8 collective-permute-start
  92.1 0.8 select_add_fusion.qpos_ref
  93.0 0.0 copy-done.5
  93.0 0.1 copy.22
  93.1 0.1 fusion.35
  93.2 0.1 select_reduce_fusion.2
  93.3 0.1 fusion.26
  93.4 0.1 reduce_window_sum.11
  93.5 0.2 select_reduce_fusion.1
  93.7 0.0 copy-done.6
  93.7 0.7 fusion.33
  94.4 1.3 compare_select_fusion.kpos_ref
  95.7 7.1 %collective-permute-done = bf16[2,1024,128]{2,1,0:T(8,128)(2,1)} collective-permute-done((bf16[2,1024,128]{2,1,0:T(8,128)(2,1)}, bf16[2,1024,128]{2,1,0:T(8,128)(2,1)}, u32[]{:S(2)}, u32[]{:S(2)}) %collective-permute-start) | collective-permute-done | bytes 524320 | tf_op jit(solution)/shard_map/ppermute | solution.py:30
  102.8 1.1 slice_bitcast_fusion
  103.9 1.8 pad_maximum_fusion.4.v_ref
  105.7 1.8 pad_maximum_fusion.3.k_ref
  107.5 9.0 %shard_map.160 = bf16[1024,256]{1,0:T(8,128)(2,1)} custom-call(bf16[1024,256]{1,0:T(8,128)(2,1)} %get-tuple-element.14.q_ref, bf16[2048,128]{1,0:T(8,128)(2,1)} %pad_maximum_fusion.3.k_ref, bf16[2048,128]{1,0:T(8,128)(2,1)} %pad_maximum_fusion.4.v_ref, s32[1024,1]{1,0:T(8,128)} %select_add_fusion.qpos_ref, s32[1,2048]{1,0:T(1,128)} %compare_select_fusion.kpos_ref), custom_call_target="tpu_custom_call" | custom-call | flops 2147483648 | bytes 2097152 | tf_op jit(solution)/shard_map/pallas_call | solution.py:327
  116.5 4.6 %convolution_convert_fusion = bf16[1024,2048]{1,0:T(8,128)(2,1)} fusion(bf16[1024,256]{1,0:T(8,128)(2,1)} %shard_map.160, bf16[256,2048]{1,0:T(8,128)(2,1)} %get-tuple-element.17), kind=kOutput, calls=%fused_computation.5 | convolution fusion | flops 1075838976 | bytes 5767168 | tf_op jit(solution)/shard_map/dot_general | solution.py:518
  121.1 8.8 %shard_map.161 = bf16[8,64,2048]{2,1,0:T(8,128)(2,1)} custom-call(bf16[8,2,64,2048]{3,2,1,0:T(8,128)(2,1)} %bitcast.37), custom_call_target="tpu_custom_call" | custom-call | tf_op jit(solution)/shard_map/pallas_call | solution.py:203
  129.8 4.5 %fusion.2.part = bf16[8,64,2048]{2,1,0:T(8,128)(2,1)} fusion(bf16[8,64,2048]{2,1,0:T(8,128)(2,1)} %shard_map.161, bf16[8,2,64,2048]{3,2,1,0:T(8,128)(2,1)} %bitcast.38, s32[]{:T(128)S(6)} %select_n.149), kind=kLoop, calls=%fused_computation.3 | loop fusion | flops 4194304 | bytes 6291460 | tf_op jit(solution)/shard_map/convert_element_type | solution.py:524
  134.3 0.0 copy-start.3
  134.3 31.8 %shard_map.162 = bf16[8,64,2048]{2,1,0:T(8,128)(2,1)} custom-call(bf16[8,64,2048]{2,1,0:T(8,128)(2,1)} %fusion.2.part), custom_call_target="tpu_custom_call" | custom-call | tf_op jit(solution)/shard_map/pallas_call | solution.py:245
  166.1 2.0 convert_reduce_fusion
  168.1 0.2 fusion.9
  168.3 0.0 copy-start.2
  168.3 0.0 copy-done.3
  168.3 1.4 fusion.20
  169.8 0.2 select_reduce_fusion
  170.0 0.1 exponential_reduce_fusion
  170.1 0.2 select_reduce_fusion.3
  170.3 0.0 copy-done.2
  170.3 0.3 convolution_convert_fusion.1
  170.6 0.8 reshape.140.part
  171.4 13.3 %shard_map.163 = bf16[16,4,2048]{2,1,0:T(4,128)(2,1)} custom-call(bf16[16,4,2048]{2,1,0:T(4,128)(2,1)} %reshape.140.part), custom_call_target="tpu_custom_call" | custom-call | tf_op jit(solution)/shard_map/pallas_call | solution.py:288
  184.7 1.0 reshape.141
  185.7 4.0 %fusion = f32[64,1536]{1,0:T(8,128)S(1)} fusion(bf16[64,2048]{1,0:T(8,128)(2,1)S(1)} %reshape.141, bf16[1,2048,1536]{2,1,0:T(8,128)(2,1)} %param.25), kind=kOutput, calls=%fused_computation | convolution fusion | flops 402653184 | bytes 6946816 | tf_op jit(solution)/shard_map/dot_general | solution.py:557
  189.7 0.0 copy-done
  189.7 0.7 fusion.6
  190.3 0.8 reshape.142.part
  191.2 8.8 %shard_map.164 = bf16[16,4,2048]{2,1,0:T(4,128)(2,1)} custom-call(bf16[16,4,2048]{2,1,0:T(4,128)(2,1)} %reshape.142.part), custom_call_target="tpu_custom_call" | custom-call | tf_op jit(solution)/shard_map/pallas_call | solution.py:288
  200.0 1.0 reshape.143
  201.0 1.0 fusion.5
  (5 shorter events, 0.0 us)
Async XLA Ops:
  0.6 189.0 %copy-start = (bf16[1,768,2048]{2,1,0:T(8,128)(2,1)S(1)}, bf16[1,768,2048]{2,1,0:T(8,128)(2,1)}, u32[]{:S(2)}) copy-start(bf16[1,768,2048]{2,1,0:T(8,128)(2,1)} %param.26) | copy-start | bytes 9437188
  0.6 8.3 %copy-start.1 = (bf16[64,2048]{1,0:T(8,128)(2,1)S(1)}, bf16[64,2048]{1,0:T(8,128)(2,1)}, u32[]{:S(2)}) copy-start(bf16[64,2048]{1,0:T(8,128)(2,1)} %param.15) | copy-start | bytes 786436
  0.7 8.3 %copy-start.4 = (f32[2048]{0:T(1024)S(1)}, f32[2048]{0:T(1024)}, u32[]{:S(2)}) copy-start(f32[2048]{0:T(1024)} %param.16) | copy-start | bytes 24580
  82.3 10.6 %copy-start.5 = (s32[64,8]{0,1:T(8,128)S(1)}, s32[64,8]{0,1:T(8,128)}, u32[]{:S(2)}) copy-start(s32[64,8]{0,1:T(8,128)} %param.27) | copy-start | bytes 6148
  82.4 11.3 %copy-start.6 = (s32[8]{0:T(128)S(1)}, s32[8]{0:T(128)}, u32[]{:S(2)}) copy-start(s32[8]{0:T(128)} %param.23) | copy-start | bytes 100
  91.3 11.6 %collective-permute-start = (bf16[2,1024,128]{2,1,0:T(8,128)(2,1)}, bf16[2,1024,128]{2,1,0:T(8,128)(2,1)}, u32[]{:S(2)}, u32[]{:S(2)}) collective-permute-start(bf16[2,1024,128]{2,1,0:T(8,128)(2,1)} %pad_maximum_fusion.2), channel_id=1, source_target_pairs={{0,16},{16,0},{32,48},{48,32},{64,80},{80,64},{96,112},{112,96},{1... | collective-permute-start | bytes 1572872 | tf_op jit(solution)/shard_map/ppermute | solution.py:30
  134.3 34.1 %copy-start.3 = (f32[2048]{0:T(1024)S(1)}, f32[2048]{0:T(1024)}, u32[]{:S(2)}) copy-start(f32[2048]{0:T(1024)} %param.17) | copy-start | bytes 24580
  168.3 2.0 copy-start.2

commit v6 on v5

--- a/solution.py
+++ b/solution.py
@@ -375,6 +375,49 @@
     return indices + offset
 
 
+def pair_keys_kernel(k_ref, v_ref, k_all, v_all, send, recv, local):
+    g = lax.axis_index("group")
+    e = lax.axis_index("expert")
+    pair_dev = (g + 1 - 2 * lax.rem(g, 2), e)
+    rows = k_ref.shape[0]
+    barrier = pltpu.get_barrier_semaphore()
+    pl.semaphore_signal(barrier, 1, device_id=pair_dev, device_id_type=MESH)
+    pl.semaphore_wait(barrier, 1)
+    copies = []
+    for i, (src, dst) in enumerate(((k_ref, k_all), (v_ref, v_all))):
+        copy = pltpu.make_async_remote_copy(
+            src_ref=src,
+            dst_ref=dst.at[pl.ds(rows, rows)],
+            send_sem=send.at[i],
+            recv_sem=recv.at[i],
+            device_id=pair_dev,
+            device_id_type=MESH,
+        )
+        copy.start()
+        copies.append(copy)
+    own = [
+        pltpu.make_async_copy(src, dst.at[pl.ds(0, rows)], local.at[i])
+        for i, (src, dst) in enumerate(((k_ref, k_all), (v_ref, v_all)))
+    ]
+    for copy in own:
+        copy.start()
+    for copy in copies + own:
+        copy.wait()
+
+
+def pair_keys(keys, values):
+    any_spec = pl.BlockSpec(memory_space=pl.ANY)
+    shape = jax.ShapeDtypeStruct((2 * keys.shape[0], keys.shape[1]), keys.dtype)
+    return pl.pallas_call(
+        pair_keys_kernel,
+        out_shape=(shape, shape),
+        in_specs=[any_spec, any_spec],
+        out_specs=(any_spec, any_spec),
+        scratch_shapes=[pltpu.SemaphoreType.DMA((2,))] * 3,
+        compiler_params=pltpu.CompilerParams(collective_id=6, has_side_effects=True),
+    )(keys, values)
+
+
 def prep_kernel(x_ref, wq_ref, wk_ref, wv_ref, cos_ref, sin_ref, qg_ref, kg_ref, q_out, k_out, v_out):
     x = x_ref[...]
     cosines = cos_ref[...]
@@ -500,9 +543,7 @@
         query_gain,
         key_gain,
     )
-    partner = from_partner(jnp.stack([key_rows, value_rows]), "group", 0)
-    all_keys = jnp.concatenate([key_rows, partner[0]], axis=0)
-    all_values = jnp.concatenate([value_rows, partner[1]], axis=0)
+    all_keys, all_values = pair_keys(key_rows, value_rows)
     key_places = jnp.concatenate([own_places, partner_places])
     valid_length = jnp.sum(jnp.where(jnp.arange(lengths.shape[0]) == group_index // 2, lengths, 0))
     past_end = jnp.full_like(key_places, 4 * key_places.shape[0])

time: 203 us -> 207 us (1.020)
  Pallas kernels: 150 us -> 167 us
  waiting for transfers between devices: 7.15 us -> 0 us
  other arithmetic: 24.5 us -> 19.9 us
    pallas_call x0 -> x1, Pallas kernels: none -> 17.9 us  [pair_keys(): pl.pallas_call(pair_keys_kernel, out_shape=(shape, shape), in_specs=[any_...]
    ppermute x1 -> x0, waiting for transfers between devices: 7.15 us -> none  [from_partner(): return lax.ppermute(block, axis, route)]
    concatenate x2 -> x0, other arithmetic: 3.57 us -> none  [the longest x1 1.8 us: per_device(): all_values = jnp.concatenate([value_rows, partner[1]], axis=0)]
  transfers between devices with their start and end apart: 1 -> 0, of which waited for: 1 -> 0; matrix products, arithmetic and copies ran while one was open for 2% -> 0% of each run, Pallas kernels for 0% -> 0%
where the time goes in v6:
time: 207 us; the launch traced here: 206 us
  Pallas kernels  167 us (81%)
  other arithmetic  19.9 us (10%)
  matrix products  12.8 us (6%)
  local copies, waits for them, and re-layouts  6.14 us (3%)
    pallas_call x1, Pallas kernels, gather_all(): pl.pallas_call(functools.partial(gather_kernel, n_group, n_expert), out_s...  71.5 us
    pallas_call x1, Pallas kernels, scatter_to_chips(): pl.pallas_call(functools.partial(chip_scatter_kernel, chips), out_shape=j...  31.8 us
    pallas_call x2, Pallas kernels, scatter_blocks(): pl.pallas_call(functools.partial(scatter_kernel, n_expert), out_shape=jax...  22.1 us
    pallas_call x1, Pallas kernels, pair_keys(): pl.pallas_call(pair_keys_kernel, out_shape=(shape, shape), in_specs=[any_...  17.9 us
    pallas_call x1, Pallas kernels, attention(): pl.pallas_call(functools.partial(attention_kernel, scale, width // depth)...  9.01 us
    pallas_call x1, Pallas kernels, exchange_with_mate(): pl.pallas_call(mate_kernel, out_shape=jax.ShapeDtypeStruct(shape, part.dt...  7.54 us
    pallas_call x1, Pallas kernels, prep(): pl.pallas_call(prep_kernel, out_shape=(jax.ShapeDtypeStruct((rows, wq.sha...  7.02 us
    dot_general x1, matrix products, per_device(): jnp.dot(attended, output_parts, preferred_element_type=jnp.float32)  4.57 us

profile of v6, /device:TPU:1, one launch (start us, length us, event | category | flops | bytes accessed | tf_op | source)
XLA Modules:
  0.0 206.5 jit_solution(14639954498275940249)
XLA Ops:
  0.6 0.0 copy-start
  0.7 1.1 dynamic-slice_convert_fusion
  1.7 0.6 slice_bitcast_fusion
  2.4 1.1 fusion.12
  3.5 1.8 fusion.14.xn
  5.3 1.5 convert_element_type.60.wq
  6.8 1.5 convert_element_type.62.wo
  8.3 71.5 %shard_map.158 = (bf16[16,128,256]{2,1,0:T(8,128)(2,1)}, bf16[16,128,128]{2,1,0:T(8,128)(2,1)}, bf16[16,128,128]{2,1,0:T(8,128)(2,1)}, bf16[256,2048]{1,0:T(8,128)(2,1)}, bf16[16,64,2048]{2,1,0:T(8,128)(2,1)}) custom-call(bf16[128,256]{1,0:T(8,128)(2,1)} %convert_element_type.60.wq, bf16[128,128]{1,0:T(8,128)(2,1)} %get-tuple-element.27.wk, ...), custom_call_target="tpu_custom_call" | custom-call | tf_op jit(solution)/shard_map/pallas_call | solution.py:164
  79.9 1.3 dynamic-slice_negate_fusion
  81.2 1.1 pad_maximum_fusion.1.sin_ref
  82.3 1.0 pad_maximum_fusion.cos_ref
  83.3 0.0 copy-start.5
  83.3 7.0 %shard_map.159 = (bf16[1024,256]{1,0:T(8,128)(2,1)}, bf16[1024,128]{1,0:T(8,128)(2,1)}, bf16[1024,128]{1,0:T(8,128)(2,1)}) custom-call(bf16[1024,2048]{1,0:T(8,128)(2,1)} %bitcast.35, bf16[2048,256]{1,0:T(8,128)(2,1)} %bitcast.36, bf16[2048,128]{1,0:T(8,128)(2,1)} %bitcast.37, bf16[2048,128]{1,0:T(8,128)(2,1)} %bitcast.38, ...), custom_call_target="tpu_custom_call" | custom-call | flops 2147483648 | bytes 7340032 | tf_op jit(solution)/shard_map/pallas_call | solution.py:451
  90.3 17.9 %shard_map.160 = (bf16[2048,128]{1,0:T(8,128)(2,1)}, bf16[2048,128]{1,0:T(8,128)(2,1)}) custom-call(bf16[1024,128]{1,0:T(8,128)(2,1)} %get-tuple-element.17.k_ref, bf16[1024,128]{1,0:T(8,128)(2,1)} %get-tuple-element.18.v_ref), custom_call_target="tpu_custom_call" | custom-call | tf_op jit(solution)/shard_map/pallas_call | solution.py:411
  108.2 0.9 select_add_fusion.qpos_ref
  109.1 0.0 copy-done.5
  109.1 0.6 fusion.33
  109.7 1.3 compare_select_fusion.kpos_ref
  111.0 9.0 %shard_map.161 = bf16[1024,256]{1,0:T(8,128)(2,1)} custom-call(bf16[1024,256]{1,0:T(8,128)(2,1)} %get-tuple-element.16.q_ref, bf16[2048,128]{1,0:T(8,128)(2,1)} %get-tuple-element.19.k_ref, bf16[2048,128]{1,0:T(8,128)(2,1)} %get-tuple-element.20.v_ref, s32[1024,1]{1,0:T(8,128)} %select_add_fusion.qpos_ref, s32[1,2048]{1,0:T(1,128)} %compare_select_fusion.kpos_ref), custom_call_target="tpu_custom_call" | custom-call | flops 2147483648 | bytes 2097152 | tf_op jit(solution)/shard_map/pallas_call | solution.py:327
  120.0 4.6 %convolution_convert_fusion = bf16[1024,2048]{1,0:T(8,128)(2,1)} fusion(bf16[1024,256]{1,0:T(8,128)(2,1)} %shard_map.161, bf16[256,2048]{1,0:T(8,128)(2,1)} %get-tuple-element.21), kind=kOutput, calls=%fused_computation.5 | convolution fusion | flops 1075838976 | bytes 5767168 | tf_op jit(solution)/shard_map/dot_general | solution.py:559
  124.5 7.5 %shard_map.162 = bf16[8,64,2048]{2,1,0:T(8,128)(2,1)} custom-call(bf16[8,2,64,2048]{3,2,1,0:T(8,128)(2,1)} %bitcast.31), custom_call_target="tpu_custom_call" | custom-call | tf_op jit(solution)/shard_map/pallas_call | solution.py:203
  132.1 4.5 %fusion.2.part = bf16[8,64,2048]{2,1,0:T(8,128)(2,1)} fusion(bf16[8,64,2048]{2,1,0:T(8,128)(2,1)} %shard_map.162, bf16[8,2,64,2048]{3,2,1,0:T(8,128)(2,1)} %bitcast.32, s32[]{:T(128)S(6)} %select_n.149), kind=kLoop, calls=%fused_computation.3 | loop fusion | flops 4194304 | bytes 6291460 | tf_op jit(solution)/shard_map/convert_element_type | solution.py:565
  136.6 0.0 copy-start.1
  136.6 0.0 copy-start.3
  136.6 0.0 copy-start.4
  136.6 31.8 %shard_map.163 = bf16[8,64,2048]{2,1,0:T(8,128)(2,1)} custom-call(bf16[8,64,2048]{2,1,0:T(8,128)(2,1)} %fusion.2.part), custom_call_target="tpu_custom_call" | custom-call | tf_op jit(solution)/shard_map/pallas_call | solution.py:245
  168.3 2.0 convert_reduce_fusion
  170.4 0.0 copy-done.1
  170.4 0.2 fusion.9
  170.6 0.0 copy-start.2
  170.6 0.7 copy-done.2
  171.3 0.0 copy-done.3
  171.3 1.3 fusion.20
  172.6 0.0 copy-done.4
  172.6 0.1 copy.22
  172.7 0.2 select_reduce_fusion
  172.9 0.1 exponential_reduce_fusion
  173.0 0.2 select_reduce_fusion.3
  173.2 0.1 fusion.35
  173.3 0.1 select_reduce_fusion.2
  173.5 0.1 fusion.26
  173.6 0.1 reduce_window_sum.11
  173.7 0.2 select_reduce_fusion.1
  173.8 1.2 convolution_convert_fusion.1
  175.1 0.8 reshape.140.part
  175.9 13.2 %shard_map.164 = bf16[16,4,2048]{2,1,0:T(4,128)(2,1)} custom-call(bf16[16,4,2048]{2,1,0:T(4,128)(2,1)} %reshape.140.part), custom_call_target="tpu_custom_call" | custom-call | tf_op jit(solution)/shard_map/pallas_call | solution.py:288
  189.2 1.0 reshape.141
  190.2 4.0 %fusion = f32[64,1536]{1,0:T(8,128)S(1)} fusion(bf16[64,2048]{1,0:T(8,128)(2,1)S(1)} %reshape.141, bf16[1,2048,1536]{2,1,0:T(8,128)(2,1)} %param.25), kind=kOutput, calls=%fused_computation | convolution fusion | flops 402653184 | bytes 6946816 | tf_op jit(solution)/shard_map/dot_general | solution.py:598
  194.1 0.0 copy-done
  194.2 0.7 fusion.6
  194.8 0.8 reshape.142.part
  195.6 8.8 %shard_map.165 = bf16[16,4,2048]{2,1,0:T(4,128)(2,1)} custom-call(bf16[16,4,2048]{2,1,0:T(4,128)(2,1)} %reshape.142.part), custom_call_target="tpu_custom_call" | custom-call | tf_op jit(solution)/shard_map/pallas_call | solution.py:288
  204.5 1.0 reshape.143
  205.5 1.0 fusion.5
  (5 shorter events, 0.0 us)
Async XLA Ops:
  0.6 193.5 %copy-start = (bf16[1,768,2048]{2,1,0:T(8,128)(2,1)S(1)}, bf16[1,768,2048]{2,1,0:T(8,128)(2,1)}, u32[]{:S(2)}) copy-start(bf16[1,768,2048]{2,1,0:T(8,128)(2,1)} %param.26) | copy-start | bytes 9437188
  83.3 25.8 %copy-start.5 = (s32[8]{0:T(128)S(1)}, s32[8]{0:T(128)}, u32[]{:S(2)}) copy-start(s32[8]{0:T(128)} %param.23) | copy-start | bytes 100
  136.6 33.8 %copy-start.1 = (bf16[64,2048]{1,0:T(8,128)(2,1)S(1)}, bf16[64,2048]{1,0:T(8,128)(2,1)}, u32[]{:S(2)}) copy-start(bf16[64,2048]{1,0:T(8,128)(2,1)} %param.15) | copy-start | bytes 786436
  136.6 34.7 %copy-start.3 = (f32[2048]{0:T(1024)S(1)}, f32[2048]{0:T(1024)}, u32[]{:S(2)}) copy-start(f32[2048]{0:T(1024)} %param.17) | copy-start | bytes 24580
  136.6 36.0 %copy-start.4 = (s32[64,8]{0,1:T(8,128)S(1)}, s32[64,8]{0,1:T(8,128)}, u32[]{:S(2)}) copy-start(s32[64,8]{0,1:T(8,128)} %param.27) | copy-start | bytes 6148
  170.6 0.7 copy-start.2

commit v7 on v5

--- a/solution.py
+++ b/solution.py
@@ -30,7 +30,7 @@
     return lax.ppermute(block, axis, route)
 
 
-def gather_kernel(n_group, n_expert, wq, wk, wv, wo, xn, oq, ok, ov, oo, oxn, send, recv, xsend, xrecv, local):
+def gather_kernel(n_group, n_expert, wqkv, wo, xn, oqkv, oo, oxn, send, recv, xsend, xrecv, local):
     g = lax.axis_index("group")
     e = lax.axis_index("expert")
     columns = n_group // 2
@@ -52,12 +52,8 @@
         pl.semaphore_signal(barrier, 1, device_id=dev, device_id_type=MESH)
     pl.semaphore_wait(barrier, len(peers))
 
-    width = wo.shape[1]
-
     def slot(k, origin):
-        if k == 3:
-            return oo.at[:, pl.ds(pl.multiple_of(origin * width, width), width)]
-        return (oq, ok, ov)[k].at[origin]
+        return (oqkv, oo)[k].at[origin]
 
     sends = []
 
@@ -74,11 +70,11 @@
         sends.append(copy)
 
     def forward(origin, dev):
-        for k in range(4):
+        for k in range(2):
             push(k, origin, slot(k, origin), dev)
 
     def arrive(origin):
-        for k in range(4):
+        for k in range(2):
             pltpu.make_async_remote_copy(
                 src_ref=slot(k, origin),
                 dst_ref=slot(k, origin),
@@ -112,16 +108,16 @@
             device_id_type=MESH,
         ).wait_recv()
 
-    inputs = (wq, wk, wv, wo)
-    own = [pltpu.make_async_copy(xn, oxn.at[e], local.at[4])]
-    own += [pltpu.make_async_copy(inputs[k], slot(k, g), local.at[k]) for k in range(4)]
+    inputs = (wqkv, wo)
+    own = [pltpu.make_async_copy(xn, oxn.at[e], local.at[2])]
+    own += [pltpu.make_async_copy(inputs[k], slot(k, g), local.at[k]) for k in range(2)]
     for copy in own:
         copy.start()
     xpush(xn, e, mate_dev)
     for dev in chip_devs:
         xpush(xn, e, dev)
     for dev in (pair_dev, plus_dev, minus_dev):
-        for k in range(4):
+        for k in range(2):
             push(k, g, inputs[k], dev)
     partner = g + 1 - 2 * xh
     arrive(partner)
@@ -156,25 +152,24 @@
         copy.wait()
 
 
-def gather_all(wq, wk, wv, wo, xn, n_group, n_expert):
+def gather_all(wqkv, wo, xn, n_group, n_expert):
     any_spec = pl.BlockSpec(memory_space=pl.ANY)
-    shapes = [jax.ShapeDtypeStruct((n_group,) + a.shape, a.dtype) for a in (wq, wk, wv)]
-    shapes += [jax.ShapeDtypeStruct((wo.shape[0], n_group * wo.shape[1]), wo.dtype)]
+    shapes = [jax.ShapeDtypeStruct((n_group,) + a.shape, a.dtype) for a in (wqkv, wo)]
     shapes += [jax.ShapeDtypeStruct((n_expert,) + xn.shape, xn.dtype)]
     return pl.pallas_call(
         functools.partial(gather_kernel, n_group, n_expert),
         out_shape=tuple(shapes),
-        in_specs=[any_spec] * 5,
-        out_specs=tuple([any_spec] * 5),
+        in_specs=[any_spec] * 3,
+        out_specs=tuple([any_spec] * 3),
         scratch_shapes=[
-            pltpu.SemaphoreType.DMA((64,)),
-            pltpu.SemaphoreType.DMA((4, n_group)),
+            pltpu.SemaphoreType.DMA((32,)),
+            pltpu.SemaphoreType.DMA((2, n_group)),
             pltpu.SemaphoreType.DMA((n_expert,)),
             pltpu.SemaphoreType.DMA((n_expert,)),
-            pltpu.SemaphoreType.DMA((5,)),
+            pltpu.SemaphoreType.DMA((3,)),
         ],
         compiler_params=pltpu.CompilerParams(collective_id=0, has_side_effects=True),
-    )(wq, wk, wv, wo, xn)
+    )(wqkv, wo, xn)
 
 
 def mate_kernel(part, out, send, recv):
@@ -375,14 +370,14 @@
     return indices + offset
 
 
-def prep_kernel(x_ref, wq_ref, wk_ref, wv_ref, cos_ref, sin_ref, qg_ref, kg_ref, q_out, k_out, v_out):
+def prep_kernel(query_width, x_ref, w_ref, cos_ref, sin_ref, qg_ref, kg_ref, q_out, k_out, v_out):
     x = x_ref[...]
     cosines = cos_ref[...]
     sines = sin_ref[...]
     depth = cosines.shape[1]
 
-    def project(w_ref):
-        return jnp.dot(x, w_ref[...], preferred_element_type=jnp.float32).astype(jnp.bfloat16)
+    def project(start, stop):
+        return jnp.dot(x, w_ref[:, start:stop], preferred_element_type=jnp.float32).astype(jnp.bfloat16)
 
     def norm_rope(values, gain):
         values = values.astype(jnp.float32)
@@ -390,46 +385,45 @@
         normed = values * inverse_rms * gain
         return (normed * cosines + pltpu.roll(normed, depth // 2, 1) * sines).astype(jnp.bfloat16)
 
-    queries = project(wq_ref)
+    queries = project(0, query_width)
     for h in range(queries.shape[1] // depth):
         q_out[:, h * depth : (h + 1) * depth] = norm_rope(
             queries[:, h * depth : (h + 1) * depth], qg_ref[...]
         )
-    k_out[...] = norm_rope(project(wk_ref), kg_ref[...])
-    v_out[...] = project(wv_ref)
-
-
-def prep(normed_rows, wq, wk, wv, cosines, sines, query_gain, key_gain):
+    k_out[...] = norm_rope(project(query_width, query_width + depth), kg_ref[...])
+    v_out[...] = project(query_width + depth, query_width + 2 * depth)
+
+
+def prep(normed_rows, joined, cosines, sines, query_gain, key_gain):
     rows, width = normed_rows.shape
-    depth = wk.shape[1]
+    depth = cosines.shape[1]
+    query_width = joined.shape[1] - 2 * depth
     block = min(256, rows)
     whole = lambda shape: pl.BlockSpec(shape, lambda i: (0, 0))
     per_row = lambda cols: pl.BlockSpec((block, cols), lambda i: (i, 0))
     return pl.pallas_call(
-        prep_kernel,
+        functools.partial(prep_kernel, query_width),
         out_shape=(
-            jax.ShapeDtypeStruct((rows, wq.shape[1]), jnp.bfloat16),
+            jax.ShapeDtypeStruct((rows, query_width), jnp.bfloat16),
             jax.ShapeDtypeStruct((rows, depth), jnp.bfloat16),
             jax.ShapeDtypeStruct((rows, depth), jnp.bfloat16),
         ),
         grid=(rows // block,),
         in_specs=[
             per_row(width),
-            whole(wq.shape),
-            whole(wk.shape),
-            whole(wv.shape),
+            whole(joined.shape),
             per_row(depth),
             per_row(depth),
             whole((1, depth)),
             whole((1, depth)),
         ],
-        out_specs=(per_row(wq.shape[1]), per_row(depth), per_row(depth)),
+        out_specs=(per_row(query_width), per_row(depth), per_row(depth)),
         cost_estimate=pl.CostEstimate(
-            flops=2 * rows * width * (wq.shape[1] + 2 * depth),
-            transcendentals=rows * (wq.shape[1] // depth + 1),
-            bytes_accessed=2 * (rows * width + width * (wq.shape[1] + 2 * depth) + rows * (wq.shape[1] + 2 * depth)),
+            flops=2 * rows * width * joined.shape[1],
+            transcendentals=rows * (query_width // depth + 1),
+            bytes_accessed=2 * (rows * width + width * joined.shape[1] + rows * joined.shape[1]),
         ),
-    )(normed_rows, wq, wk, wv, cosines, sines, query_gain.reshape(1, depth), key_gain.reshape(1, depth))
+    )(normed_rows, joined, cosines, sines, query_gain.reshape(1, depth), key_gain.reshape(1, depth))
 
 
 def rope_tables(parity, row_count, depth):
@@ -475,10 +469,10 @@
         trainer_key_value_weight, common_head * HEAD_DIMENSION, HEAD_DIMENSION, 2
     ).astype(jnp.bfloat16)
     normed = norm_rows(hidden_in, norm_attention).astype(jnp.bfloat16)
-    query_parts, key_parts, value_parts, output_parts, normed_parts = gather_all(
-        query_master.astype(jnp.bfloat16),
-        keyvalue_slice[0],
-        keyvalue_slice[1],
+    joined_parts, output_parts, normed_parts = gather_all(
+        jnp.concatenate(
+            [query_master.astype(jnp.bfloat16), keyvalue_slice[0], keyvalue_slice[1]], axis=1
+        ),
         output_master.astype(jnp.bfloat16),
         normed,
         groups_axis,
@@ -492,9 +486,7 @@
     cosines, sines = rope_tables(parity, local_rows, HEAD_DIMENSION)
     query_rows_list, key_rows, value_rows = prep(
         normed_parts.reshape(local_rows, model_width),
-        query_parts.reshape(model_width, -1),
-        key_parts.reshape(model_width, -1),
-        value_parts.reshape(model_width, -1),
+        joined_parts.reshape(model_width, -1),
         cosines,
         sines,
         query_gain,
@@ -515,8 +507,9 @@
         key_limits,
         HEAD_DIMENSION ** (-0.5),
     )
+    output_weight = jnp.transpose(output_parts, (1, 0, 2)).reshape(output_parts.shape[1], -1)
     head_partials = jnp.dot(
-        attended, output_parts, preferred_element_type=jnp.float32
+        attended, output_weight, preferred_element_type=jnp.float32
     ).astype(jnp.bfloat16)
     paired = head_partials.reshape(experts_axis // 2, 2, -1, model_width)
     from_mate = exchange_with_mate(paired)

time: 203 us -> 201 us (level)
  waiting for transfers between devices: 7.15 us -> 5.01 us
    transpose x0 -> x1, local copies, waits for them, and re-layouts: none -> 2.29 us  [per_device(): jnp.transpose(output_parts, (1, 0, 2)).reshape(output_parts.shape[1], -1)]
    ppermute x1, waiting for transfers between devices: 7.15 us -> 5.01 us  [from_partner(): return lax.ppermute(block, axis, route)]
  transfers between devices with their start and end apart: 1 -> 1, of which waited for: 1 -> 1; matrix products, arithmetic and copies ran while one was open for 2% -> 3% of each run, Pallas kernels for 0% -> 0%
where the time goes in v7:
time: 201 us
  Pallas kernels  150 us (75%)
  other arithmetic  24.4 us (12%)
  matrix products  11.9 us (6%)
  local copies, waits for them, and re-layouts  8.21 us (4%)
  waiting for transfers between devices  5.01 us (2%)
    pallas_call x1, Pallas kernels, gather_all(): pl.pallas_call(functools.partial(gather_kernel, n_group, n_expert), out_s...  70.8 us
    pallas_call x1, Pallas kernels, scatter_to_chips(): pl.pallas_call(functools.partial(chip_scatter_kernel, chips), out_shape=j...  31.8 us
    pallas_call x2, Pallas kernels, scatter_blocks(): pl.pallas_call(functools.partial(scatter_kernel, n_expert), out_shape=jax...  22.1 us
    pallas_call x1, Pallas kernels, attention(): pl.pallas_call(functools.partial(attention_kernel, scale, width // depth)...  9 us
    pallas_call x1, Pallas kernels, exchange_with_mate(): pl.pallas_call(mate_kernel, out_shape=jax.ShapeDtypeStruct(shape, part.dt...  8.8 us
    pallas_call x1, Pallas kernels, prep(): pl.pallas_call(functools.partial(prep_kernel, query_width), out_shape=(ja...  7.11 us
    ppermute x1, waiting for transfers between devices, from_partner(): return lax.ppermute(block, axis, route)  5.01 us
    dot_general x1, matrix products, per_device(): jnp.dot(attended, output_weight, preferred_element_type=jnp.float32)  4.6 us
  transfers between devices with their start and end apart: 1, of which 1 were waited for; matrix products, arithmetic and copies ran while one was open for 3% of the time, Pallas kernels for 0%

profile of v7, /device:TPU:1, one launch (start us, length us, event | category | flops | bytes accessed | tf_op | source)
XLA Modules:
  0.0 200.9 jit_solution(2099362404689646778)
XLA Ops:
  0.6 0.0 copy-start
  0.6 0.0 copy-start.1
  0.7 0.0 copy-start.4
  0.7 1.1 dynamic-slice_convert_fusion
  1.8 0.9 convert_element_type.60
  2.7 1.1 fusion.12
  3.8 1.5 convert_element_type.62.wo
  5.4 1.3 dynamic-slice_negate_fusion
  6.7 1.0 pad_maximum_fusion.cos_ref
  7.7 0.0 copy-done.1
  7.7 0.0 copy-done.4
  7.7 0.8 fusion.14.xn
  8.5 1.1 pad_maximum_fusion.1.sin_ref
  9.6 0.7 pad_maximum_fusion.5.wqkv
  10.2 70.8 %shard_map.158 = (bf16[16,128,512]{2,1,0:T(8,128)(2,1)}, bf16[16,256,128]{2,1,0:T(8,128)(2,1)}, bf16[16,64,2048]{2,1,0:T(8,128)(2,1)}) custom-call(bf16[128,512]{1,0:T(8,128)(2,1)} %pad_maximum_fusion.5.wqkv, bf16[256,128]{1,0:T(8,128)(2,1)} %convert_element_type.62.wo, bf16[64,2048]{1,0:T(8,128)(2,1)} %fusion.14.xn), custom_call_target="tpu_custom_call" | custom-call | tf_op jit(solution)/shard_map/pallas_call | solution.py:159
  81.1 0.0 copy-start.5
  81.1 0.0 copy-start.6
  81.1 7.1 %shard_map.159 = (bf16[1024,256]{1,0:T(8,128)(2,1)}, bf16[1024,128]{1,0:T(8,128)(2,1)}, bf16[1024,128]{1,0:T(8,128)(2,1)}) custom-call(bf16[1024,2048]{1,0:T(8,128)(2,1)} %bitcast.45, bf16[2048,512]{1,0:T(8,128)(2,1)} %bitcast.46, f32[1024,128]{1,0:T(8,128)} %pad_maximum_fusion.cos_ref, f32[1024,128]{1,0:T(8,128)} %pad_maximum_fusion.1.sin_ref, ...), custom_call_target="tpu_custom_call" | custom-call | flops 2147483648 | bytes 7340032 | tf_op jit(solution)/shard_map/pallas_call | solution.py:404
  88.2 1.9 pad_maximum_fusion.2
  90.1 0.8 collective-permute-start
  90.9 0.8 select_add_fusion.qpos_ref
  91.8 0.0 copy-done.5
  91.8 0.1 copy.24
  91.9 0.1 fusion.35
  92.0 0.1 select_reduce_fusion.2
  92.1 2.3 %copy.22 = bf16[256,16,128]{0,2,1:T(8,128)(2,1)} copy(bf16[256,16,128]{2,0,1:T(8,128)(2,1)} %bitcast.40) | data formatting | bytes 2097152 | tf_op jit(solution)/shard_map/transpose | solution.py:510
  94.4 0.1 fusion.26
  94.5 0.1 reduce_window_sum.11
  94.6 0.2 select_reduce_fusion.1
  94.8 0.0 copy-done.6
  94.8 0.6 fusion.33
  95.4 1.2 compare_select_fusion.kpos_ref
  96.6 5.0 %collective-permute-done = bf16[2,1024,128]{2,1,0:T(8,128)(2,1)} collective-permute-done((bf16[2,1024,128]{2,1,0:T(8,128)(2,1)}, bf16[2,1024,128]{2,1,0:T(8,128)(2,1)}, u32[]{:S(2)}, u32[]{:S(2)}) %collective-permute-start) | collective-permute-done | bytes 524320 | tf_op jit(solution)/shard_map/ppermute | solution.py:30
  101.6 1.1 slice_bitcast_fusion
  102.7 1.8 pad_maximum_fusion.4.v_ref
  104.5 1.8 pad_maximum_fusion.3.k_ref
  106.3 9.0 %shard_map.160 = bf16[1024,256]{1,0:T(8,128)(2,1)} custom-call(bf16[1024,256]{1,0:T(8,128)(2,1)} %get-tuple-element.10.q_ref, bf16[2048,128]{1,0:T(8,128)(2,1)} %pad_maximum_fusion.3.k_ref, bf16[2048,128]{1,0:T(8,128)(2,1)} %pad_maximum_fusion.4.v_ref, s32[1024,1]{1,0:T(8,128)} %select_add_fusion.qpos_ref, s32[1,2048]{1,0:T(1,128)} %compare_select_fusion.kpos_ref), custom_call_target="tpu_custom_call" | custom-call | flops 2147483648 | bytes 2097152 | tf_op jit(solution)/shard_map/pallas_call | solution.py:322
  115.3 4.6 %convolution_convert_fusion = bf16[1024,2048]{1,0:T(8,128)(2,1)} fusion(bf16[1024,256]{1,0:T(8,128)(2,1)} %shard_map.160, bf16[256,2048]{0,1:T(8,128)(2,1)} %bitcast.39), kind=kOutput, calls=%fused_computation.5 | convolution fusion | flops 1075838976 | bytes 5767168 | tf_op jit(solution)/shard_map/dot_general | solution.py:511
  119.9 8.8 %shard_map.161 = bf16[8,64,2048]{2,1,0:T(8,128)(2,1)} custom-call(bf16[8,2,64,2048]{3,2,1,0:T(8,128)(2,1)} %bitcast.37), custom_call_target="tpu_custom_call" | custom-call | tf_op jit(solution)/shard_map/pallas_call | solution.py:198
  128.7 4.5 %fusion.2.part = bf16[8,64,2048]{2,1,0:T(8,128)(2,1)} fusion(bf16[8,64,2048]{2,1,0:T(8,128)(2,1)} %shard_map.161, bf16[8,2,64,2048]{3,2,1,0:T(8,128)(2,1)} %bitcast.38, s32[]{:T(128)S(6)} %select_n.149), kind=kLoop, calls=%fused_computation.3 | loop fusion | flops 4194304 | bytes 6291460 | tf_op jit(solution)/shard_map/convert_element_type | solution.py:517
  133.2 0.0 copy-start.3
  133.2 31.8 %shard_map.162 = bf16[8,64,2048]{2,1,0:T(8,128)(2,1)} custom-call(bf16[8,64,2048]{2,1,0:T(8,128)(2,1)} %fusion.2.part), custom_call_target="tpu_custom_call" | custom-call | tf_op jit(solution)/shard_map/pallas_call | solution.py:240
  165.0 2.0 %convert_reduce_fusion = f32[64,2048]{1,0:T(8,128)S(1)} fusion(bf16[8,64,2048]{2,1,0:T(8,128)(2,1)} %shard_map.162), kind=kLoop, calls=%fused_computation.4 | loop fusion | flops 1966080 | bytes 2621440 | tf_op jit(solution)/shard_map/reduce_sum | solution.py:519
  167.0 0.2 fusion.9
  167.2 0.0 copy-start.2
  167.2 0.0 copy-done.3
  167.2 1.4 fusion.20
  168.6 0.2 select_reduce_fusion
  168.9 0.1 exponential_reduce_fusion
  169.0 0.2 select_reduce_fusion.3
  169.2 0.0 copy-done.2
  169.2 0.3 convolution_convert_fusion.1
  169.5 0.8 reshape.136.part
  170.3 13.3 %shard_map.163 = bf16[16,4,2048]{2,1,0:T(4,128)(2,1)} custom-call(bf16[16,4,2048]{2,1,0:T(4,128)(2,1)} %reshape.136.part), custom_call_target="tpu_custom_call" | custom-call | tf_op jit(solution)/shard_map/pallas_call | solution.py:283
  183.6 1.0 reshape.137
  184.6 4.0 %fusion = f32[64,1536]{1,0:T(8,128)S(1)} fusion(bf16[64,2048]{1,0:T(8,128)(2,1)S(1)} %reshape.137, bf16[1,2048,1536]{2,1,0:T(8,128)(2,1)} %param.25), kind=kOutput, calls=%fused_computation | convolution fusion | flops 402653184 | bytes 6946816 | tf_op jit(solution)/shard_map/dot_general | solution.py:550
  188.5 0.0 copy-done
  188.5 0.7 fusion.6
  189.2 0.8 reshape.138.part
  190.0 8.8 %shard_map.164 = bf16[16,4,2048]{2,1,0:T(4,128)(2,1)} custom-call(bf16[16,4,2048]{2,1,0:T(4,128)(2,1)} %reshape.138.part), custom_call_target="tpu_custom_call" | custom-call | tf_op jit(solution)/shard_map/pallas_call | solution.py:283
  198.9 1.0 reshape.139
  199.9 1.0 fusion.5
  (6 shorter events, 0.0 us)
Async XLA Ops:
  0.6 187.9 %copy-start = (bf16[1,768,2048]{2,1,0:T(8,128)(2,1)S(1)}, bf16[1,768,2048]{2,1,0:T(8,128)(2,1)}, u32[]{:S(2)}) copy-start(bf16[1,768,2048]{2,1,0:T(8,128)(2,1)} %param.26) | copy-start | bytes 9437188
  0.6 7.0 %copy-start.1 = (bf16[64,2048]{1,0:T(8,128)(2,1)S(1)}, bf16[64,2048]{1,0:T(8,128)(2,1)}, u32[]{:S(2)}) copy-start(bf16[64,2048]{1,0:T(8,128)(2,1)} %param.15) | copy-start | bytes 786436
  0.7 7.0 %copy-start.4 = (f32[2048]{0:T(1024)S(1)}, f32[2048]{0:T(1024)}, u32[]{:S(2)}) copy-start(f32[2048]{0:T(1024)} %param.16) | copy-start | bytes 24580
  81.1 10.7 %copy-start.5 = (s32[64,8]{0,1:T(8,128)S(1)}, s32[64,8]{0,1:T(8,128)}, u32[]{:S(2)}) copy-start(s32[64,8]{0,1:T(8,128)} %param.27) | copy-start | bytes 6148
  81.1 13.7 %copy-start.6 = (s32[8]{0:T(128)S(1)}, s32[8]{0:T(128)}, u32[]{:S(2)}) copy-start(s32[8]{0:T(128)} %param.23) | copy-start | bytes 100
  90.1 11.5 %collective-permute-start = (bf16[2,1024,128]{2,1,0:T(8,128)(2,1)}, bf16[2,1024,128]{2,1,0:T(8,128)(2,1)}, u32[]{:S(2)}, u32[]{:S(2)}) collective-permute-start(bf16[2,1024,128]{2,1,0:T(8,128)(2,1)} %pad_maximum_fusion.2), channel_id=1, source_target_pairs={{0,16},{16,0},{32,48},{48,32},{64,80},{80,64},{96,112},{112,96},{1... | collective-permute-start | bytes 1572872 | tf_op jit(solution)/shard_map/ppermute | solution.py:30
  133.2 34.1 %copy-start.3 = (f32[2048]{0:T(1024)S(1)}, f32[2048]{0:T(1024)}, u32[]{:S(2)}) copy-start(f32[2048]{0:T(1024)} %param.17) | copy-start | bytes 24580
  167.2 2.0 copy-start.2

commit v8 on v7

--- a/solution.py
+++ b/solution.py
@@ -172,6 +172,62 @@
     )(wqkv, wo, xn)
 
 
+def combine_kernel(blocks, attended_ref, weight_ref, out_ref, outgoing, incoming, send, recv):
+    g = lax.axis_index("group")
+    e = lax.axis_index("expert")
+    core = lax.rem(e, 2)
+    mate_dev = (g, e + 1 - 2 * core)
+    rows = out_ref.shape[1]
+    barrier = pltpu.get_barrier_semaphore()
+    pl.semaphore_signal(barrier, 1, device_id=mate_dev, device_id_type=MESH)
+    pl.semaphore_wait(barrier, 1)
+
+    def partial(block):
+        start = pl.multiple_of(block * rows, rows)
+        return jnp.dot(
+            attended_ref[pl.ds(start, rows), :], weight_ref[...], preferred_element_type=jnp.float32
+        ).astype(jnp.bfloat16)
+
+    for i in range(blocks):
+        outgoing[i] = partial(2 * i + 1 - core)
+    copy = pltpu.make_async_remote_copy(
+        src_ref=outgoing,
+        dst_ref=incoming,
+        send_sem=send.at[0],
+        recv_sem=recv.at[0],
+        device_id=mate_dev,
+        device_id_type=MESH,
+    )
+    copy.start()
+    for i in range(blocks):
+        out_ref[i] = partial(2 * i + core)
+    copy.wait()
+    for i in range(blocks):
+        out_ref[i] = (out_ref[i].astype(jnp.float32) + incoming[i].astype(jnp.float32)).astype(
+            jnp.bfloat16
+        )
+
+
+def project_and_combine(attended, weight, experts_axis):
+    rows = attended.shape[0] // experts_axis
+    blocks = experts_axis // 2
+    shape = (blocks, rows, weight.shape[1])
+    vmem = pl.BlockSpec(memory_space=pltpu.VMEM)
+    return pl.pallas_call(
+        functools.partial(combine_kernel, blocks),
+        out_shape=jax.ShapeDtypeStruct(shape, jnp.bfloat16),
+        in_specs=[vmem, vmem],
+        out_specs=vmem,
+        scratch_shapes=[
+            pltpu.VMEM(shape, jnp.bfloat16),
+            pltpu.VMEM(shape, jnp.bfloat16),
+            pltpu.SemaphoreType.DMA((1,)),
+            pltpu.SemaphoreType.DMA((1,)),
+        ],
+        compiler_params=pltpu.CompilerParams(collective_id=4, has_side_effects=True),
+    )(attended, weight)
+
+
 def mate_kernel(part, out, send, recv):
     g = lax.axis_index("group")
     e = lax.axis_index("expert")
@@ -508,13 +564,7 @@
         HEAD_DIMENSION ** (-0.5),
     )
     output_weight = jnp.transpose(output_parts, (1, 0, 2)).reshape(output_parts.shape[1], -1)
-    head_partials = jnp.dot(
-        attended, output_weight, preferred_element_type=jnp.float32
-    ).astype(jnp.bfloat16)
-    paired = head_partials.reshape(experts_axis // 2, 2, -1, model_width)
-    from_mate = exchange_with_mate(paired)
-    own_parity = lax.dynamic_index_in_dim(paired, group_member % 2, 1, keepdims=False)
-    chip_sums = (own_parity.astype(jnp.float32) + from_mate.astype(jnp.float32)).astype(jnp.bfloat16)
+    chip_sums = project_and_combine(attended, output_weight, experts_axis)
     owned = scatter_to_chips(chip_sums)
     summed = jnp.sum(owned.astype(jnp.float32), axis=0)
     hidden = (hidden_in.astype(jnp.float32) + summed).astype(jnp.bfloat16)

time: 201 us -> 194 us (0.965)
  other arithmetic: 24.4 us -> 18.2 us
  matrix products: 11.9 us -> 6.2 us
  Pallas kernels: 150 us -> 154 us
    dot_general x1 -> x0, matrix products: 4.6 us -> none  [per_device(): jnp.dot(attended, output_weight, preferred_element_type=jnp.float32)]
    convert_element_type x1 -> x0, other arithmetic: 4.46 us -> none  [per_device(): (own_parity.astype(jnp.float32) + from_mate.astype(jnp.float32)).astype(j...]
    pallas_call x1, Pallas kernels: 8.8 us -> 13.2 us  [project_and_combine(): pl.pallas_call(functools.partial(combine_kernel, blocks), out_shape=jax.S...]
    reshape x0 -> x1, local copies, waits for them, and re-layouts: none -> 2.37 us  [per_device(): jnp.transpose(output_parts, (1, 0, 2)).reshape(output_parts.shape[1], -1)]
    transpose x1 -> x0, local copies, waits for them, and re-layouts: 2.29 us -> none  [per_device(): jnp.transpose(output_parts, (1, 0, 2)).reshape(output_parts.shape[1], -1)]
where the time goes in v8:
time: 194 us; the launch traced here: 193 us
  Pallas kernels  154 us (79%)
  other arithmetic  18.2 us (9%)
  local copies, waits for them, and re-layouts  8.3 us (4%)
  matrix products  6.2 us (3%)
  waiting for transfers between devices  4.72 us (2%)
    pallas_call x1, Pallas kernels, gather_all(): pl.pallas_call(functools.partial(gather_kernel, n_group, n_expert), out_s...  70.8 us
    pallas_call x1, Pallas kernels, scatter_to_chips(): pl.pallas_call(functools.partial(chip_scatter_kernel, chips), out_shape=j...  32 us
    pallas_call x2, Pallas kernels, scatter_blocks(): pl.pallas_call(functools.partial(scatter_kernel, n_expert), out_shape=jax...  22.1 us
    pallas_call x1, Pallas kernels, project_and_combine(): pl.pallas_call(functools.partial(combine_kernel, blocks), out_shape=jax.S...  13.2 us
    pallas_call x1, Pallas kernels, attention(): pl.pallas_call(functools.partial(attention_kernel, scale, width // depth)...  9 us
    pallas_call x1, Pallas kernels, prep(): pl.pallas_call(functools.partial(prep_kernel, query_width), out_shape=(ja...  7.11 us
    ppermute x1, waiting for transfers between devices, from_partner(): return lax.ppermute(block, axis, route)  4.72 us
    dot_general x1, matrix products, per_device(): jnp.dot(flattened, gateup_here, preferred_element_type=jnp.float32)  3.97 us
  transfers between devices with their start and end apart: 1, of which 1 were waited for; matrix products, arithmetic and copies ran while one was open for 3% of the time, Pallas kernels for 0%

profile of v8, /device:TPU:1, one launch (start us, length us, event | category | flops | bytes accessed | tf_op | source)
XLA Modules:
  0.0 193.5 jit_solution(17935708977340181626)
XLA Ops:
  0.6 0.0 copy-start
  0.6 0.0 copy-start.1
  0.7 0.0 copy-start.7
  0.7 1.1 dynamic-slice_convert_fusion
  1.8 0.9 convert_element_type.45
  2.7 1.1 fusion.11
  3.8 1.5 convert_element_type.47.wo
  5.4 1.3 dynamic-slice_negate_fusion
  6.7 1.0 pad_maximum_fusion.cos_ref
  7.7 0.0 copy-done.1
  7.7 0.0 copy-done.7
  7.7 0.8 fusion.13.xn
  8.5 1.1 pad_maximum_fusion.1.sin_ref
  9.6 0.7 pad_maximum_fusion.5.wqkv
  10.2 70.8 %shard_map.158 = (bf16[16,128,512]{2,1,0:T(8,128)(2,1)}, bf16[16,256,128]{2,1,0:T(8,128)(2,1)}, bf16[16,64,2048]{2,1,0:T(8,128)(2,1)}) custom-call(bf16[128,512]{1,0:T(8,128)(2,1)} %pad_maximum_fusion.5.wqkv, bf16[256,128]{1,0:T(8,128)(2,1)} %convert_element_type.47.wo, bf16[64,2048]{1,0:T(8,128)(2,1)} %fusion.13.xn), custom_call_target="tpu_custom_call" | custom-call | tf_op jit(solution)/shard_map/pallas_call | solution.py:159
  81.1 0.0 copy-start.8
  81.1 0.0 copy-start.9
  81.1 7.1 %shard_map.159 = (bf16[1024,256]{1,0:T(8,128)(2,1)}, bf16[1024,128]{1,0:T(8,128)(2,1)}, bf16[1024,128]{1,0:T(8,128)(2,1)}) custom-call(bf16[1024,2048]{1,0:T(8,128)(2,1)} %bitcast.37, bf16[2048,512]{1,0:T(8,128)(2,1)} %bitcast.38, f32[1024,128]{1,0:T(8,128)} %pad_maximum_fusion.cos_ref, f32[1024,128]{1,0:T(8,128)} %pad_maximum_fusion.1.sin_ref, ...), custom_call_target="tpu_custom_call" | custom-call | flops 2147483648 | bytes 7340032 | tf_op jit(solution)/shard_map/pallas_call | solution.py:460
  88.2 1.9 pad_maximum_fusion.2
  90.1 0.8 collective-permute-start
  90.9 0.0 copy-done.8
  90.9 0.1 copy.20
  91.0 0.1 fusion.34
  91.1 0.1 select_reduce_fusion.2
  91.3 0.1 fusion.25
  91.4 0.1 reduce_window_sum.11
  91.5 0.2 select_reduce_fusion.1
  91.7 0.0 copy-done.9
  91.7 0.0 copy-start.4
  91.7 0.0 copy-start.3
  91.7 0.7 fusion.32
  92.4 1.3 compare_select_fusion.kpos_ref
  93.7 0.8 select_add_fusion.qpos_ref
  94.5 2.4 %copy_bitcast_fusion.weight_ref = bf16[256,2048]{1,0:T(8,128)(2,1)} fusion(bf16[16,256,128]{2,1,0:T(8,128)(2,1)} %get-tuple-element.13), kind=kLoop, calls=%fused_computation.9 | loop fusion | bytes 2097152 | tf_op jit(solution)/shard_map/reshape | solution.py:566
  96.9 4.7 %collective-permute-done = bf16[2,1024,128]{2,1,0:T(8,128)(2,1)} collective-permute-done((bf16[2,1024,128]{2,1,0:T(8,128)(2,1)}, bf16[2,1024,128]{2,1,0:T(8,128)(2,1)}, u32[]{:S(2)}, u32[]{:S(2)}) %collective-permute-start) | collective-permute-done | bytes 524320 | tf_op jit(solution)/shard_map/ppermute | solution.py:30
  101.6 1.1 slice_bitcast_fusion
  102.7 0.0 copy-done.4
  102.7 0.9 pad_maximum_fusion.4.v_ref
  103.5 0.8 pad_maximum_fusion.3.k_ref
  104.4 9.0 %shard_map.160.attended_ref = bf16[1024,256]{1,0:T(8,128)(2,1)} custom-call(bf16[1024,256]{1,0:T(8,128)(2,1)} %get-tuple-element.10.q_ref, bf16[2048,128]{1,0:T(8,128)(2,1)} %pad_maximum_fusion.3.k_ref, bf16[2048,128]{1,0:T(8,128)(2,1)} %pad_maximum_fusion.4.v_ref, s32[1024,1]{1,0:T(8,128)} %select_add_fusion.qpos_ref, s32[1,2048]{1,0:T(1,128)} %compare_select_fusion.kpos_ref), custom_call_target="tpu_custom_call" | custom-call | flops 2147483648 | bytes 2097152 | tf_op jit(solution)/shard_map/pallas_call | solution.py:378
  113.4 13.2 %shard_map.161.part = bf16[8,64,2048]{2,1,0:T(8,128)(2,1)} custom-call(bf16[1024,256]{1,0:T(8,128)(2,1)} %shard_map.160.attended_ref, bf16[256,2048]{1,0:T(8,128)(2,1)} %copy_bitcast_fusion.weight_ref), custom_call_target="tpu_custom_call" | custom-call | tf_op jit(solution)/shard_map/pallas_call | solution.py:216
  126.6 0.0 copy-start.6
  126.7 32.0 %shard_map.162 = bf16[8,64,2048]{2,1,0:T(8,128)(2,1)} custom-call(bf16[8,64,2048]{2,1,0:T(8,128)(2,1)} %shard_map.161.part), custom_call_target="tpu_custom_call" | custom-call | tf_op jit(solution)/shard_map/pallas_call | solution.py:296
  158.7 0.0 copy-start.5
  158.7 2.1 %convert_reduce_fusion = f32[64,2048]{1,0:T(8,128)S(1)} fusion(bf16[8,64,2048]{2,1,0:T(8,128)(2,1)} %shard_map.162), kind=kLoop, calls=%fused_computation.2 | loop fusion | flops 1966080 | bytes 2621440 | tf_op jit(solution)/shard_map/reduce_sum | solution.py:569
  160.8 0.2 fusion.8
  161.0 0.0 copy-done.6
  161.0 0.0 copy-done.5
  161.0 0.3 fusion.19
  161.3 0.2 select_reduce_fusion
  161.5 0.1 exponential_reduce_fusion
  161.6 0.2 select_reduce_fusion.3
  161.8 0.0 copy-done.2
  161.8 0.3 convolution_convert_fusion
  162.1 0.8 reshape.130.part
  162.9 13.2 %shard_map.163 = bf16[16,4,2048]{2,1,0:T(4,128)(2,1)} custom-call(bf16[16,4,2048]{2,1,0:T(4,128)(2,1)} %reshape.130.part), custom_call_target="tpu_custom_call" | custom-call | tf_op jit(solution)/shard_map/pallas_call | solution.py:339
  176.2 1.0 reshape.131
  177.2 4.0 %fusion = f32[64,1536]{1,0:T(8,128)S(1)} fusion(bf16[64,2048]{1,0:T(8,128)(2,1)S(1)} %reshape.131, bf16[1,2048,1536]{2,1,0:T(8,128)(2,1)} %param.25), kind=kOutput, calls=%fused_computation | convolution fusion | flops 402653184 | bytes 6946816 | tf_op jit(solution)/shard_map/dot_general | solution.py:600
  181.1 0.0 copy-done
  181.2 0.7 fusion.5
  181.8 0.8 reshape.132.part
  182.7 8.8 %shard_map.164 = bf16[16,4,2048]{2,1,0:T(4,128)(2,1)} custom-call(bf16[16,4,2048]{2,1,0:T(4,128)(2,1)} %reshape.132.part), custom_call_target="tpu_custom_call" | custom-call | tf_op jit(solution)/shard_map/pallas_call | solution.py:339
  191.5 1.0 reshape.133
  192.5 1.0 fusion.4
  (8 shorter events, 0.0 us)
Async XLA Ops:
  0.6 180.5 %copy-start = (bf16[1,768,2048]{2,1,0:T(8,128)(2,1)S(1)}, bf16[1,768,2048]{2,1,0:T(8,128)(2,1)}, u32[]{:S(2)}) copy-start(bf16[1,768,2048]{2,1,0:T(8,128)(2,1)} %param.26) | copy-start | bytes 9437188
  0.6 7.0 %copy-start.1 = (bf16[64,2048]{1,0:T(8,128)(2,1)S(1)}, bf16[64,2048]{1,0:T(8,128)(2,1)}, u32[]{:S(2)}) copy-start(bf16[64,2048]{1,0:T(8,128)(2,1)} %param.15) | copy-start | bytes 786436
  0.7 7.0 %copy-start.7 = (f32[2048]{0:T(1024)S(1)}, f32[2048]{0:T(1024)}, u32[]{:S(2)}) copy-start(f32[2048]{0:T(1024)} %param.16) | copy-start | bytes 24580
  81.1 9.8 %copy-start.8 = (s32[64,8]{0,1:T(8,128)S(1)}, s32[64,8]{0,1:T(8,128)}, u32[]{:S(2)}) copy-start(s32[64,8]{0,1:T(8,128)} %param.27) | copy-start | bytes 6148
  81.1 10.6 %copy-start.9 = (s32[8]{0:T(128)S(1)}, s32[8]{0:T(128)}, u32[]{:S(2)}) copy-start(s32[8]{0:T(128)} %param.23) | copy-start | bytes 100
  90.1 11.5 %collective-permute-start = (bf16[2,1024,128]{2,1,0:T(8,128)(2,1)}, bf16[2,1024,128]{2,1,0:T(8,128)(2,1)}, u32[]{:S(2)}, u32[]{:S(2)}) collective-permute-start(bf16[2,1024,128]{2,1,0:T(8,128)(2,1)} %pad_maximum_fusion.2), channel_id=1, source_target_pairs={{0,16},{16,0},{32,48},{48,32},{64,80},{80,64},{96,112},{112,96},{1... | collective-permute-start | bytes 1572872 | tf_op jit(solution)/shard_map/ppermute | solution.py:30
  91.7 11.0 %copy-start.4 = (bf16[1024,128]{1,0:T(8,128)(2,1)S(1)}, bf16[1024,128]{1,0:T(8,128)(2,1)}, u32[]{:S(2)}) copy-start(bf16[1024,128]{1,0:T(8,128)(2,1)} %get-tuple-element.12) | copy-start | bytes 786436
  91.7 11.9 %copy-start.3 = (bf16[1024,128]{1,0:T(8,128)(2,1)S(1)}, bf16[1024,128]{1,0:T(8,128)(2,1)}, u32[]{:S(2)}) copy-start(bf16[1024,128]{1,0:T(8,128)(2,1)} %get-tuple-element.11) | copy-start | bytes 786436
  126.6 34.3 %copy-start.6 = (f32[2048]{0:T(1024)S(1)}, f32[2048]{0:T(1024)}, u32[]{:S(2)}) copy-start(f32[2048]{0:T(1024)} %param.17) | copy-start | bytes 24580
  158.7 2.3 %copy-start.5 = (bf16[2048,128]{1,0:T(8,128)(2,1)S(1)}, bf16[2048,128]{1,0:T(8,128)(2,1)}, u32[]{:S(2)}) copy-start(bf16[2048,128]{1,0:T(8,128)(2,1)} %param.24) | copy-start | bytes 1572868
  160.9 0.9 copy-start.2

commit v9 on v8

--- a/solution.py
+++ b/solution.py
@@ -228,6 +228,89 @@
     )(attended, weight)
 
 
+def combine_scatter_kernel(blocks, attended_ref, weight_ref, out_ref, outgoing, incoming, combined, send, recv, chip_send, chip_recv, local):
+    g = lax.axis_index("group")
+    e = lax.axis_index("expert")
+    core = lax.rem(e, 2)
+    chip = lax.div(e, 2)
+    mate_dev = (g, e + 1 - 2 * core)
+    chip_devs = [(g, 2 * lax.rem(chip + j, blocks) + core) for j in range(1, blocks)]
+    rows = out_ref.shape[1]
+    barrier = pltpu.get_barrier_semaphore()
+    for dev in [mate_dev] + chip_devs:
+        pl.semaphore_signal(barrier, 1, device_id=dev, device_id_type=MESH)
+    pl.semaphore_wait(barrier, blocks)
+
+    def partial(block):
+        start = pl.multiple_of(block * rows, rows)
+        return jnp.dot(
+            attended_ref[pl.ds(start, rows), :], weight_ref[...], preferred_element_type=jnp.float32
+        ).astype(jnp.bfloat16)
+
+    for i in range(blocks):
+        outgoing[i] = partial(2 * i + 1 - core)
+    copy = pltpu.make_async_remote_copy(
+        src_ref=outgoing,
+        dst_ref=incoming,
+        send_sem=send.at[0],
+        recv_sem=recv.at[0],
+        device_id=mate_dev,
+        device_id_type=MESH,
+    )
+    copy.start()
+    for i in range(blocks):
+        combined[i] = partial(2 * i + core)
+    copy.wait()
+    pushes = []
+    for j in range(1, blocks):
+        i = lax.rem(chip + j, blocks)
+        combined[i] = (combined[i].astype(jnp.float32) + incoming[i].astype(jnp.float32)).astype(
+            jnp.bfloat16
+        )
+        push = pltpu.make_async_remote_copy(
+            src_ref=combined.at[i],
+            dst_ref=out_ref.at[chip],
+            send_sem=chip_send.at[j],
+            recv_sem=chip_recv.at[j],
+            device_id=chip_devs[j - 1],
+            device_id_type=MESH,
+        )
+        push.start()
+        pushes.append(push)
+    combined[chip] = (combined[chip].astype(jnp.float32) + incoming[chip].astype(jnp.float32)).astype(
+        jnp.bfloat16
+    )
+    own = pltpu.make_async_copy(combined.at[chip], out_ref.at[chip], local.at[0])
+    own.start()
+    for push in pushes:
+        push.wait()
+    own.wait()
+
+
+def combine_and_scatter(attended, weight, experts_axis):
+    rows = attended.shape[0] // experts_axis
+    blocks = experts_axis // 2
+    shape = (blocks, rows, weight.shape[1])
+    vmem = pl.BlockSpec(memory_space=pltpu.VMEM)
+    return pl.pallas_call(
+        functools.partial(combine_scatter_kernel, blocks),
+        out_shape=jax.ShapeDtypeStruct(shape, jnp.bfloat16),
+        in_specs=[vmem, vmem],
+        out_specs=pl.BlockSpec(memory_space=pl.ANY),
+        scratch_shapes=[
+            pltpu.VMEM(shape, jnp.bfloat16),
+            pltpu.VMEM(shape, jnp.bfloat16),
+            pltpu.VMEM(shape, jnp.bfloat16),
+            pltpu.SemaphoreType.DMA((1,)),
+            pltpu.SemaphoreType.DMA((1,)),
+            pltpu.SemaphoreType.DMA((blocks,)),
+            pltpu.SemaphoreType.DMA((blocks,)),
+            pltpu.SemaphoreType.DMA((1,)),
+        ],
+        compiler_params=pltpu.CompilerParams(collective_id=7, has_side_effects=True),
+    )(attended, weight)
+
+
 def mate_kernel(part, out, send, recv):
     g = lax.axis_index("group")
     e = lax.axis_index("expert")
@@ -564,8 +647,7 @@
         HEAD_DIMENSION ** (-0.5),
     )
     output_weight = jnp.transpose(output_parts, (1, 0, 2)).reshape(output_parts.shape[1], -1)
-    chip_sums = project_and_combine(attended, output_weight, experts_axis)
-    owned = scatter_to_chips(chip_sums)
+    owned = combine_and_scatter(attended, output_weight, experts_axis)
     summed = jnp.sum(owned.astype(jnp.float32), axis=0)
     hidden = (hidden_in.astype(jnp.float32) + summed).astype(jnp.bfloat16)
     normed_second = norm_rows(hidden, norm_experts).astype(jnp.bfloat16)

time: 194 us -> 193 us (level)
    pallas_call x2 -> x1, Pallas kernels: 45.2 us -> 44.8 us  [combine_and_scatter(): pl.pallas_call(functools.partial(combine_scatter_kernel, blocks), out_sha...]
where the time goes in v9:
time: 193 us; the launch traced here: 192 us
  Pallas kernels  153 us (79%)
  other arithmetic  18.2 us (9%)
  local copies, waits for them, and re-layouts  8.3 us (4%)
  matrix products  6.2 us (3%)
  waiting for transfers between devices  4.72 us (2%)
    pallas_call x1, Pallas kernels, gather_all(): pl.pallas_call(functools.partial(gather_kernel, n_group, n_expert), out_s...  70.8 us
    pallas_call x1, Pallas kernels, combine_and_scatter(): pl.pallas_call(functools.partial(combine_scatter_kernel, blocks), out_sha...  44.8 us
    pallas_call x2, Pallas kernels, scatter_blocks(): pl.pallas_call(functools.partial(scatter_kernel, n_expert), out_shape=jax...  21.5 us
    pallas_call x1, Pallas kernels, attention(): pl.pallas_call(functools.partial(attention_kernel, scale, width // depth)...  9 us
    pallas_call x1, Pallas kernels, prep(): pl.pallas_call(functools.partial(prep_kernel, query_width), out_shape=(ja...  7.11 us
    ppermute x1, waiting for transfers between devices, from_partner(): return lax.ppermute(block, axis, route)  4.72 us
    dot_general x1, matrix products, per_device(): jnp.dot(flattened, gateup_here, preferred_element_type=jnp.float32)  3.97 us
  transfers between devices with their start and end apart: 1, of which 1 were waited for; matrix products, arithmetic and copies ran while one was open for 3% of the time, Pallas kernels for 0%

profile of v9, /device:TPU:1, one launch (start us, length us, event | category | flops | bytes accessed | tf_op | source)
XLA Modules:
  0.0 192.5 jit_solution(10487974660971329202)
XLA Ops:
  0.6 0.0 copy-start
  0.6 0.0 copy-start.1
  0.7 0.0 copy-start.7
  0.7 1.1 dynamic-slice_convert_fusion
  1.8 0.9 convert_element_type.45
  2.7 1.1 fusion.11
  3.8 1.5 convert_element_type.47.wo
  5.4 1.3 dynamic-slice_negate_fusion
  6.7 1.0 pad_maximum_fusion.cos_ref
  7.7 0.0 copy-done.1
  7.7 0.0 copy-done.7
  7.7 0.8 fusion.13.xn
  8.5 1.1 pad_maximum_fusion.1.sin_ref
  9.6 0.7 pad_maximum_fusion.5.wqkv
  10.2 70.8 %shard_map.158 = (bf16[16,128,512]{2,1,0:T(8,128)(2,1)}, bf16[16,256,128]{2,1,0:T(8,128)(2,1)}, bf16[16,64,2048]{2,1,0:T(8,128)(2,1)}) custom-call(bf16[128,512]{1,0:T(8,128)(2,1)} %pad_maximum_fusion.5.wqkv, bf16[256,128]{1,0:T(8,128)(2,1)} %convert_element_type.47.wo, bf16[64,2048]{1,0:T(8,128)(2,1)} %fusion.13.xn), custom_call_target="tpu_custom_call" | custom-call | tf_op jit(solution)/shard_map/pallas_call | solution.py:159
  81.1 0.0 copy-start.8
  81.1 0.0 copy-start.9
  81.1 7.1 %shard_map.159 = (bf16[1024,256]{1,0:T(8,128)(2,1)}, bf16[1024,128]{1,0:T(8,128)(2,1)}, bf16[1024,128]{1,0:T(8,128)(2,1)}) custom-call(bf16[1024,2048]{1,0:T(8,128)(2,1)} %bitcast.37, bf16[2048,512]{1,0:T(8,128)(2,1)} %bitcast.38, f32[1024,128]{1,0:T(8,128)} %pad_maximum_fusion.cos_ref, f32[1024,128]{1,0:T(8,128)} %pad_maximum_fusion.1.sin_ref, ...), custom_call_target="tpu_custom_call" | custom-call | flops 2147483648 | bytes 7340032 | tf_op jit(solution)/shard_map/pallas_call | solution.py:543
  88.2 1.9 pad_maximum_fusion.2
  90.1 0.8 collective-permute-start
  90.9 0.0 copy-done.8
  90.9 0.1 copy.20
  91.0 0.1 fusion.34
  91.1 0.1 select_reduce_fusion.2
  91.3 0.1 fusion.25
  91.4 0.1 reduce_window_sum.11
  91.5 0.2 select_reduce_fusion.1
  91.7 0.0 copy-done.9
  91.7 0.0 copy-start.4
  91.7 0.0 copy-start.3
  91.7 0.7 fusion.32
  92.4 1.3 compare_select_fusion.kpos_ref
  93.7 0.8 select_add_fusion.qpos_ref
  94.5 2.4 %copy_bitcast_fusion.weight_ref = bf16[256,2048]{1,0:T(8,128)(2,1)} fusion(bf16[16,256,128]{2,1,0:T(8,128)(2,1)} %get-tuple-element.13), kind=kLoop, calls=%fused_computation.9 | loop fusion | bytes 2097152 | tf_op jit(solution)/shard_map/reshape | solution.py:649
  96.9 4.7 %collective-permute-done = bf16[2,1024,128]{2,1,0:T(8,128)(2,1)} collective-permute-done((bf16[2,1024,128]{2,1,0:T(8,128)(2,1)}, bf16[2,1024,128]{2,1,0:T(8,128)(2,1)}, u32[]{:S(2)}, u32[]{:S(2)}) %collective-permute-start) | collective-permute-done | bytes 524320 | tf_op jit(solution)/shard_map/ppermute | solution.py:30
  101.6 1.1 slice_bitcast_fusion
  102.7 0.0 copy-done.4
  102.7 0.9 pad_maximum_fusion.4.v_ref
  103.5 0.0 copy-done.3
  103.5 0.8 pad_maximum_fusion.3.k_ref
  104.4 9.0 %shard_map.160.attended_ref = bf16[1024,256]{1,0:T(8,128)(2,1)} custom-call(bf16[1024,256]{1,0:T(8,128)(2,1)} %get-tuple-element.10.q_ref, bf16[2048,128]{1,0:T(8,128)(2,1)} %pad_maximum_fusion.3.k_ref, bf16[2048,128]{1,0:T(8,128)(2,1)} %pad_maximum_fusion.4.v_ref, s32[1024,1]{1,0:T(8,128)} %select_add_fusion.qpos_ref, s32[1,2048]{1,0:T(1,128)} %compare_select_fusion.kpos_ref), custom_call_target="tpu_custom_call" | custom-call | flops 2147483648 | bytes 2097152 | tf_op jit(solution)/shard_map/pallas_call | solution.py:461
  113.4 0.0 copy-start.6
  113.4 44.8 %shard_map.161 = bf16[8,64,2048]{2,1,0:T(8,128)(2,1)} custom-call(bf16[1024,256]{1,0:T(8,128)(2,1)} %shard_map.160.attended_ref, bf16[256,2048]{1,0:T(8,128)(2,1)} %copy_bitcast_fusion.weight_ref), custom_call_target="tpu_custom_call" | custom-call | tf_op jit(solution)/shard_map/pallas_call | solution.py:295
  158.2 0.0 copy-start.5
  158.2 2.1 %convert_reduce_fusion = f32[64,2048]{1,0:T(8,128)S(1)} fusion(bf16[8,64,2048]{2,1,0:T(8,128)(2,1)} %shard_map.161), kind=kLoop, calls=%fused_computation.2 | loop fusion | flops 1966080 | bytes 2621440 | tf_op jit(solution)/shard_map/reduce_sum | solution.py:651
  160.3 0.2 fusion.8
  160.5 0.0 copy-done.6
  160.5 0.0 copy-done.5
  160.5 0.3 fusion.19
  160.8 0.2 select_reduce_fusion
  161.0 0.1 exponential_reduce_fusion
  161.1 0.2 select_reduce_fusion.3
  161.3 0.0 copy-done.2
  161.4 0.3 convolution_convert_fusion
  161.6 0.8 reshape.130.part
  162.5 12.7 %shard_map.162 = bf16[16,4,2048]{2,1,0:T(4,128)(2,1)} custom-call(bf16[16,4,2048]{2,1,0:T(4,128)(2,1)} %reshape.130.part), custom_call_target="tpu_custom_call" | custom-call | tf_op jit(solution)/shard_map/pallas_call | solution.py:422
  175.1 1.0 reshape.131
  176.2 4.0 %fusion = f32[64,1536]{1,0:T(8,128)S(1)} fusion(bf16[64,2048]{1,0:T(8,128)(2,1)S(1)} %reshape.131, bf16[1,2048,1536]{2,1,0:T(8,128)(2,1)} %param.25), kind=kOutput, calls=%fused_computation | convolution fusion | flops 402653184 | bytes 6946816 | tf_op jit(solution)/shard_map/dot_general | solution.py:682
  180.1 0.0 copy-done
  180.1 0.7 fusion.5
  180.8 0.8 reshape.132.part
  181.6 8.8 %shard_map.163 = bf16[16,4,2048]{2,1,0:T(4,128)(2,1)} custom-call(bf16[16,4,2048]{2,1,0:T(4,128)(2,1)} %reshape.132.part), custom_call_target="tpu_custom_call" | custom-call | tf_op jit(solution)/shard_map/pallas_call | solution.py:422
  190.5 1.0 reshape.133
  191.5 1.0 fusion.4
  (7 shorter events, 0.0 us)
Async XLA Ops:
  0.6 179.5 %copy-start = (bf16[1,768,2048]{2,1,0:T(8,128)(2,1)S(1)}, bf16[1,768,2048]{2,1,0:T(8,128)(2,1)}, u32[]{:S(2)}) copy-start(bf16[1,768,2048]{2,1,0:T(8,128)(2,1)} %param.26) | copy-start | bytes 9437188
  0.6 7.0 %copy-start.1 = (bf16[64,2048]{1,0:T(8,128)(2,1)S(1)}, bf16[64,2048]{1,0:T(8,128)(2,1)}, u32[]{:S(2)}) copy-start(bf16[64,2048]{1,0:T(8,128)(2,1)} %param.15) | copy-start | bytes 786436
  0.7 7.0 %copy-start.7 = (f32[2048]{0:T(1024)S(1)}, f32[2048]{0:T(1024)}, u32[]{:S(2)}) copy-start(f32[2048]{0:T(1024)} %param.16) | copy-start | bytes 24580
  81.1 9.8 %copy-start.8 = (s32[64,8]{0,1:T(8,128)S(1)}, s32[64,8]{0,1:T(8,128)}, u32[]{:S(2)}) copy-start(s32[64,8]{0,1:T(8,128)} %param.27) | copy-start | bytes 6148
  81.1 10.6 %copy-start.9 = (s32[8]{0:T(128)S(1)}, s32[8]{0:T(128)}, u32[]{:S(2)}) copy-start(s32[8]{0:T(128)} %param.23) | copy-start | bytes 100
  90.1 11.5 %collective-permute-start = (bf16[2,1024,128]{2,1,0:T(8,128)(2,1)}, bf16[2,1024,128]{2,1,0:T(8,128)(2,1)}, u32[]{:S(2)}, u32[]{:S(2)}) collective-permute-start(bf16[2,1024,128]{2,1,0:T(8,128)(2,1)} %pad_maximum_fusion.2), channel_id=1, source_target_pairs={{0,16},{16,0},{32,48},{48,32},{64,80},{80,64},{96,112},{112,96},{1... | collective-permute-start | bytes 1572872 | tf_op jit(solution)/shard_map/ppermute | solution.py:30
  91.7 11.0 %copy-start.4 = (bf16[1024,128]{1,0:T(8,128)(2,1)S(1)}, bf16[1024,128]{1,0:T(8,128)(2,1)}, u32[]{:S(2)}) copy-start(bf16[1024,128]{1,0:T(8,128)(2,1)} %get-tuple-element.12) | copy-start | bytes 786436
  91.7 11.9 %copy-start.3 = (bf16[1024,128]{1,0:T(8,128)(2,1)S(1)}, bf16[1024,128]{1,0:T(8,128)(2,1)}, u32[]{:S(2)}) copy-start(bf16[1024,128]{1,0:T(8,128)(2,1)} %get-tuple-element.11) | copy-start | bytes 786436
  113.4 47.1 %copy-start.6 = (f32[2048]{0:T(1024)S(1)}, f32[2048]{0:T(1024)}, u32[]{:S(2)}) copy-start(f32[2048]{0:T(1024)} %param.17) | copy-start | bytes 24580
  158.2 2.3 %copy-start.5 = (bf16[2048,128]{1,0:T(8,128)(2,1)S(1)}, bf16[2048,128]{1,0:T(8,128)(2,1)}, u32[]{:S(2)}) copy-start(bf16[2048,128]{1,0:T(8,128)(2,1)} %param.24) | copy-start | bytes 1572868
  160.5 0.9 copy-start.2

commit v10 on v9

--- a/solution.py
+++ b/solution.py
@@ -30,7 +30,18 @@
     return lax.ppermute(block, axis, route)
 
 
-def gather_kernel(n_group, n_expert, wqkv, wo, xn, oqkv, oo, oxn, send, recv, xsend, xrecv, local):
+def gather_kernel(n_group, n_expert, heads_here, q_in, kv_in, o_in, h_in, gain_in, oqkv, oo, oxn, send, recv, xsend, xrecv, local, wqkv, wo, xn):
+    e_here = lax.axis_index("expert")
+    depth = HEAD_DIMENSION
+    column = pl.multiple_of(lax.div(e_here * heads_here, QUERY_HEADS // KEY_VALUE_HEADS) * depth, depth)
+    query_width = q_in.shape[1]
+    wqkv[:, 0:query_width] = q_in[...].astype(jnp.bfloat16)
+    wqkv[:, query_width : query_width + depth] = kv_in[0, :, pl.ds(column, depth)].astype(jnp.bfloat16)
+    wqkv[:, query_width + depth : query_width + 2 * depth] = kv_in[1, :, pl.ds(column, depth)].astype(
+        jnp.bfloat16
+    )
+    wo[...] = o_in[...].astype(jnp.bfloat16)
+    xn[...] = norm_rows(h_in[...], gain_in[...]).astype(jnp.bfloat16)
     g = lax.axis_index("group")
     e = lax.axis_index("expert")
     columns = n_group // 2
@@ -152,14 +163,20 @@
         copy.wait()
 
 
-def gather_all(wqkv, wo, xn, n_group, n_expert):
+def gather_all(q_in, kv_in, o_in, h_in, gain_in, n_group, n_expert):
     any_spec = pl.BlockSpec(memory_space=pl.ANY)
-    shapes = [jax.ShapeDtypeStruct((n_group,) + a.shape, a.dtype) for a in (wqkv, wo)]
-    shapes += [jax.ShapeDtypeStruct((n_expert,) + xn.shape, xn.dtype)]
+    vmem = pl.BlockSpec(memory_space=pltpu.VMEM)
+    depth = HEAD_DIMENSION
+    joined = (q_in.shape[0], q_in.shape[1] + 2 * depth)
+    shapes = [
+        jax.ShapeDtypeStruct((n_group,) + joined, jnp.bfloat16),
+        jax.ShapeDtypeStruct((n_group,) + o_in.shape, jnp.bfloat16),
+        jax.ShapeDtypeStruct((n_expert,) + h_in.shape, jnp.bfloat16),
+    ]
     return pl.pallas_call(
-        functools.partial(gather_kernel, n_group, n_expert),
+        functools.partial(gather_kernel, n_group, n_expert, q_in.shape[1] // depth),
         out_shape=tuple(shapes),
-        in_specs=[any_spec] * 3,
+        in_specs=[vmem] * 5,
         out_specs=tuple([any_spec] * 3),
         scratch_shapes=[
             pltpu.SemaphoreType.DMA((32,)),
@@ -167,9 +184,12 @@
             pltpu.SemaphoreType.DMA((n_expert,)),
             pltpu.SemaphoreType.DMA((n_expert,)),
             pltpu.SemaphoreType.DMA((3,)),
+            pltpu.VMEM(joined, jnp.bfloat16),
+            pltpu.VMEM(o_in.shape, jnp.bfloat16),
+            pltpu.VMEM(h_in.shape, jnp.bfloat16),
         ],
         compiler_params=pltpu.CompilerParams(collective_id=0, has_side_effects=True),
-    )(wqkv, wo, xn)
+    )(q_in, kv_in, o_in, h_in, gain_in)
 
 
 def combine_kernel(blocks, attended_ref, weight_ref, out_ref, outgoing, incoming, send, recv):
@@ -604,16 +624,12 @@
     width_here = local_head_count * HEAD_DIMENSION
     common_head = group_member * local_head_count // (QUERY_HEADS // KEY_VALUE_HEADS)
     groups_axis = lax.axis_size("group")
-    keyvalue_slice = lax.dynamic_slice_in_dim(
-        trainer_key_value_weight, common_head * HEAD_DIMENSION, HEAD_DIMENSION, 2
-    ).astype(jnp.bfloat16)
-    normed = norm_rows(hidden_in, norm_attention).astype(jnp.bfloat16)
     joined_parts, output_parts, normed_parts = gather_all(
-        jnp.concatenate(
-            [query_master.astype(jnp.bfloat16), keyvalue_slice[0], keyvalue_slice[1]], axis=1
-        ),
-        output_master.astype(jnp.bfloat16),
-        normed,
+        query_master,
+        trainer_key_value_weight,
+        output_master,
+        hidden_in,
+        norm_attention.reshape(1, -1),
         groups_axis,
         experts_axis,
     )

time: 193 us -> 193 us (level)
  other arithmetic: 18.2 us -> 14.3 us
  Pallas kernels: 153 us -> 155 us
    convert_element_type x3 -> x0, other arithmetic: 3.29 us -> none  [the longest x1 1.54 us: per_device(): output_master.astype(jnp.bfloat16)]
where the time goes in v10:
time: 193 us
  Pallas kernels  155 us (80%)
  other arithmetic  14.3 us (7%)
  local copies, waits for them, and re-layouts  9.78 us (5%)
  matrix products  7.7 us (4%)
  waiting for transfers between devices  4.84 us (3%)
    pallas_call x1, Pallas kernels, gather_all(): pl.pallas_call(functools.partial(gather_kernel, n_group, n_expert, q_in.s...  71.9 us
    pallas_call x1, Pallas kernels, combine_and_scatter(): pl.pallas_call(functools.partial(combine_scatter_kernel, blocks), out_sha...  45 us
    pallas_call x2, Pallas kernels, scatter_blocks(): pl.pallas_call(functools.partial(scatter_kernel, n_expert), out_shape=jax...  21.5 us
    pallas_call x1, Pallas kernels, attention(): pl.pallas_call(functools.partial(attention_kernel, scale, width // depth)...  9 us
    pallas_call x1, Pallas kernels, prep(): pl.pallas_call(functools.partial(prep_kernel, query_width), out_shape=(ja...  7.11 us
    ppermute x1, waiting for transfers between devices, from_partner(): return lax.ppermute(block, axis, route)  4.84 us
    dot_general x1, matrix products, per_device(): jnp.dot(flattened, gateup_here, preferred_element_type=jnp.float32)  4.04 us
  transfers between devices with their start and end apart: 1, of which 1 were waited for; matrix products, arithmetic and copies ran while one was open for 3% of the time, Pallas kernels for 0%

profile of v10, /device:TPU:1, one launch (start us, length us, event | category | flops | bytes accessed | tf_op | source)
XLA Modules:
  0.0 192.8 jit_solution(11626751342851502416)
XLA Ops:
  0.6 0.0 copy-start
  0.7 1.5 dynamic-slice_negate_fusion
  2.1 1.0 pad_maximum_fusion.cos_ref
  3.1 1.1 pad_maximum_fusion.1.sin_ref
  4.2 71.9 %shard_map.158 = (bf16[16,128,512]{2,1,0:T(8,128)(2,1)}, bf16[16,256,128]{2,1,0:T(8,128)(2,1)}, bf16[16,64,2048]{2,1,0:T(8,128)(2,1)}) custom-call(f32[128,256]{1,0:T(8,128)} %q_in.1, f32[2,128,512]{2,1,0:T(8,128)} %kv_in.1, f32[256,128]{1,0:T(8,128)} %o_in.1, bf16[64,2048]{1,0:T(8,128)(2,1)} %h_in.1, f32[1,2048]{1,0:T(1,128)} %bitcast.34), custom_call_target="tpu_custom_call" | custom-call | tf_op jit(solution)/shard_map/pallas_call | solution.py:176
  76.1 0.0 copy-start.6
  76.1 0.0 copy-start.7
  76.1 7.1 %shard_map.159 = (bf16[1024,256]{1,0:T(8,128)(2,1)}, bf16[1024,128]{1,0:T(8,128)(2,1)}, bf16[1024,128]{1,0:T(8,128)(2,1)}) custom-call(bf16[1024,2048]{1,0:T(8,128)(2,1)} %bitcast.35, bf16[2048,512]{1,0:T(8,128)(2,1)} %bitcast.36, f32[1024,128]{1,0:T(8,128)} %pad_maximum_fusion.cos_ref, f32[1024,128]{1,0:T(8,128)} %pad_maximum_fusion.1.sin_ref, ...), custom_call_target="tpu_custom_call" | custom-call | flops 2147483648 | bytes 7340032 | tf_op jit(solution)/shard_map/pallas_call | solution.py:563
  83.2 0.0 copy-start.2
  83.2 1.9 %pad_maximum_fusion.2 = bf16[2,1024,128]{2,1,0:T(8,128)(2,1)} fusion(bf16[1,1024,128]{2,1,0:T(8,128)(2,1)} %bitcast.31, bf16[1,1024,128]{2,1,0:T(8,128)(2,1)} %bitcast.30), kind=kLoop, calls=%fused_computation.17 | loop fusion | flops 262144 | bytes 1048576 | tf_op jit(solution)/shard_map/stack | solution.py:650
  85.2 0.8 collective-permute-start
  86.0 0.0 copy-done.6
  86.0 0.1 copy.20
  86.0 0.1 fusion.30
  86.2 0.1 select_reduce_fusion.2
  86.3 0.1 fusion.21
  86.4 0.1 reduce_window_sum.11
  86.5 0.2 select_reduce_fusion.1
  86.7 0.0 copy-done.7
  86.7 0.0 copy-start.3
  86.7 0.7 fusion.28
  87.4 1.3 compare_select_fusion.kpos_ref
  88.7 0.8 select_add_fusion.qpos_ref
  89.6 2.4 %copy_bitcast_fusion.weight_ref = bf16[256,2048]{1,0:T(8,128)(2,1)} fusion(bf16[16,256,128]{2,1,0:T(8,128)(2,1)} %get-tuple-element.13), kind=kLoop, calls=%fused_computation.9 | loop fusion | bytes 2097152 | tf_op jit(solution)/shard_map/reshape | solution.py:665
  91.9 4.8 %collective-permute-done = bf16[2,1024,128]{2,1,0:T(8,128)(2,1)} collective-permute-done((bf16[2,1024,128]{2,1,0:T(8,128)(2,1)}, bf16[2,1024,128]{2,1,0:T(8,128)(2,1)}, u32[]{:S(2)}, u32[]{:S(2)}) %collective-permute-start) | collective-permute-done | bytes 524320 | tf_op jit(solution)/shard_map/ppermute | solution.py:30
  96.8 1.1 slice_bitcast_fusion
  97.8 0.0 copy-done.3
  97.8 0.9 pad_maximum_fusion.4.v_ref
  98.7 0.0 copy-done.2
  98.7 0.8 pad_maximum_fusion.3.k_ref
  99.5 9.0 %shard_map.160.attended_ref = bf16[1024,256]{1,0:T(8,128)(2,1)} custom-call(bf16[1024,256]{1,0:T(8,128)(2,1)} %get-tuple-element.10.q_ref, bf16[2048,128]{1,0:T(8,128)(2,1)} %pad_maximum_fusion.3.k_ref, bf16[2048,128]{1,0:T(8,128)(2,1)} %pad_maximum_fusion.4.v_ref, s32[1024,1]{1,0:T(8,128)} %select_add_fusion.qpos_ref, s32[1,2048]{1,0:T(1,128)} %compare_select_fusion.kpos_ref), custom_call_target="tpu_custom_call" | custom-call | flops 2147483648 | bytes 2097152 | tf_op jit(solution)/shard_map/pallas_call | solution.py:481
  108.5 0.0 copy-start.5
  108.5 45.0 %shard_map.161 = bf16[8,64,2048]{2,1,0:T(8,128)(2,1)} custom-call(bf16[1024,256]{1,0:T(8,128)(2,1)} %shard_map.160.attended_ref, bf16[256,2048]{1,0:T(8,128)(2,1)} %copy_bitcast_fusion.weight_ref), custom_call_target="tpu_custom_call" | custom-call | tf_op jit(solution)/shard_map/pallas_call | solution.py:315
  153.5 0.0 copy-start.4
  153.5 2.1 %convert_reduce_fusion = f32[64,2048]{1,0:T(8,128)S(1)} fusion(bf16[8,64,2048]{2,1,0:T(8,128)(2,1)} %shard_map.161), kind=kLoop, calls=%fused_computation.2 | loop fusion | flops 1966080 | bytes 2621440 | tf_op jit(solution)/shard_map/reduce_sum | solution.py:667
  155.6 1.1 fusion.8
  156.8 0.0 copy-start.1
  156.8 0.0 copy-done.5
  156.8 0.0 copy-done.4
  156.8 0.3 fusion.15
  157.1 0.2 select_reduce_fusion
  157.3 0.1 exponential_reduce_fusion
  157.4 0.2 select_reduce_fusion.3
  157.6 1.0 convolution_convert_fusion
  158.6 1.7 reshape.125.part
  160.4 12.7 %shard_map.162 = bf16[16,4,2048]{2,1,0:T(4,128)(2,1)} custom-call(bf16[16,4,2048]{2,1,0:T(4,128)(2,1)} %reshape.125.part), custom_call_target="tpu_custom_call" | custom-call | tf_op jit(solution)/shard_map/pallas_call | solution.py:442
  173.1 1.7 reshape.126
  174.8 4.0 %fusion = f32[64,1536]{1,0:T(8,128)S(1)} fusion(bf16[64,2048]{1,0:T(8,128)(2,1)} %reshape.126, bf16[1,2048,1536]{2,1,0:T(8,128)(2,1)} %param.25), kind=kOutput, calls=%fused_computation | convolution fusion | flops 402653184 | bytes 6946816 | tf_op jit(solution)/shard_map/dot_general | solution.py:698
  178.8 0.0 copy-done.1
  178.8 0.0 copy-done
  178.8 1.4 fusion.5
  180.2 1.7 reshape.127.part
  182.0 8.8 %shard_map.163 = bf16[16,4,2048]{2,1,0:T(4,128)(2,1)} custom-call(bf16[16,4,2048]{2,1,0:T(4,128)(2,1)} %reshape.127.part), custom_call_target="tpu_custom_call" | custom-call | tf_op jit(solution)/shard_map/pallas_call | solution.py:442
  190.8 1.0 reshape.128
  191.9 1.0 fusion.4
  (4 shorter events, 0.0 us)
Async XLA Ops:
  0.6 178.2 %copy-start = (bf16[1,768,2048]{2,1,0:T(8,128)(2,1)S(1)}, bf16[1,768,2048]{2,1,0:T(8,128)(2,1)}, u32[]{:S(2)}) copy-start(bf16[1,768,2048]{2,1,0:T(8,128)(2,1)} %param.26) | copy-start | bytes 9437188
  76.1 9.9 %copy-start.6 = (s32[64,8]{0,1:T(8,128)S(1)}, s32[64,8]{0,1:T(8,128)}, u32[]{:S(2)}) copy-start(s32[64,8]{0,1:T(8,128)} %param.27) | copy-start | bytes 6148
  76.1 10.6 %copy-start.7 = (s32[8]{0:T(128)S(1)}, s32[8]{0:T(128)}, u32[]{:S(2)}) copy-start(s32[8]{0:T(128)} %param.23) | copy-start | bytes 100
  83.2 15.5 %copy-start.2 = (bf16[1024,128]{1,0:T(8,128)(2,1)S(1)}, bf16[1024,128]{1,0:T(8,128)(2,1)}, u32[]{:S(2)}) copy-start(bf16[1024,128]{1,0:T(8,128)(2,1)} %get-tuple-element.11) | copy-start | bytes 786436
  85.2 11.6 %collective-permute-start = (bf16[2,1024,128]{2,1,0:T(8,128)(2,1)}, bf16[2,1024,128]{2,1,0:T(8,128)(2,1)}, u32[]{:S(2)}, u32[]{:S(2)}) collective-permute-start(bf16[2,1024,128]{2,1,0:T(8,128)(2,1)} %pad_maximum_fusion.2), channel_id=1, source_target_pairs={{0,16},{16,0},{32,48},{48,32},{64,80},{80,64},{96,112},{112,96},{1... | collective-permute-start | bytes 1572872 | tf_op jit(solution)/shard_map/ppermute | solution.py:30
  86.7 11.1 %copy-start.3 = (bf16[1024,128]{1,0:T(8,128)(2,1)S(1)}, bf16[1024,128]{1,0:T(8,128)(2,1)}, u32[]{:S(2)}) copy-start(bf16[1024,128]{1,0:T(8,128)(2,1)} %get-tuple-element.12) | copy-start | bytes 786436
  108.5 48.2 %copy-start.5 = (f32[2048]{0:T(1024)S(1)}, f32[2048]{0:T(1024)}, u32[]{:S(2)}) copy-start(f32[2048]{0:T(1024)} %param.17) | copy-start | bytes 24580
  153.5 3.3 %copy-start.4 = (bf16[2048,128]{1,0:T(8,128)(2,1)S(1)}, bf16[2048,128]{1,0:T(8,128)(2,1)}, u32[]{:S(2)}) copy-start(bf16[2048,128]{1,0:T(8,128)(2,1)} %param.24) | copy-start | bytes 1572868
  156.8 22.1 %copy-start.1 = (bf16[64,2048]{1,0:T(8,128)(2,1)}, bf16[64,2048]{1,0:T(8,128)(2,1)S(1)}, u32[]{:S(2)}) copy-start(bf16[64,2048]{1,0:T(8,128)(2,1)S(1)} %get-tuple-element.15) | copy-start | bytes 786436

commit v11 on v10

--- a/solution.py
+++ b/solution.py
@@ -685,28 +685,24 @@
     select = (
         (jnp.arange(experts_axis * capacity)[:, None] == slot_index[None, :]) & present[None, :]
     ).astype(jnp.bfloat16)
-    outgoing = (
-        jnp.dot(select, normed_second, preferred_element_type=jnp.float32)
-        .astype(jnp.bfloat16)
-        .reshape(experts_axis, capacity, model_width)
-    )
+    select_slots = select.reshape(experts_axis, capacity, -1)
+    outgoing = jnp.einsum(
+        "jct,td->jcd", select_slots, normed_second, preferred_element_type=jnp.float32
+    ).astype(jnp.bfloat16)
     gateup_here = expert_gateup[0]
     down_here = expert_down[0]
     hidden_units = down_here.shape[0]
     slot_items = scatter_blocks(outgoing, experts_axis, 2)
-    flattened = slot_items.reshape(-1, slot_items.shape[-1])
-    gate_up = jnp.dot(flattened, gateup_here, preferred_element_type=jnp.float32)
-    active = (jax.nn.silu(gate_up[:, :hidden_units]) * gate_up[:, hidden_units:]).astype(
+    gate_up = jnp.einsum("jcd,df->jcf", slot_items, gateup_here, preferred_element_type=jnp.float32)
+    active = (jax.nn.silu(gate_up[..., :hidden_units]) * gate_up[..., hidden_units:]).astype(
         jnp.bfloat16
     )
-    result = (
-        jnp.dot(active, down_here, preferred_element_type=jnp.float32)
-        .astype(jnp.bfloat16)
-        .reshape(slot_items.shape)
-    )
+    result = jnp.einsum(
+        "jcf,fd->jcd", active, down_here, preferred_element_type=jnp.float32
+    ).astype(jnp.bfloat16)
     returned = scatter_blocks(result, experts_axis, 3)
-    combined = jnp.dot(
-        jnp.transpose(select), returned.reshape(-1, model_width), preferred_element_type=jnp.float32
+    combined = jnp.einsum(
+        "jct,jcd->td", select_slots, returned, preferred_element_type=jnp.float32
     )
     expert_mix = (gate_window[:, None] * combined).astype(jnp.bfloat16)
     return (hidden, expert_mix)

time: 193 us -> 189 us (0.979)
  local copies, waits for them, and re-layouts: 9.78 us -> 5.39 us
    reshape x4 -> x0, local copies, waits for them, and re-layouts: 6.22 us -> none  [the longest x1 1.75 us: per_device(): outgoing = jnp.dot(select, normed_second, preferred_element_type=jnp.floa...]
where the time goes in v11:
time: 189 us; the launch traced here: 188 us
  Pallas kernels  155 us (82%)
  other arithmetic  14.3 us (8%)
  matrix products  7.42 us (4%)
  local copies, waits for them, and re-layouts  5.39 us (3%)
  waiting for transfers between devices  4.91 us (3%)
    pallas_call x1, Pallas kernels, gather_all(): pl.pallas_call(functools.partial(gather_kernel, n_group, n_expert, q_in.s...  71.9 us
    pallas_call x1, Pallas kernels, combine_and_scatter(): pl.pallas_call(functools.partial(combine_scatter_kernel, blocks), out_sha...  45 us
    pallas_call x2, Pallas kernels, scatter_blocks(): pl.pallas_call(functools.partial(scatter_kernel, n_expert), out_shape=jax...  21.5 us
    pallas_call x1, Pallas kernels, attention(): pl.pallas_call(functools.partial(attention_kernel, scale, width // depth)...  9 us
    pallas_call x1, Pallas kernels, prep(): pl.pallas_call(functools.partial(prep_kernel, query_width), out_shape=(ja...  7.11 us
    ppermute x1, waiting for transfers between devices, from_partner(): return lax.ppermute(block, axis, route)  4.91 us
    dot_general x1, matrix products, per_device(): jnp.einsum('jcd,df->jcf', slot_items, gateup_here, preferred_element_type...  4.16 us
  transfers between devices with their start and end apart: 1, of which 1 were waited for; matrix products, arithmetic and copies ran while one was open for 3% of the time, Pallas kernels for 0%

profile of v11, /device:TPU:1, one launch (start us, length us, event | category | flops | bytes accessed | tf_op | source)
XLA Modules:
  0.0 188.2 jit_solution(12836641162702600900)
XLA Ops:
  0.6 0.0 copy-start
  0.7 1.5 dynamic-slice_negate_fusion
  2.1 1.0 pad_maximum_fusion.cos_ref
  3.1 1.1 pad_maximum_fusion.1.sin_ref
  4.2 71.9 %shard_map.158 = (bf16[16,128,512]{2,1,0:T(8,128)(2,1)}, bf16[16,256,128]{2,1,0:T(8,128)(2,1)}, bf16[16,64,2048]{2,1,0:T(8,128)(2,1)}) custom-call(f32[128,256]{1,0:T(8,128)} %q_in.1, f32[2,128,512]{2,1,0:T(8,128)} %kv_in.1, f32[256,128]{1,0:T(8,128)} %o_in.1, bf16[64,2048]{1,0:T(8,128)(2,1)} %h_in.1, f32[1,2048]{1,0:T(1,128)} %bitcast.41), custom_call_target="tpu_custom_call" | custom-call | tf_op jit(solution)/shard_map/pallas_call | solution.py:176
  76.1 0.0 copy-start.6
  76.1 0.0 copy-start.7
  76.1 7.1 %shard_map.159 = (bf16[1024,256]{1,0:T(8,128)(2,1)}, bf16[1024,128]{1,0:T(8,128)(2,1)}, bf16[1024,128]{1,0:T(8,128)(2,1)}) custom-call(bf16[1024,2048]{1,0:T(8,128)(2,1)} %bitcast.42, bf16[2048,512]{1,0:T(8,128)(2,1)} %bitcast.43, f32[1024,128]{1,0:T(8,128)} %pad_maximum_fusion.cos_ref, f32[1024,128]{1,0:T(8,128)} %pad_maximum_fusion.1.sin_ref, ...), custom_call_target="tpu_custom_call" | custom-call | flops 2147483648 | bytes 7340032 | tf_op jit(solution)/shard_map/pallas_call | solution.py:563
  83.2 0.0 copy-start.2
  83.2 1.9 %pad_maximum_fusion.2 = bf16[2,1024,128]{2,1,0:T(8,128)(2,1)} fusion(bf16[1,1024,128]{2,1,0:T(8,128)(2,1)} %bitcast.38, bf16[1,1024,128]{2,1,0:T(8,128)(2,1)} %bitcast.37), kind=kLoop, calls=%fused_computation.16 | loop fusion | flops 262144 | bytes 1048576 | tf_op jit(solution)/shard_map/stack | solution.py:650
  85.2 0.8 collective-permute-start
  86.0 0.8 select_add_fusion.qpos_ref
  86.8 0.0 copy-done.6
  86.8 0.1 copy.22
  86.9 0.1 fusion.31
  87.0 0.1 select_reduce_fusion.2
  87.1 0.1 fusion.20
  87.2 0.1 reduce_window_sum.11
  87.3 0.2 select_reduce_fusion.1
  87.5 0.0 copy-done.7
  87.5 0.0 copy-start.3
  87.5 0.7 fusion.29
  88.2 1.2 compare_select_fusion.kpos_ref
  89.5 2.4 %copy_bitcast_fusion.weight_ref = bf16[256,2048]{1,0:T(8,128)(2,1)} fusion(bf16[16,256,128]{2,1,0:T(8,128)(2,1)} %get-tuple-element.13), kind=kLoop, calls=%fused_computation.8 | loop fusion | bytes 2097152 | tf_op jit(solution)/shard_map/reshape | solution.py:665
  91.9 4.9 %collective-permute-done = bf16[2,1024,128]{2,1,0:T(8,128)(2,1)} collective-permute-done((bf16[2,1024,128]{2,1,0:T(8,128)(2,1)}, bf16[2,1024,128]{2,1,0:T(8,128)(2,1)}, u32[]{:S(2)}, u32[]{:S(2)}) %collective-permute-start) | collective-permute-done | bytes 524320 | tf_op jit(solution)/shard_map/ppermute | solution.py:30
  96.8 1.1 slice_bitcast_fusion
  97.8 0.0 copy-done.3
  97.8 0.9 pad_maximum_fusion.4.v_ref
  98.7 0.0 copy-done.2
  98.7 0.8 pad_maximum_fusion.3.k_ref
  99.5 9.0 %shard_map.160.attended_ref = bf16[1024,256]{1,0:T(8,128)(2,1)} custom-call(bf16[1024,256]{1,0:T(8,128)(2,1)} %get-tuple-element.10.q_ref, bf16[2048,128]{1,0:T(8,128)(2,1)} %pad_maximum_fusion.3.k_ref, bf16[2048,128]{1,0:T(8,128)(2,1)} %pad_maximum_fusion.4.v_ref, s32[1024,1]{1,0:T(8,128)} %select_add_fusion.qpos_ref, s32[1,2048]{1,0:T(1,128)} %compare_select_fusion.kpos_ref), custom_call_target="tpu_custom_call" | custom-call | flops 2147483648 | bytes 2097152 | tf_op jit(solution)/shard_map/pallas_call | solution.py:481
  108.5 0.0 copy-start.5
  108.5 45.0 %shard_map.161 = bf16[8,64,2048]{2,1,0:T(8,128)(2,1)} custom-call(bf16[1024,256]{1,0:T(8,128)(2,1)} %shard_map.160.attended_ref, bf16[256,2048]{1,0:T(8,128)(2,1)} %copy_bitcast_fusion.weight_ref), custom_call_target="tpu_custom_call" | custom-call | tf_op jit(solution)/shard_map/pallas_call | solution.py:315
  153.5 0.0 copy-start.4
  153.5 2.1 %convert_reduce_fusion = f32[64,2048]{1,0:T(8,128)S(1)} fusion(bf16[8,64,2048]{2,1,0:T(8,128)(2,1)} %shard_map.161), kind=kLoop, calls=%fused_computation.2 | loop fusion | flops 1966080 | bytes 2621440 | tf_op jit(solution)/shard_map/reduce_sum | solution.py:667
  155.6 1.1 fusion.6
  156.8 0.0 copy-start.1
  156.8 0.0 copy-done.5
  156.8 0.0 copy-done.4
  156.8 0.3 fusion.17
  157.1 0.2 select_reduce_fusion
  157.3 0.1 exponential_reduce_fusion
  157.4 0.2 select_reduce_fusion.3
  157.6 0.3 fusion.9
  157.9 0.9 copy.38.part
  158.9 12.7 %shard_map.162 = bf16[16,4,2048]{2,1,0:T(4,128)(2,1)} custom-call(bf16[16,4,2048]{2,1,0:T(4,128)(2,1)} %copy.38.part), custom_call_target="tpu_custom_call" | custom-call | tf_op jit(solution)/shard_map/pallas_call | solution.py:442
  171.5 4.2 %fusion = f32[16,4,1536]{2,0,1:T(8,128)S(1)} fusion(bf16[1,2048,1536]{2,1,0:T(8,128)(2,1)} %param.25, bf16[16,4,2048]{2,1,0:T(4,128)(2,1)} %shard_map.162), kind=kOutput, calls=%fused_computation | convolution fusion | flops 402653184 | bytes 6946816 | tf_op jit(solution)/shard_map/jcd,df->jcf/dot_general | solution.py:696
  175.7 0.0 copy-done.1
  175.7 0.0 copy-done
  175.7 0.7 fusion.2
  176.4 0.9 copy.37.part
  177.3 8.8 %shard_map.163 = bf16[16,4,2048]{2,1,0:T(4,128)(2,1)} custom-call(bf16[16,4,2048]{2,1,0:T(4,128)(2,1)} %copy.37.part), custom_call_target="tpu_custom_call" | custom-call | tf_op jit(solution)/shard_map/pallas_call | solution.py:442
  186.2 2.0 %fusion.5 = bf16[64,2048]{1,0:T(8,128)(2,1)} fusion(bf16[16,4,2048]{2,1,0:T(4,128)(2,1)} %shard_map.163, f32[64]{0:T(128)S(1)} %select_reduce_fusion.3, s32[64]{0:T(128)S(1)} %add_add_fusion, s32[16,4]{0,1:T(4,128)S(1)} %multiply_add_fusion, pred[64]{0:T(512)(128)(4,1)S(1)} %fusion.31), kind=kOutput, calls=%fused_computation.7 | convolution fusion | flops 17047552 | bytes 525120 | tf_op jit(solution)/shard_map/jct,jcd->td/dot_general | solution.py:704
  (5 shorter events, 0.0 us)
Async XLA Ops:
  0.6 175.1 %copy-start = (bf16[1,768,2048]{2,1,0:T(8,128)(2,1)S(1)}, bf16[1,768,2048]{2,1,0:T(8,128)(2,1)}, u32[]{:S(2)}) copy-start(bf16[1,768,2048]{2,1,0:T(8,128)(2,1)} %param.26) | copy-start | bytes 9437188
  76.1 10.7 %copy-start.6 = (s32[64,8]{0,1:T(8,128)S(1)}, s32[64,8]{0,1:T(8,128)}, u32[]{:S(2)}) copy-start(s32[64,8]{0,1:T(8,128)} %param.27) | copy-start | bytes 6148
  76.1 11.4 %copy-start.7 = (s32[8]{0:T(128)S(1)}, s32[8]{0:T(128)}, u32[]{:S(2)}) copy-start(s32[8]{0:T(128)} %param.23) | copy-start | bytes 100
  83.2 15.5 %copy-start.2 = (bf16[1024,128]{1,0:T(8,128)(2,1)S(1)}, bf16[1024,128]{1,0:T(8,128)(2,1)}, u32[]{:S(2)}) copy-start(bf16[1024,128]{1,0:T(8,128)(2,1)} %get-tuple-element.11) | copy-start | bytes 786436
  85.2 11.6 %collective-permute-start = (bf16[2,1024,128]{2,1,0:T(8,128)(2,1)}, bf16[2,1024,128]{2,1,0:T(8,128)(2,1)}, u32[]{:S(2)}, u32[]{:S(2)}) collective-permute-start(bf16[2,1024,128]{2,1,0:T(8,128)(2,1)} %pad_maximum_fusion.2), channel_id=1, source_target_pairs={{0,16},{16,0},{32,48},{48,32},{64,80},{80,64},{96,112},{112,96},{1... | collective-permute-start | bytes 1572872 | tf_op jit(solution)/shard_map/ppermute | solution.py:30
  87.5 10.3 %copy-start.3 = (bf16[1024,128]{1,0:T(8,128)(2,1)S(1)}, bf16[1024,128]{1,0:T(8,128)(2,1)}, u32[]{:S(2)}) copy-start(bf16[1024,128]{1,0:T(8,128)(2,1)} %get-tuple-element.12) | copy-start | bytes 786436
  108.5 48.2 %copy-start.5 = (f32[2048]{0:T(1024)S(1)}, f32[2048]{0:T(1024)}, u32[]{:S(2)}) copy-start(f32[2048]{0:T(1024)} %param.17) | copy-start | bytes 24580
  153.5 3.3 %copy-start.4 = (bf16[2048,128]{1,0:T(8,128)(2,1)S(1)}, bf16[2048,128]{1,0:T(8,128)(2,1)}, u32[]{:S(2)}) copy-start(bf16[2048,128]{1,0:T(8,128)(2,1)} %param.24) | copy-start | bytes 1572868
  156.8 18.9 %copy-start.1 = (bf16[64,2048]{1,0:T(8,128)(2,1)}, bf16[64,2048]{1,0:T(8,128)(2,1)S(1)}, u32[]{:S(2)}) copy-start(bf16[64,2048]{1,0:T(8,128)(2,1)S(1)} %get-tuple-element.15) | copy-start | bytes 786436

commit v12 on v11

--- a/solution.py
+++ b/solution.py
@@ -529,11 +529,17 @@
     return indices + offset
 
 
-def prep_kernel(query_width, x_ref, w_ref, cos_ref, sin_ref, qg_ref, kg_ref, q_out, k_out, v_out):
+def prep_kernel(query_width, x_ref, w_ref, table_ref, qg_ref, kg_ref, q_out, k_out, v_out):
     x = x_ref[...]
-    cosines = cos_ref[...]
-    sines = sin_ref[...]
-    depth = cosines.shape[1]
+    block = x.shape[0]
+    depth = table_ref.shape[1]
+    parity = lax.rem(lax.axis_index("group"), 2)
+    start = pl.multiple_of(parity * (table_ref.shape[0] // 2) + pl.program_id(0) * block, block)
+    table = table_ref[pl.ds(start, block), :]
+    swapped = pltpu.roll(table, depth // 2, 1)
+    first_half = lax.broadcasted_iota(jnp.int32, table.shape, 1) < depth // 2
+    cosines = jnp.where(first_half, table, swapped)
+    sines = jnp.where(first_half, -swapped, table)
 
     def project(start, stop):
         return jnp.dot(x, w_ref[:, start:stop], preferred_element_type=jnp.float32).astype(jnp.bfloat16)
@@ -553,9 +559,9 @@
     v_out[...] = project(query_width + depth, query_width + 2 * depth)
 
 
-def prep(normed_rows, joined, cosines, sines, query_gain, key_gain):
+def prep(normed_rows, joined, table, query_gain, key_gain):
     rows, width = normed_rows.shape
-    depth = cosines.shape[1]
+    depth = table.shape[1]
     query_width = joined.shape[1] - 2 * depth
     block = min(256, rows)
     whole = lambda shape: pl.BlockSpec(shape, lambda i: (0, 0))
@@ -571,8 +577,7 @@
         in_specs=[
             per_row(width),
             whole(joined.shape),
-            per_row(depth),
-            per_row(depth),
+            whole(table.shape),
             whole((1, depth)),
             whole((1, depth)),
         ],
@@ -582,25 +587,17 @@
             transcendentals=rows * (query_width // depth + 1),
             bytes_accessed=2 * (rows * width + width * joined.shape[1] + rows * joined.shape[1]),
         ),
-    )(normed_rows, joined, cosines, sines, query_gain.reshape(1, depth), key_gain.reshape(1, depth))
-
-
-def rope_tables(parity, row_count, depth):
+    )(normed_rows, joined, table, query_gain.reshape(1, depth), key_gain.reshape(1, depth))
+
+
+def rope_table(row_count, depth):
     half = depth // 2
     frequencies = rope_theta ** (-2.0 * np.arange(half) / depth)
     indices = np.arange(row_count)
     quarter = row_count // 2
     places = np.concatenate([np.where(indices < quarter, indices, indices + 2 * quarter), indices + quarter])
     angles = places[:, None].astype(np.float64) * frequencies[None, :]
-    cosines = jnp.asarray(np.cos(angles), jnp.float32)
-    sines = jnp.asarray(np.sin(angles), jnp.float32)
-    cosines = lax.dynamic_slice_in_dim(cosines, parity * row_count, row_count, 0)
-    sines = lax.dynamic_slice_in_dim(sines, parity * row_count, row_count, 0)
-    return (
-        jnp.concatenate([cosines, cosines], axis=1),
-        jnp.concatenate([-sines, sines], axis=1),
-    )
-
+    return jnp.asarray(np.concatenate([np.cos(angles), np.sin(angles)], axis=1), jnp.float32)
 
 def per_device(
     hidden_in,
@@ -638,12 +635,10 @@
     parity = group_index % 2
     own_places = local_positions(parity, local_rows)
     partner_places = local_positions(1 - parity, local_rows)
-    cosines, sines = rope_tables(parity, local_rows, HEAD_DIMENSION)
     query_rows_list, key_rows, value_rows = prep(
         normed_parts.reshape(local_rows, model_width),
         joined_parts.reshape(model_width, -1),
-        cosines,
-        sines,
+        rope_table(local_rows, HEAD_DIMENSION),
         query_gain,
         key_gain,
     )

time: 189 us -> 186 us (0.984)
  other arithmetic: 14.3 us -> 10 us
    concatenate x3 -> x0, other arithmetic: 2.92 us -> none  [the longest x1 1.05 us: rope_tables(): jnp.concatenate([-sines, sines], axis=1)]
where the time goes in v12:
time: 186 us; the launch traced here: 185 us
  Pallas kernels  155 us (83%)
  other arithmetic  10 us (5%)
  matrix products  8.46 us (5%)
  local copies, waits for them, and re-layouts  5.38 us (3%)
  waiting for transfers between devices  4.91 us (3%)
    pallas_call x1, Pallas kernels, gather_all(): pl.pallas_call(functools.partial(gather_kernel, n_group, n_expert, q_in.s...  72.2 us
    pallas_call x1, Pallas kernels, combine_and_scatter(): pl.pallas_call(functools.partial(combine_scatter_kernel, blocks), out_sha...  44.9 us
    pallas_call x2, Pallas kernels, scatter_blocks(): pl.pallas_call(functools.partial(scatter_kernel, n_expert), out_shape=jax...  21.5 us
    pallas_call x1, Pallas kernels, attention(): pl.pallas_call(functools.partial(attention_kernel, scale, width // depth)...  8.99 us
    pallas_call x1, Pallas kernels, prep(): pl.pallas_call(functools.partial(prep_kernel, query_width), out_shape=(ja...  7.21 us
    ppermute x1, waiting for transfers between devices, from_partner(): return lax.ppermute(block, axis, route)  4.91 us
    dot_general x1, matrix products, per_device(): jnp.einsum('jcd,df->jcf', slot_items, gateup_here, preferred_element_type...  4.16 us
  transfers between devices with their start and end apart: 1, of which 1 were waited for; matrix products, arithmetic and copies ran while one was open for 3% of the time, Pallas kernels for 0%

profile of v12, /device:TPU:1, one launch (start us, length us, event | category | flops | bytes accessed | tf_op | source)
XLA Modules:
  0.0 185.3 jit_solution(8524303332744283072)
XLA Ops:
  0.6 0.0 copy-start
  0.6 72.2 %shard_map.149 = (bf16[16,128,512]{2,1,0:T(8,128)(2,1)}, bf16[16,256,128]{2,1,0:T(8,128)(2,1)}, bf16[16,64,2048]{2,1,0:T(8,128)(2,1)}) custom-call(f32[128,256]{1,0:T(8,128)} %q_in.1, f32[2,128,512]{2,1,0:T(8,128)} %kv_in.1, f32[256,128]{1,0:T(8,128)} %o_in.1, bf16[64,2048]{1,0:T(8,128)(2,1)} %h_in.1, f32[1,2048]{1,0:T(1,128)} %bitcast.41), custom_call_target="tpu_custom_call" | custom-call | tf_op jit(solution)/shard_map/pallas_call | solution.py:176
  72.8 0.0 copy-start.5
  72.9 0.0 copy-start.6
  72.9 7.2 %shard_map.150 = (bf16[1024,256]{1,0:T(8,128)(2,1)}, bf16[1024,128]{1,0:T(8,128)(2,1)}, bf16[1024,128]{1,0:T(8,128)(2,1)}) custom-call(bf16[1024,2048]{1,0:T(8,128)(2,1)} %bitcast.42, bf16[2048,512]{1,0:T(8,128)(2,1)} %bitcast.43, f32[2048,128]{1,0:T(8,128)} %constant.63.clone.table_ref, f32[1,128]{1,0:T(1,128)} %bitcast.44, f32[1,128]{1,0:T(1,128)} %bitcast.45), custom_call_target="tpu_custom_call" | custom-call | flops 2147483648 | bytes 7340032 | tf_op jit(solution)/shard_map/pallas_call | solution.py:569
  80.1 0.0 copy-start.2
  80.1 1.9 %pad_maximum_fusion = bf16[2,1024,128]{2,1,0:T(8,128)(2,1)} fusion(bf16[1,1024,128]{2,1,0:T(8,128)(2,1)} %bitcast.38, bf16[1,1024,128]{2,1,0:T(8,128)(2,1)} %bitcast.37), kind=kLoop, calls=%fused_computation.14 | loop fusion | flops 262144 | bytes 1048576 | tf_op jit(solution)/shard_map/stack | solution.py:645
  82.0 0.8 collective-permute-start
  82.8 0.8 select_add_fusion.qpos_ref
  83.6 0.0 copy-done.5
  83.6 0.1 copy.21
  83.7 0.1 select_reduce_fusion.2
  83.8 0.1 fusion.31
  84.0 0.1 fusion.20
  84.1 0.1 reduce_window_sum.11
  84.2 0.2 select_reduce_fusion.1
  84.4 0.0 copy-done.6
  84.4 0.0 copy-start.3
  84.4 0.7 fusion.29
  85.1 1.2 compare_select_fusion.kpos_ref
  86.3 2.4 %copy_bitcast_fusion.weight_ref = bf16[256,2048]{1,0:T(8,128)(2,1)} fusion(bf16[16,256,128]{2,1,0:T(8,128)(2,1)} %get-tuple-element.13), kind=kLoop, calls=%fused_computation.8 | loop fusion | bytes 2097152 | tf_op jit(solution)/shard_map/reshape | solution.py:660
  88.7 4.9 %collective-permute-done = bf16[2,1024,128]{2,1,0:T(8,128)(2,1)} collective-permute-done((bf16[2,1024,128]{2,1,0:T(8,128)(2,1)}, bf16[2,1024,128]{2,1,0:T(8,128)(2,1)}, u32[]{:S(2)}, u32[]{:S(2)}) %collective-permute-start) | collective-permute-done | bytes 524320 | tf_op jit(solution)/shard_map/ppermute | solution.py:30
  93.6 1.1 slice_bitcast_fusion
  94.7 0.0 copy-done.2
  94.7 0.0 copy-done.3
  94.7 1.1 pad_maximum_fusion.1
  95.7 9.0 %shard_map.151.attended_ref = bf16[1024,256]{1,0:T(8,128)(2,1)} custom-call(bf16[1024,256]{1,0:T(8,128)(2,1)} %get-tuple-element.10.q_ref, bf16[2048,128]{1,0:T(8,128)(2,1)} %get-tuple-element.18.k_ref, bf16[2048,128]{1,0:T(8,128)(2,1)} %get-tuple-element.19.v_ref, s32[1024,1]{1,0:T(8,128)} %select_add_fusion.qpos_ref, s32[1,2048]{1,0:T(1,128)} %compare_select_fusion.kpos_ref), custom_call_target="tpu_custom_call" | custom-call | flops 2147483648 | bytes 2097152 | tf_op jit(solution)/shard_map/pallas_call | solution.py:481
  104.7 0.0 copy-start.4
  104.7 44.9 %shard_map.152 = bf16[8,64,2048]{2,1,0:T(8,128)(2,1)} custom-call(bf16[1024,256]{1,0:T(8,128)(2,1)} %shard_map.151.attended_ref, bf16[256,2048]{1,0:T(8,128)(2,1)} %copy_bitcast_fusion.weight_ref), custom_call_target="tpu_custom_call" | custom-call | tf_op jit(solution)/shard_map/pallas_call | solution.py:315
  149.7 2.0 %convert_reduce_fusion = f32[64,2048]{1,0:T(8,128)S(1)} fusion(bf16[8,64,2048]{2,1,0:T(8,128)(2,1)} %shard_map.152), kind=kLoop, calls=%fused_computation.2 | loop fusion | flops 1966080 | bytes 2621440 | tf_op jit(solution)/shard_map/reduce_sum | solution.py:662
  151.7 1.1 fusion.6
  152.8 0.0 copy-start.1
  152.9 0.0 copy-done.4
  152.9 0.3 fusion.9
  153.2 0.9 copy.37.part
  154.1 12.7 %shard_map.153 = bf16[16,4,2048]{2,1,0:T(4,128)(2,1)} custom-call(bf16[16,4,2048]{2,1,0:T(4,128)(2,1)} %copy.37.part), custom_call_target="tpu_custom_call" | custom-call | tf_op jit(solution)/shard_map/pallas_call | solution.py:442
  166.8 4.2 %fusion = f32[16,4,1536]{2,0,1:T(8,128)S(1)} fusion(bf16[1,2048,1536]{2,1,0:T(8,128)(2,1)} %param.24, bf16[16,4,2048]{2,1,0:T(4,128)(2,1)} %shard_map.153), kind=kOutput, calls=%fused_computation | convolution fusion | flops 402653184 | bytes 6946816 | tf_op jit(solution)/shard_map/jcd,df->jcf/dot_general | solution.py:691
  170.9 0.0 copy-done
  171.0 0.7 fusion.2
  171.6 0.9 copy.36.part
  172.5 8.8 %shard_map.154 = bf16[16,4,2048]{2,1,0:T(4,128)(2,1)} custom-call(bf16[16,4,2048]{2,1,0:T(4,128)(2,1)} %copy.36.part), custom_call_target="tpu_custom_call" | custom-call | tf_op jit(solution)/shard_map/pallas_call | solution.py:442
  181.4 0.0 copy-done.1
  181.4 1.3 fusion.17
  182.7 0.2 select_reduce_fusion
  183.0 0.1 exponential_reduce_fusion
  183.1 0.2 select_reduce_fusion.3
  183.3 2.0 %fusion.5 = bf16[64,2048]{1,0:T(8,128)(2,1)} fusion(bf16[16,4,2048]{2,1,0:T(4,128)(2,1)} %shard_map.154, f32[64]{0:T(128)S(1)} %select_reduce_fusion.3, s32[64]{0:T(128)S(1)} %add_add_fusion, s32[16,4]{0,1:T(4,128)S(1)} %multiply_add_fusion, pred[64]{0:T(512)(128)(4,1)S(1)} %fusion.31), kind=kOutput, calls=%fused_computation.7 | convolution fusion | flops 17047552 | bytes 525120 | tf_op jit(solution)/shard_map/jct,jcd->td/dot_general | solution.py:699
  (5 shorter events, 0.0 us)
Async XLA Ops:
  0.6 170.3 %copy-start = (bf16[1,768,2048]{2,1,0:T(8,128)(2,1)S(1)}, bf16[1,768,2048]{2,1,0:T(8,128)(2,1)}, u32[]{:S(2)}) copy-start(bf16[1,768,2048]{2,1,0:T(8,128)(2,1)} %param.25) | copy-start | bytes 9437188
  72.8 10.8 %copy-start.5 = (s32[64,8]{0,1:T(8,128)S(1)}, s32[64,8]{0,1:T(8,128)}, u32[]{:S(2)}) copy-start(s32[64,8]{0,1:T(8,128)} %param.26) | copy-start | bytes 6148
  72.9 11.5 %copy-start.6 = (s32[8]{0:T(128)S(1)}, s32[8]{0:T(128)}, u32[]{:S(2)}) copy-start(s32[8]{0:T(128)} %param.22) | copy-start | bytes 100
  80.1 14.6 %copy-start.2 = (bf16[1024,128]{1,0:T(8,128)(2,1)S(1)}, bf16[1024,128]{1,0:T(8,128)(2,1)}, u32[]{:S(2)}) copy-start(bf16[1024,128]{1,0:T(8,128)(2,1)} %get-tuple-element.11) | copy-start | bytes 786436
  82.0 11.6 %collective-permute-start = (bf16[2,1024,128]{2,1,0:T(8,128)(2,1)}, bf16[2,1024,128]{2,1,0:T(8,128)(2,1)}, u32[]{:S(2)}, u32[]{:S(2)}) collective-permute-start(bf16[2,1024,128]{2,1,0:T(8,128)(2,1)} %pad_maximum_fusion), channel_id=1, source_target_pairs={{0,16},{16,0},{32,48},{48,32},{64,80},{80,64},{96,112},{112,96},{1... | collective-permute-start | bytes 1572872 | tf_op jit(solution)/shard_map/ppermute | solution.py:30
  84.4 10.3 %copy-start.3 = (bf16[1024,128]{1,0:T(8,128)(2,1)S(1)}, bf16[1024,128]{1,0:T(8,128)(2,1)}, u32[]{:S(2)}) copy-start(bf16[1024,128]{1,0:T(8,128)(2,1)} %get-tuple-element.12) | copy-start | bytes 786436
  104.7 48.1 %copy-start.4 = (f32[2048]{0:T(1024)S(1)}, f32[2048]{0:T(1024)}, u32[]{:S(2)}) copy-start(f32[2048]{0:T(1024)} %param.16) | copy-start | bytes 24580
  152.8 28.6 %copy-start.1 = (bf16[64,2048]{1,0:T(8,128)(2,1)}, bf16[64,2048]{1,0:T(8,128)(2,1)S(1)}, u32[]{:S(2)}) copy-start(bf16[64,2048]{1,0:T(8,128)(2,1)S(1)} %get-tuple-element.15) | copy-start | bytes 786436

commit v13 on v12

--- a/solution.py
+++ b/solution.py
@@ -453,50 +453,69 @@
     )(part)
 
 
-def attention_kernel(scale, heads, q_ref, k_ref, v_ref, qpos_ref, kpos_ref, o_ref):
-    allowed = kpos_ref[...] <= qpos_ref[...]
-    keys = k_ref[...]
-    values = v_ref[...]
-    depth = keys.shape[1]
+def attention_kernel(scale, heads, q_ref, own_ref, far_ref, length_ref, o_ref):
+    block = q_ref.shape[0]
+    rows = own_ref.shape[1]
+    half = rows // 2
+    parity = lax.rem(lax.axis_index("group"), 2)
+
+    def places(side, shape, axis, start):
+        indices = lax.broadcasted_iota(jnp.int32, shape, axis) + start
+        return indices + jnp.where(side == 0, jnp.where(indices < half, 0, rows), half)
+
+    query_places = places(parity, (block, 1), 0, pl.program_id(0) * block)
+    length = length_ref[0, 0]
+    own_places = places(parity, (1, rows), 1, 0)
+    far_places = places(1 - parity, (1, rows), 1, 0)
+    own_allowed = (own_places <= query_places) & (own_places < length)
+    far_allowed = (far_places <= query_places) & (far_places < length)
+    own_keys, own_values = own_ref[0], own_ref[1]
+    far_keys, far_values = far_ref[0], far_ref[1]
+    depth = own_keys.shape[1]
+    contract = (((1,), (1,)), ((), ()))
     for h in range(heads):
         query = q_ref[:, h * depth : (h + 1) * depth]
-        scores = (
-            lax.dot_general(
-                query, keys, (((1,), (1,)), ((), ())), preferred_element_type=jnp.float32
-            )
-            * scale
-        )
-        weights = jnp.where(allowed, jnp.exp(scores), 0.0)
-        denominators = jnp.sum(weights, axis=-1, keepdims=True)
+        own_weights = jnp.where(
+            own_allowed,
+            jnp.exp(lax.dot_general(query, own_keys, contract, preferred_element_type=jnp.float32) * scale),
+            0.0,
+        )
+        far_weights = jnp.where(
+            far_allowed,
+            jnp.exp(lax.dot_general(query, far_keys, contract, preferred_element_type=jnp.float32) * scale),
+            0.0,
+        )
+        denominators = jnp.sum(own_weights, axis=-1, keepdims=True) + jnp.sum(
+            far_weights, axis=-1, keepdims=True
+        )
         weighted = jnp.dot(
-            weights.astype(jnp.bfloat16), values, preferred_element_type=jnp.float32
-        )
+            own_weights.astype(jnp.bfloat16), own_values, preferred_element_type=jnp.float32
+        ) + jnp.dot(far_weights.astype(jnp.bfloat16), far_values, preferred_element_type=jnp.float32)
         o_ref[:, h * depth : (h + 1) * depth] = (weighted / denominators).astype(o_ref.dtype)
 
 
-def attention(queries, keys, values, query_places, key_places, scale):
+def attention(queries, own_kv, far_kv, length, scale):
     rows, width = queries.shape
-    key_rows, depth = keys.shape
+    key_rows, depth = own_kv.shape[1:]
     block = min(256, rows)
+    pair = pl.BlockSpec((2, key_rows, depth), lambda i: (0, 0, 0))
     return pl.pallas_call(
         functools.partial(attention_kernel, scale, width // depth),
         out_shape=jax.ShapeDtypeStruct((rows, width), jnp.bfloat16),
         grid=(rows // block,),
         in_specs=[
             pl.BlockSpec((block, width), lambda i: (i, 0)),
-            pl.BlockSpec((key_rows, depth), lambda i: (0, 0)),
-            pl.BlockSpec((key_rows, depth), lambda i: (0, 0)),
-            pl.BlockSpec((block, 1), lambda i: (i, 0)),
-            pl.BlockSpec((1, key_rows), lambda i: (0, 0)),
+            pair,
+            pair,
+            pl.BlockSpec(memory_space=pltpu.SMEM),
         ],
         out_specs=pl.BlockSpec((block, width), lambda i: (i, 0)),
         cost_estimate=pl.CostEstimate(
-            flops=4 * rows * key_rows * width,
-            transcendentals=rows * key_rows * (width // depth),
-            bytes_accessed=2 * (2 * rows * width + 2 * key_rows * depth),
+            flops=8 * rows * key_rows * width,
+            transcendentals=2 * rows * key_rows * (width // depth),
+            bytes_accessed=2 * (2 * rows * width + 4 * key_rows * depth),
         ),
-    )(queries, keys, values, query_places.reshape(rows, 1), key_places.reshape(1, key_rows))
-
+    )(queries, own_kv, far_kv, length.reshape(1, 1))
 
 def norm_rows(values, gain_vector):
     widened = values.astype(jnp.float32)
@@ -529,7 +548,7 @@
     return indices + offset
 
 
-def prep_kernel(query_width, x_ref, w_ref, table_ref, qg_ref, kg_ref, q_out, k_out, v_out):
+def prep_kernel(query_width, x_ref, w_ref, table_ref, qg_ref, kg_ref, q_out, kv_out):
     x = x_ref[...]
     block = x.shape[0]
     depth = table_ref.shape[1]
@@ -555,8 +574,8 @@
         q_out[:, h * depth : (h + 1) * depth] = norm_rope(
             queries[:, h * depth : (h + 1) * depth], qg_ref[...]
         )
-    k_out[...] = norm_rope(project(query_width, query_width + depth), kg_ref[...])
-    v_out[...] = project(query_width + depth, query_width + 2 * depth)
+    kv_out[0] = norm_rope(project(query_width, query_width + depth), kg_ref[...])
+    kv_out[1] = project(query_width + depth, query_width + 2 * depth)
 
 
 def prep(normed_rows, joined, table, query_gain, key_gain):
@@ -570,8 +589,7 @@
         functools.partial(prep_kernel, query_width),
         out_shape=(
             jax.ShapeDtypeStruct((rows, query_width), jnp.bfloat16),
-            jax.ShapeDtypeStruct((rows, depth), jnp.bfloat16),
-            jax.ShapeDtypeStruct((rows, depth), jnp.bfloat16),
+            jax.ShapeDtypeStruct((2, rows, depth), jnp.bfloat16),
         ),
         grid=(rows // block,),
         in_specs=[
@@ -581,7 +599,7 @@
             whole((1, depth)),
             whole((1, depth)),
         ],
-        out_specs=(per_row(query_width), per_row(depth), per_row(depth)),
+        out_specs=(per_row(query_width), pl.BlockSpec((2, block, depth), lambda i: (0, i, 0))),
         cost_estimate=pl.CostEstimate(
             flops=2 * rows * width * joined.shape[1],
             transcendentals=rows * (query_width // depth + 1),
@@ -633,28 +651,20 @@
     model_width = hidden_in.shape[1]
     local_rows = normed_parts.shape[0] * normed_parts.shape[1]
     parity = group_index % 2
-    own_places = local_positions(parity, local_rows)
-    partner_places = local_positions(1 - parity, local_rows)
-    query_rows_list, key_rows, value_rows = prep(
+    query_rows_list, key_values = prep(
         normed_parts.reshape(local_rows, model_width),
         joined_parts.reshape(model_width, -1),
         rope_table(local_rows, HEAD_DIMENSION),
         query_gain,
         key_gain,
     )
-    partner = from_partner(jnp.stack([key_rows, value_rows]), "group", 0)
-    all_keys = jnp.concatenate([key_rows, partner[0]], axis=0)
-    all_values = jnp.concatenate([value_rows, partner[1]], axis=0)
-    key_places = jnp.concatenate([own_places, partner_places])
+    partner = from_partner(key_values, "group", 0)
     valid_length = jnp.sum(jnp.where(jnp.arange(lengths.shape[0]) == group_index // 2, lengths, 0))
-    past_end = jnp.full_like(key_places, 4 * key_places.shape[0])
-    key_limits = jnp.where(key_places < valid_length, key_places, past_end)
     attended = attention(
         query_rows_list,
-        all_keys,
-        all_values,
-        own_places,
-        key_limits,
+        key_values,
+        partner,
+        valid_length.astype(jnp.int32),
         HEAD_DIMENSION ** (-0.5),
     )
     output_weight = jnp.transpose(output_parts, (1, 0, 2)).reshape(output_parts.shape[1], -1)

time: 186 us -> 183 us (0.984)
  other arithmetic: 10 us -> 4.9 us
  waiting for transfers between devices: 4.91 us -> 7.08 us
    ppermute x1, waiting for transfers between devices: 4.91 us -> 7.08 us  [from_partner(): return lax.ppermute(block, axis, route)]
    another operation x1 -> x0, other arithmetic: 1.93 us -> none  [per_device(): partner = from_partner(jnp.stack([key_rows, value_rows]), 'group', 0)]
  transfers between devices with their start and end apart: 1 -> 1, of which waited for: 1 -> 1; matrix products, arithmetic and copies ran while one was open for 3% -> 2% of each run, Pallas kernels for 0% -> 0%
where the time goes in v13:
time: 183 us; the launch traced here: 182 us
  Pallas kernels  156 us (85%)
  matrix products  8.44 us (5%)
  waiting for transfers between devices  7.08 us (4%)
  other arithmetic  4.9 us (3%)
  local copies, waits for them, and re-layouts  4.31 us (2%)
    pallas_call x1, Pallas kernels, gather_all(): pl.pallas_call(functools.partial(gather_kernel, n_group, n_expert, q_in.s...  72.2 us
    pallas_call x1, Pallas kernels, combine_and_scatter(): pl.pallas_call(functools.partial(combine_scatter_kernel, blocks), out_sha...  44.9 us
    pallas_call x2, Pallas kernels, scatter_blocks(): pl.pallas_call(functools.partial(scatter_kernel, n_expert), out_shape=jax...  21.5 us
    pallas_call x1, Pallas kernels, attention(): pl.pallas_call(functools.partial(attention_kernel, scale, width // depth)...  9.89 us
    pallas_call x1, Pallas kernels, prep(): pl.pallas_call(functools.partial(prep_kernel, query_width), out_shape=(ja...  7.29 us
    ppermute x1, waiting for transfers between devices, from_partner(): return lax.ppermute(block, axis, route)  7.08 us
    dot_general x1, matrix products, per_device(): jnp.einsum('jcd,df->jcf', slot_items, gateup_here, preferred_element_type...  4.15 us
  transfers between devices with their start and end apart: 1, of which 1 were waited for; matrix products, arithmetic and copies ran while one was open for 2% of the time, Pallas kernels for 0%

profile of v13, /device:TPU:1, one launch (start us, length us, event | category | flops | bytes accessed | tf_op | source)
XLA Modules:
  0.0 182.2 jit_solution(3588311266827702606)
XLA Ops:
  0.6 0.0 copy-start
  0.6 72.2 %shard_map.149 = (bf16[16,128,512]{2,1,0:T(8,128)(2,1)}, bf16[16,256,128]{2,1,0:T(8,128)(2,1)}, bf16[16,64,2048]{2,1,0:T(8,128)(2,1)}) custom-call(f32[128,256]{1,0:T(8,128)} %q_in.1, f32[2,128,512]{2,1,0:T(8,128)} %kv_in.1, f32[256,128]{1,0:T(8,128)} %o_in.1, bf16[64,2048]{1,0:T(8,128)(2,1)} %h_in.1, f32[1,2048]{1,0:T(1,128)} %bitcast.30), custom_call_target="tpu_custom_call" | custom-call | tf_op jit(solution)/shard_map/pallas_call | solution.py:176
  72.8 0.0 copy-start.3
  72.9 0.0 copy-start.4
  72.9 7.3 %shard_map.150 = (bf16[1024,256]{1,0:T(8,128)(2,1)}, bf16[2,1024,128]{2,1,0:T(8,128)(2,1)}) custom-call(bf16[1024,2048]{1,0:T(8,128)(2,1)} %bitcast.31, bf16[2048,512]{1,0:T(8,128)(2,1)} %bitcast.32, f32[2048,128]{1,0:T(8,128)} %constant.45.clone.table_ref, f32[1,128]{1,0:T(1,128)} %bitcast.33, f32[1,128]{1,0:T(1,128)} %bitcast.34), custom_call_target="tpu_custom_call" | custom-call | flops 2147483648 | bytes 7340032 | tf_op jit(solution)/shard_map/pallas_call | solution.py:588
  80.2 0.8 collective-permute-start
  80.9 0.0 copy-done.3
  80.9 0.1 copy.21
  81.0 0.1 select_reduce_fusion.2
  81.1 0.1 fusion.29
  81.3 0.1 fusion.20
  81.4 0.1 reduce_window_sum.11
  81.4 0.2 select_reduce_fusion.1
  81.6 0.0 copy-done.4
  81.7 0.6 fusion.27
  82.3 2.4 %copy_bitcast_fusion.weight_ref = bf16[256,2048]{1,0:T(8,128)(2,1)} fusion(bf16[16,256,128]{2,1,0:T(8,128)(2,1)} %get-tuple-element.11), kind=kLoop, calls=%fused_computation.8 | loop fusion | bytes 2097152 | tf_op jit(solution)/shard_map/reshape | solution.py:670
  84.7 7.1 %collective-permute-done.far_ref = bf16[2,1024,128]{2,1,0:T(8,128)(2,1)} collective-permute-done((bf16[2,1024,128]{2,1,0:T(8,128)(2,1)}, bf16[2,1024,128]{2,1,0:T(8,128)(2,1)}, u32[]{:S(2)}, u32[]{:S(2)}) %collective-permute-start) | collective-permute-done | bytes 524320 | tf_op jit(solution)/shard_map/ppermute | solution.py:30
  91.7 9.9 %shard_map.151.attended_ref = bf16[1024,256]{1,0:T(8,128)(2,1)} custom-call(bf16[1024,256]{1,0:T(8,128)(2,1)} %get-tuple-element.9.q_ref, bf16[2,1024,128]{2,1,0:T(8,128)(2,1)} %get-tuple-element.10.own_ref, bf16[2,1024,128]{2,1,0:T(8,128)(2,1)} %collective-permute-done.far_ref, s32[1,1]{1,0:T(1,128)} %bitcast.5.length_ref), custom_call_target="tpu_custom_call" | custom-call | flops 2147483648 | bytes 2097152 | tf_op jit(solution)/shard_map/pallas_call | solution.py:502
  101.6 0.0 copy-start.2
  101.6 44.9 %shard_map.152 = bf16[8,64,2048]{2,1,0:T(8,128)(2,1)} custom-call(bf16[1024,256]{1,0:T(8,128)(2,1)} %shard_map.151.attended_ref, bf16[256,2048]{1,0:T(8,128)(2,1)} %copy_bitcast_fusion.weight_ref), custom_call_target="tpu_custom_call" | custom-call | tf_op jit(solution)/shard_map/pallas_call | solution.py:315
  146.6 2.0 %convert_reduce_fusion = f32[64,2048]{1,0:T(8,128)S(1)} fusion(bf16[8,64,2048]{2,1,0:T(8,128)(2,1)} %shard_map.152), kind=kLoop, calls=%fused_computation.2 | loop fusion | flops 1966080 | bytes 2621440 | tf_op jit(solution)/shard_map/reduce_sum | solution.py:672
  148.6 1.1 fusion.6
  149.7 0.0 copy-start.1
  149.8 0.0 copy-done.2
  149.8 0.3 fusion.9
  150.1 0.9 copy.37.part
  151.0 12.7 %shard_map.153 = bf16[16,4,2048]{2,1,0:T(4,128)(2,1)} custom-call(bf16[16,4,2048]{2,1,0:T(4,128)(2,1)} %copy.37.part), custom_call_target="tpu_custom_call" | custom-call | tf_op jit(solution)/shard_map/pallas_call | solution.py:442
  163.7 4.1 %fusion = f32[16,4,1536]{2,0,1:T(8,128)S(1)} fusion(bf16[1,2048,1536]{2,1,0:T(8,128)(2,1)} %param.24, bf16[16,4,2048]{2,1,0:T(4,128)(2,1)} %shard_map.153), kind=kOutput, calls=%fused_computation | convolution fusion | flops 402653184 | bytes 6946816 | tf_op jit(solution)/shard_map/jcd,df->jcf/dot_general | solution.py:701
  167.8 0.0 copy-done
  167.9 0.7 fusion.2
  168.5 0.9 copy.36.part
  169.4 8.9 %shard_map.154 = bf16[16,4,2048]{2,1,0:T(4,128)(2,1)} custom-call(bf16[16,4,2048]{2,1,0:T(4,128)(2,1)} %copy.36.part), custom_call_target="tpu_custom_call" | custom-call | tf_op jit(solution)/shard_map/pallas_call | solution.py:442
  178.3 0.0 copy-done.1
  178.3 1.3 fusion.17
  179.6 0.2 select_reduce_fusion
  179.9 0.1 exponential_reduce_fusion
  180.0 0.2 select_reduce_fusion.3
  180.2 2.0 %fusion.5 = bf16[64,2048]{1,0:T(8,128)(2,1)} fusion(bf16[16,4,2048]{2,1,0:T(4,128)(2,1)} %shard_map.154, f32[64]{0:T(128)S(1)} %select_reduce_fusion.3, s32[64]{0:T(128)S(1)} %add_add_fusion, s32[16,4]{0,1:T(4,128)S(1)} %multiply_add_fusion, pred[64]{0:T(512)(128)(4,1)S(1)} %fusion.29), kind=kOutput, calls=%fused_computation.7 | convolution fusion | flops 17047552 | bytes 525120 | tf_op jit(solution)/shard_map/jct,jcd->td/dot_general | solution.py:709
  (3 shorter events, 0.0 us)
Async XLA Ops:
  0.6 167.2 %copy-start = (bf16[1,768,2048]{2,1,0:T(8,128)(2,1)S(1)}, bf16[1,768,2048]{2,1,0:T(8,128)(2,1)}, u32[]{:S(2)}) copy-start(bf16[1,768,2048]{2,1,0:T(8,128)(2,1)} %param.25) | copy-start | bytes 9437188
  72.8 8.1 %copy-start.3 = (s32[64,8]{0,1:T(8,128)S(1)}, s32[64,8]{0,1:T(8,128)}, u32[]{:S(2)}) copy-start(s32[64,8]{0,1:T(8,128)} %param.26) | copy-start | bytes 6148
  72.9 8.8 %copy-start.4 = (s32[8]{0:T(128)S(1)}, s32[8]{0:T(128)}, u32[]{:S(2)}) copy-start(s32[8]{0:T(128)} %param.22) | copy-start | bytes 100
  80.2 11.6 %collective-permute-start = (bf16[2,1024,128]{2,1,0:T(8,128)(2,1)}, bf16[2,1024,128]{2,1,0:T(8,128)(2,1)}, u32[]{:S(2)}, u32[]{:S(2)}) collective-permute-start(bf16[2,1024,128]{2,1,0:T(8,128)(2,1)} %get-tuple-element.10.own_ref), channel_id=1, source_target_pairs={{0,16},{16,0},{32,48},{48,32},{64,80},{80,64},{96,112},{112,96},{1... | collective-permute-start | bytes 1572872 | tf_op jit(solution)/shard_map/ppermute | solution.py:30
  101.6 48.1 %copy-start.2 = (f32[2048]{0:T(1024)S(1)}, f32[2048]{0:T(1024)}, u32[]{:S(2)}) copy-start(f32[2048]{0:T(1024)} %param.16) | copy-start | bytes 24580
  149.7 28.6 %copy-start.1 = (bf16[64,2048]{1,0:T(8,128)(2,1)}, bf16[64,2048]{1,0:T(8,128)(2,1)S(1)}, u32[]{:S(2)}) copy-start(bf16[64,2048]{1,0:T(8,128)(2,1)S(1)} %get-tuple-element.13) | copy-start | bytes 786436

commit v14 on v13

--- a/solution.py
+++ b/solution.py
@@ -548,7 +548,7 @@
     return indices + offset
 
 
-def prep_kernel(query_width, x_ref, w_ref, table_ref, qg_ref, kg_ref, q_out, kv_out):
+def prep_kernel(query_width, for_queries, x_ref, w_ref, table_ref, gain_ref, out_ref):
     x = x_ref[...]
     block = x.shape[0]
     depth = table_ref.shape[1]
@@ -569,44 +569,48 @@
         normed = values * inverse_rms * gain
         return (normed * cosines + pltpu.roll(normed, depth // 2, 1) * sines).astype(jnp.bfloat16)
 
-    queries = project(0, query_width)
-    for h in range(queries.shape[1] // depth):
-        q_out[:, h * depth : (h + 1) * depth] = norm_rope(
-            queries[:, h * depth : (h + 1) * depth], qg_ref[...]
-        )
-    kv_out[0] = norm_rope(project(query_width, query_width + depth), kg_ref[...])
-    kv_out[1] = project(query_width + depth, query_width + 2 * depth)
-
-
-def prep(normed_rows, joined, table, query_gain, key_gain):
+    if for_queries:
+        queries = project(0, query_width)
+        for h in range(queries.shape[1] // depth):
+            out_ref[:, h * depth : (h + 1) * depth] = norm_rope(
+                queries[:, h * depth : (h + 1) * depth], gain_ref[...]
+            )
+    else:
+        out_ref[0] = norm_rope(project(query_width, query_width + depth), gain_ref[...])
+        out_ref[1] = project(query_width + depth, query_width + 2 * depth)
+
+
+def prep(normed_rows, joined, table, gain, for_queries):
     rows, width = normed_rows.shape
     depth = table.shape[1]
     query_width = joined.shape[1] - 2 * depth
     block = min(256, rows)
     whole = lambda shape: pl.BlockSpec(shape, lambda i: (0, 0))
-    per_row = lambda cols: pl.BlockSpec((block, cols), lambda i: (i, 0))
+    if for_queries:
+        out_shape = jax.ShapeDtypeStruct((rows, query_width), jnp.bfloat16)
+        out_spec = pl.BlockSpec((block, query_width), lambda i: (i, 0))
+        columns = query_width
+    else:
+        out_shape = jax.ShapeDtypeStruct((2, rows, depth), jnp.bfloat16)
+        out_spec = pl.BlockSpec((2, block, depth), lambda i: (0, i, 0))
+        columns = 2 * depth
     return pl.pallas_call(
-        functools.partial(prep_kernel, query_width),
-        out_shape=(
-            jax.ShapeDtypeStruct((rows, query_width), jnp.bfloat16),
-            jax.ShapeDtypeStruct((2, rows, depth), jnp.bfloat16),
-        ),
+        functools.partial(prep_kernel, query_width, for_queries),
+        out_shape=out_shape,
         grid=(rows // block,),
         in_specs=[
-            per_row(width),
+            pl.BlockSpec((block, width), lambda i: (i, 0)),
             whole(joined.shape),
             whole(table.shape),
             whole((1, depth)),
-            whole((1, depth)),
         ],
-        out_specs=(per_row(query_width), pl.BlockSpec((2, block, depth), lambda i: (0, i, 0))),
+        out_specs=out_spec,
         cost_estimate=pl.CostEstimate(
-            flops=2 * rows * width * joined.shape[1],
-            transcendentals=rows * (query_width // depth + 1),
-            bytes_accessed=2 * (rows * width + width * joined.shape[1] + rows * joined.shape[1]),
+            flops=2 * rows * width * columns,
+            transcendentals=rows * (columns // depth),
+            bytes_accessed=2 * (rows * width + width * columns + rows * columns),
         ),
-    )(normed_rows, joined, table, query_gain.reshape(1, depth), key_gain.reshape(1, depth))
-
+    )(normed_rows, joined, table, gain.reshape(1, depth))
 
 def rope_table(row_count, depth):
     half = depth // 2
@@ -651,13 +655,13 @@
     model_width = hidden_in.shape[1]
     local_rows = normed_parts.shape[0] * normed_parts.shape[1]
     parity = group_index % 2
-    query_rows_list, key_values = prep(
+    prep_args = (
         normed_parts.reshape(local_rows, model_width),
         joined_parts.reshape(model_width, -1),
         rope_table(local_rows, HEAD_DIMENSION),
-        query_gain,
-        key_gain,
-    )
+    )
+    key_values = prep(*prep_args, key_gain, False)
+    query_rows_list = prep(*prep_args, query_gain, True)
     partner = from_partner(key_values, "group", 0)
     valid_length = jnp.sum(jnp.where(jnp.arange(lengths.shape[0]) == group_index // 2, lengths, 0))
     attended = attention(

time: 183 us -> 182 us (level)
  waiting for transfers between devices: 7.08 us -> 1.04 us
  Pallas kernels: 156 us -> 161 us
    ppermute x1, waiting for transfers between devices: 7.08 us -> 1.04 us  [from_partner(): return lax.ppermute(block, axis, route)]
    pallas_call x1 -> x2, Pallas kernels: 7.29 us -> 12.4 us  [prep(): pl.pallas_call(functools.partial(prep_kernel, query_width, for_queries),...]
  transfers between devices with their start and end apart: 1 -> 1, of which waited for: 1 -> 1; matrix products, arithmetic and copies ran while one was open for 2% -> 2% of each run, Pallas kernels for 0% -> 3%
where the time goes in v14:
time: 182 us; the launch traced here: 181 us
  Pallas kernels  161 us (88%)
  matrix products  8.45 us (5%)
  other arithmetic  4.9 us (3%)
  local copies, waits for them, and re-layouts  4.31 us (2%)
    pallas_call x1, Pallas kernels, gather_all(): pl.pallas_call(functools.partial(gather_kernel, n_group, n_expert, q_in.s...  72.2 us
    pallas_call x1, Pallas kernels, combine_and_scatter(): pl.pallas_call(functools.partial(combine_scatter_kernel, blocks), out_sha...  45 us
    pallas_call x2, Pallas kernels, scatter_blocks(): pl.pallas_call(functools.partial(scatter_kernel, n_expert), out_shape=jax...  21.5 us
    pallas_call x2, Pallas kernels, prep(): pl.pallas_call(functools.partial(prep_kernel, query_width, for_queries),...  12.4 us
    pallas_call x1, Pallas kernels, attention(): pl.pallas_call(functools.partial(attention_kernel, scale, width // depth)...  9.89 us
    dot_general x1, matrix products, per_device(): jnp.einsum('jcd,df->jcf', slot_items, gateup_here, preferred_element_type...  4.15 us
  transfers between devices with their start and end apart: 1, of which 1 were waited for; matrix products, arithmetic and copies ran while one was open for 2% of the time, Pallas kernels for 3%

profile of v14, /device:TPU:1, one launch (start us, length us, event | category | flops | bytes accessed | tf_op | source)
XLA Modules:
  0.0 181.3 jit_solution(10723301755811852003)
XLA Ops:
  0.6 0.0 copy-start
  0.6 72.2 %shard_map.149 = (bf16[16,128,512]{2,1,0:T(8,128)(2,1)}, bf16[16,256,128]{2,1,0:T(8,128)(2,1)}, bf16[16,64,2048]{2,1,0:T(8,128)(2,1)}) custom-call(f32[128,256]{1,0:T(8,128)} %q_in.1, f32[2,128,512]{2,1,0:T(8,128)} %kv_in.1, f32[256,128]{1,0:T(8,128)} %o_in.1, bf16[64,2048]{1,0:T(8,128)(2,1)} %h_in.1, f32[1,2048]{1,0:T(1,128)} %bitcast.34), custom_call_target="tpu_custom_call" | custom-call | tf_op jit(solution)/shard_map/pallas_call | solution.py:176
  72.8 0.0 copy-start.3
  72.9 0.0 copy-start.4
  72.9 6.4 %shard_map.151.own_ref = bf16[2,1024,128]{2,1,0:T(8,128)(2,1)} custom-call(bf16[1024,2048]{1,0:T(8,128)(2,1)} %bitcast.30, bf16[2048,512]{1,0:T(8,128)(2,1)} %bitcast.32, f32[2048,128]{1,0:T(8,128)} %constant.45.clone.table_ref, f32[1,128]{1,0:T(1,128)} %bitcast.35), custom_call_target="tpu_custom_call" | custom-call | flops 1073741824 | bytes 5767168 | tf_op jit(solution)/shard_map/pallas_call | solution.py:597
  79.3 0.8 collective-permute-start
  80.1 0.0 copy-done.3
  80.1 0.1 copy.21
  80.1 0.1 select_reduce_fusion.2
  80.3 0.1 fusion.29
  80.4 0.1 fusion.20
  80.5 0.1 reduce_window_sum.11
  80.6 0.2 select_reduce_fusion.1
  80.8 0.0 copy-done.4
  80.8 0.6 fusion.27
  81.4 6.0 %shard_map.150.q_ref = bf16[1024,256]{1,0:T(8,128)(2,1)} custom-call(bf16[1024,2048]{1,0:T(8,128)(2,1)} %bitcast.31, bf16[2048,512]{1,0:T(8,128)(2,1)} %bitcast.33, f32[2048,128]{1,0:T(8,128)} %constant.45.clone.table_ref, f32[1,128]{1,0:T(1,128)} %bitcast.36), custom_call_target="tpu_custom_call" | custom-call | flops 1073741824 | bytes 5767168 | tf_op jit(solution)/shard_map/pallas_call | solution.py:597
  87.4 2.4 %copy_bitcast_fusion.weight_ref = bf16[256,2048]{1,0:T(8,128)(2,1)} fusion(bf16[16,256,128]{2,1,0:T(8,128)(2,1)} %get-tuple-element.7), kind=kLoop, calls=%fused_computation.8 | loop fusion | bytes 2097152 | tf_op jit(solution)/shard_map/reshape | solution.py:674
  89.8 1.0 collective-permute-done.far_ref
  90.8 9.9 %shard_map.152.attended_ref = bf16[1024,256]{1,0:T(8,128)(2,1)} custom-call(bf16[1024,256]{1,0:T(8,128)(2,1)} %shard_map.150.q_ref, bf16[2,1024,128]{2,1,0:T(8,128)(2,1)} %shard_map.151.own_ref, bf16[2,1024,128]{2,1,0:T(8,128)(2,1)} %collective-permute-done.far_ref, s32[1,1]{1,0:T(1,128)} %bitcast.5.length_ref), custom_call_target="tpu_custom_call" | custom-call | flops 2147483648 | bytes 2097152 | tf_op jit(solution)/shard_map/pallas_call | solution.py:502
  100.7 0.0 copy-start.2
  100.7 45.0 %shard_map.153 = bf16[8,64,2048]{2,1,0:T(8,128)(2,1)} custom-call(bf16[1024,256]{1,0:T(8,128)(2,1)} %shard_map.152.attended_ref, bf16[256,2048]{1,0:T(8,128)(2,1)} %copy_bitcast_fusion.weight_ref), custom_call_target="tpu_custom_call" | custom-call | tf_op jit(solution)/shard_map/pallas_call | solution.py:315
  145.7 2.0 %convert_reduce_fusion = f32[64,2048]{1,0:T(8,128)S(1)} fusion(bf16[8,64,2048]{2,1,0:T(8,128)(2,1)} %shard_map.153), kind=kLoop, calls=%fused_computation.2 | loop fusion | flops 1966080 | bytes 2621440 | tf_op jit(solution)/shard_map/reduce_sum | solution.py:676
  147.8 1.1 fusion.6
  148.9 0.0 copy-start.1
  148.9 0.0 copy-done.2
  148.9 0.3 fusion.9
  149.2 0.9 copy.37.part
  150.1 12.6 %shard_map.154 = bf16[16,4,2048]{2,1,0:T(4,128)(2,1)} custom-call(bf16[16,4,2048]{2,1,0:T(4,128)(2,1)} %copy.37.part), custom_call_target="tpu_custom_call" | custom-call | tf_op jit(solution)/shard_map/pallas_call | solution.py:442
  162.8 4.2 %fusion = f32[16,4,1536]{2,0,1:T(8,128)S(1)} fusion(bf16[1,2048,1536]{2,1,0:T(8,128)(2,1)} %param.24, bf16[16,4,2048]{2,1,0:T(4,128)(2,1)} %shard_map.154), kind=kOutput, calls=%fused_computation | convolution fusion | flops 402653184 | bytes 6946816 | tf_op jit(solution)/shard_map/jcd,df->jcf/dot_general | solution.py:705
  167.0 0.0 copy-done
  167.0 0.7 fusion.2
  167.6 0.9 copy.36.part
  168.6 8.8 %shard_map.155 = bf16[16,4,2048]{2,1,0:T(4,128)(2,1)} custom-call(bf16[16,4,2048]{2,1,0:T(4,128)(2,1)} %copy.36.part), custom_call_target="tpu_custom_call" | custom-call | tf_op jit(solution)/shard_map/pallas_call | solution.py:442
  177.4 0.0 copy-done.1
  177.4 1.3 fusion.17
  178.7 0.2 select_reduce_fusion
  179.0 0.1 exponential_reduce_fusion
  179.1 0.2 select_reduce_fusion.3
  179.3 2.0 %fusion.5 = bf16[64,2048]{1,0:T(8,128)(2,1)} fusion(bf16[16,4,2048]{2,1,0:T(4,128)(2,1)} %shard_map.155, f32[64]{0:T(128)S(1)} %select_reduce_fusion.3, s32[64]{0:T(128)S(1)} %add_add_fusion, s32[16,4]{0,1:T(4,128)S(1)} %multiply_add_fusion, pred[64]{0:T(512)(128)(4,1)S(1)} %fusion.29), kind=kOutput, calls=%fused_computation.7 | convolution fusion | flops 17047552 | bytes 525120 | tf_op jit(solution)/shard_map/jct,jcd->td/dot_general | solution.py:713
  (3 shorter events, 0.0 us)
Async XLA Ops:
  0.6 166.3 %copy-start = (bf16[1,768,2048]{2,1,0:T(8,128)(2,1)S(1)}, bf16[1,768,2048]{2,1,0:T(8,128)(2,1)}, u32[]{:S(2)}) copy-start(bf16[1,768,2048]{2,1,0:T(8,128)(2,1)} %param.25) | copy-start | bytes 9437188
  72.8 7.2 %copy-start.3 = (s32[64,8]{0,1:T(8,128)S(1)}, s32[64,8]{0,1:T(8,128)}, u32[]{:S(2)}) copy-start(s32[64,8]{0,1:T(8,128)} %param.26) | copy-start | bytes 6148
  72.9 7.9 %copy-start.4 = (s32[8]{0:T(128)S(1)}, s32[8]{0:T(128)}, u32[]{:S(2)}) copy-start(s32[8]{0:T(128)} %param.22) | copy-start | bytes 100
  79.3 11.6 %collective-permute-start = (bf16[2,1024,128]{2,1,0:T(8,128)(2,1)}, bf16[2,1024,128]{2,1,0:T(8,128)(2,1)}, u32[]{:S(2)}, u32[]{:S(2)}) collective-permute-start(bf16[2,1024,128]{2,1,0:T(8,128)(2,1)} %shard_map.151.own_ref), channel_id=1, source_target_pairs={{0,16},{16,0},{32,48},{48,32},{64,80},{80,64},{96,112},{112,96},{1... | collective-permute-start | bytes 1572872 | tf_op jit(solution)/shard_map/ppermute | solution.py:30
  100.7 48.2 %copy-start.2 = (f32[2048]{0:T(1024)S(1)}, f32[2048]{0:T(1024)}, u32[]{:S(2)}) copy-start(f32[2048]{0:T(1024)} %param.16) | copy-start | bytes 24580
  148.9 28.5 %copy-start.1 = (bf16[64,2048]{1,0:T(8,128)(2,1)}, bf16[64,2048]{1,0:T(8,128)(2,1)S(1)}, u32[]{:S(2)}) copy-start(bf16[64,2048]{1,0:T(8,128)(2,1)S(1)} %get-tuple-element.9) | copy-start | bytes 786436

commit v15 on v14

--- a/solution.py
+++ b/solution.py
@@ -576,8 +576,8 @@
                 queries[:, h * depth : (h + 1) * depth], gain_ref[...]
             )
     else:
-        out_ref[0] = norm_rope(project(query_width, query_width + depth), gain_ref[...])
-        out_ref[1] = project(query_width + depth, query_width + 2 * depth)
+        out_ref[0] = norm_rope(project(0, depth), gain_ref[...])
+        out_ref[1] = project(depth, 2 * depth)
 
 
 def prep(normed_rows, joined, table, gain, for_queries):
@@ -600,7 +600,7 @@
         grid=(rows // block,),
         in_specs=[
             pl.BlockSpec((block, width), lambda i: (i, 0)),
-            whole(joined.shape),
+            pl.BlockSpec((width, columns), lambda i: (0, 0 if for_queries else 1)),
             whole(table.shape),
             whole((1, depth)),
         ],

time: 182 us -> 181 us (level)
  no operation moved by 1% of the time
where the time goes in v15:
time: 181 us
  Pallas kernels  160 us (88%)
  matrix products  8.44 us (5%)
  other arithmetic  4.9 us (3%)
  local copies, waits for them, and re-layouts  4.31 us (2%)
    pallas_call x1, Pallas kernels, gather_all(): pl.pallas_call(functools.partial(gather_kernel, n_group, n_expert, q_in.s...  72.2 us
    pallas_call x1, Pallas kernels, combine_and_scatter(): pl.pallas_call(functools.partial(combine_scatter_kernel, blocks), out_sha...  44.9 us
    pallas_call x2, Pallas kernels, scatter_blocks(): pl.pallas_call(functools.partial(scatter_kernel, n_expert), out_shape=jax...  21.5 us
    pallas_call x2, Pallas kernels, prep(): pl.pallas_call(functools.partial(prep_kernel, query_width, for_queries),...  11.8 us
    pallas_call x1, Pallas kernels, attention(): pl.pallas_call(functools.partial(attention_kernel, scale, width // depth)...  9.88 us
    dot_general x1, matrix products, per_device(): jnp.einsum('jcd,df->jcf', slot_items, gateup_here, preferred_element_type...  4.15 us
  transfers between devices with their start and end apart: 1, of which 1 were waited for; matrix products, arithmetic and copies ran while one was open for 2% of the time, Pallas kernels for 3%

profile of v15, /device:TPU:1, one launch (start us, length us, event | category | flops | bytes accessed | tf_op | source)
XLA Modules:
  0.0 180.9 jit_solution(2682715200971191947)
XLA Ops:
  0.6 0.0 copy-start
  0.6 72.2 %shard_map.149 = (bf16[16,128,512]{2,1,0:T(8,128)(2,1)}, bf16[16,256,128]{2,1,0:T(8,128)(2,1)}, bf16[16,64,2048]{2,1,0:T(8,128)(2,1)}) custom-call(f32[128,256]{1,0:T(8,128)} %q_in.1, f32[2,128,512]{2,1,0:T(8,128)} %kv_in.1, f32[256,128]{1,0:T(8,128)} %o_in.1, bf16[64,2048]{1,0:T(8,128)(2,1)} %h_in.1, f32[1,2048]{1,0:T(1,128)} %bitcast.34), custom_call_target="tpu_custom_call" | custom-call | tf_op jit(solution)/shard_map/pallas_call | solution.py:176
  72.8 0.0 copy-start.3
  72.9 0.0 copy-start.4
  72.9 6.0 %shard_map.151.own_ref = bf16[2,1024,128]{2,1,0:T(8,128)(2,1)} custom-call(bf16[1024,2048]{1,0:T(8,128)(2,1)} %bitcast.30, bf16[2048,512]{1,0:T(8,128)(2,1)} %bitcast.32, f32[2048,128]{1,0:T(8,128)} %constant.45.clone.table_ref, f32[1,128]{1,0:T(1,128)} %bitcast.35), custom_call_target="tpu_custom_call" | custom-call | flops 1073741824 | bytes 5767168 | tf_op jit(solution)/shard_map/pallas_call | solution.py:597
  78.9 0.8 collective-permute-start
  79.7 0.0 copy-done.3
  79.7 0.1 copy.21
  79.8 0.1 select_reduce_fusion.2
  79.9 0.1 fusion.29
  80.0 0.1 fusion.20
  80.1 0.1 reduce_window_sum.11
  80.2 0.2 select_reduce_fusion.1
  80.4 0.0 copy-done.4
  80.4 0.6 fusion.27
  81.1 5.7 %shard_map.150.q_ref = bf16[1024,256]{1,0:T(8,128)(2,1)} custom-call(bf16[1024,2048]{1,0:T(8,128)(2,1)} %bitcast.31, bf16[2048,512]{1,0:T(8,128)(2,1)} %bitcast.33, f32[2048,128]{1,0:T(8,128)} %constant.45.clone.table_ref, f32[1,128]{1,0:T(1,128)} %bitcast.36), custom_call_target="tpu_custom_call" | custom-call | flops 1073741824 | bytes 5767168 | tf_op jit(solution)/shard_map/pallas_call | solution.py:597
  86.8 2.4 %copy_bitcast_fusion.weight_ref = bf16[256,2048]{1,0:T(8,128)(2,1)} fusion(bf16[16,256,128]{2,1,0:T(8,128)(2,1)} %get-tuple-element.7), kind=kLoop, calls=%fused_computation.8 | loop fusion | bytes 2097152 | tf_op jit(solution)/shard_map/reshape | solution.py:674
  89.1 1.4 collective-permute-done.far_ref
  90.5 9.9 %shard_map.152.attended_ref = bf16[1024,256]{1,0:T(8,128)(2,1)} custom-call(bf16[1024,256]{1,0:T(8,128)(2,1)} %shard_map.150.q_ref, bf16[2,1024,128]{2,1,0:T(8,128)(2,1)} %shard_map.151.own_ref, bf16[2,1024,128]{2,1,0:T(8,128)(2,1)} %collective-permute-done.far_ref, s32[1,1]{1,0:T(1,128)} %bitcast.5.length_ref), custom_call_target="tpu_custom_call" | custom-call | flops 2147483648 | bytes 2097152 | tf_op jit(solution)/shard_map/pallas_call | solution.py:502
  100.4 0.0 copy-start.2
  100.4 44.9 %shard_map.153 = bf16[8,64,2048]{2,1,0:T(8,128)(2,1)} custom-call(bf16[1024,256]{1,0:T(8,128)(2,1)} %shard_map.152.attended_ref, bf16[256,2048]{1,0:T(8,128)(2,1)} %copy_bitcast_fusion.weight_ref), custom_call_target="tpu_custom_call" | custom-call | tf_op jit(solution)/shard_map/pallas_call | solution.py:315
  145.3 2.0 %convert_reduce_fusion = f32[64,2048]{1,0:T(8,128)S(1)} fusion(bf16[8,64,2048]{2,1,0:T(8,128)(2,1)} %shard_map.153), kind=kLoop, calls=%fused_computation.2 | loop fusion | flops 1966080 | bytes 2621440 | tf_op jit(solution)/shard_map/reduce_sum | solution.py:676
  147.4 1.1 fusion.6
  148.5 0.0 copy-start.1
  148.5 0.0 copy-done.2
  148.5 0.3 fusion.9
  148.8 0.9 copy.37.part
  149.7 12.7 %shard_map.154 = bf16[16,4,2048]{2,1,0:T(4,128)(2,1)} custom-call(bf16[16,4,2048]{2,1,0:T(4,128)(2,1)} %copy.37.part), custom_call_target="tpu_custom_call" | custom-call | tf_op jit(solution)/shard_map/pallas_call | solution.py:442
  162.4 4.1 %fusion = f32[16,4,1536]{2,0,1:T(8,128)S(1)} fusion(bf16[1,2048,1536]{2,1,0:T(8,128)(2,1)} %param.24, bf16[16,4,2048]{2,1,0:T(4,128)(2,1)} %shard_map.154), kind=kOutput, calls=%fused_computation | convolution fusion | flops 402653184 | bytes 6946816 | tf_op jit(solution)/shard_map/jcd,df->jcf/dot_general | solution.py:705
  166.6 0.0 copy-done
  166.6 0.7 fusion.2
  167.3 0.9 copy.36.part
  168.2 8.9 %shard_map.155 = bf16[16,4,2048]{2,1,0:T(4,128)(2,1)} custom-call(bf16[16,4,2048]{2,1,0:T(4,128)(2,1)} %copy.36.part), custom_call_target="tpu_custom_call" | custom-call | tf_op jit(solution)/shard_map/pallas_call | solution.py:442
  177.1 0.0 copy-done.1
  177.1 1.3 fusion.17
  178.4 0.2 select_reduce_fusion
  178.6 0.1 exponential_reduce_fusion
  178.7 0.2 select_reduce_fusion.3
  178.9 2.0 %fusion.5 = bf16[64,2048]{1,0:T(8,128)(2,1)} fusion(bf16[16,4,2048]{2,1,0:T(4,128)(2,1)} %shard_map.155, f32[64]{0:T(128)S(1)} %select_reduce_fusion.3, s32[64]{0:T(128)S(1)} %add_add_fusion, s32[16,4]{0,1:T(4,128)S(1)} %multiply_add_fusion, pred[64]{0:T(512)(128)(4,1)S(1)} %fusion.29), kind=kOutput, calls=%fused_computation.7 | convolution fusion | flops 17047552 | bytes 525120 | tf_op jit(solution)/shard_map/jct,jcd->td/dot_general | solution.py:713
  (3 shorter events, 0.0 us)
Async XLA Ops:
  0.6 166.0 %copy-start = (bf16[1,768,2048]{2,1,0:T(8,128)(2,1)S(1)}, bf16[1,768,2048]{2,1,0:T(8,128)(2,1)}, u32[]{:S(2)}) copy-start(bf16[1,768,2048]{2,1,0:T(8,128)(2,1)} %param.25) | copy-start | bytes 9437188
  72.8 6.9 %copy-start.3 = (s32[64,8]{0,1:T(8,128)S(1)}, s32[64,8]{0,1:T(8,128)}, u32[]{:S(2)}) copy-start(s32[64,8]{0,1:T(8,128)} %param.26) | copy-start | bytes 6148
  72.9 7.6 %copy-start.4 = (s32[8]{0:T(128)S(1)}, s32[8]{0:T(128)}, u32[]{:S(2)}) copy-start(s32[8]{0:T(128)} %param.22) | copy-start | bytes 100
  78.9 11.6 %collective-permute-start = (bf16[2,1024,128]{2,1,0:T(8,128)(2,1)}, bf16[2,1024,128]{2,1,0:T(8,128)(2,1)}, u32[]{:S(2)}, u32[]{:S(2)}) collective-permute-start(bf16[2,1024,128]{2,1,0:T(8,128)(2,1)} %shard_map.151.own_ref), channel_id=1, source_target_pairs={{0,16},{16,0},{32,48},{48,32},{64,80},{80,64},{96,112},{112,96},{1... | collective-permute-start | bytes 1572872 | tf_op jit(solution)/shard_map/ppermute | solution.py:30
  100.4 48.1 %copy-start.2 = (f32[2048]{0:T(1024)S(1)}, f32[2048]{0:T(1024)}, u32[]{:S(2)}) copy-start(f32[2048]{0:T(1024)} %param.16) | copy-start | bytes 24580
  148.5 28.6 %copy-start.1 = (bf16[64,2048]{1,0:T(8,128)(2,1)}, bf16[64,2048]{1,0:T(8,128)(2,1)S(1)}, u32[]{:S(2)}) copy-start(bf16[64,2048]{1,0:T(8,128)(2,1)S(1)} %get-tuple-element.9) | copy-start | bytes 786436

commit v16 on v15

--- a/solution.py
+++ b/solution.py
@@ -63,8 +63,12 @@
         pl.semaphore_signal(barrier, 1, device_id=dev, device_id_type=MESH)
     pl.semaphore_wait(barrier, len(peers))
 
+    width = oo.shape[1] // n_group
+
     def slot(k, origin):
-        return (oqkv, oo)[k].at[origin]
+        if k == 1:
+            return oo.at[:, pl.ds(pl.multiple_of(origin * width, width), width)]
+        return oqkv.at[origin]
 
     sends = []
 
@@ -170,7 +174,7 @@
     joined = (q_in.shape[0], q_in.shape[1] + 2 * depth)
     shapes = [
         jax.ShapeDtypeStruct((n_group,) + joined, jnp.bfloat16),
-        jax.ShapeDtypeStruct((n_group,) + o_in.shape, jnp.bfloat16),
+        jax.ShapeDtypeStruct((o_in.shape[0], n_group * o_in.shape[1]), jnp.bfloat16),
         jax.ShapeDtypeStruct((n_expert,) + h_in.shape, jnp.bfloat16),
     ]
     return pl.pallas_call(
@@ -671,7 +675,7 @@
         valid_length.astype(jnp.int32),
         HEAD_DIMENSION ** (-0.5),
     )
-    output_weight = jnp.transpose(output_parts, (1, 0, 2)).reshape(output_parts.shape[1], -1)
+    output_weight = output_parts
     owned = combine_and_scatter(attended, output_weight, experts_axis)
     summed = jnp.sum(owned.astype(jnp.float32), axis=0)
     hidden = (hidden_in.astype(jnp.float32) + summed).astype(jnp.bfloat16)

time: 181 us -> 181 us (level)
  waiting for transfers between devices: 1.36 us -> 3.73 us
  local copies, waits for them, and re-layouts: 4.31 us -> 1.94 us
    reshape x1 -> x0, local copies, waits for them, and re-layouts: 2.37 us -> none  [per_device(): jnp.transpose(output_parts, (1, 0, 2)).reshape(output_parts.shape[1], -1)]
    ppermute x1, waiting for transfers between devices: 1.36 us -> 3.73 us  [from_partner(): return lax.ppermute(block, axis, route)]
  transfers between devices with their start and end apart: 1 -> 1, of which waited for: 1 -> 1; matrix products, arithmetic and copies ran while one was open for 2% -> 1% of each run, Pallas kernels for 3% -> 3%
where the time goes in v16:
time: 181 us
  Pallas kernels  160 us (88%)
  matrix products  8.44 us (5%)
  other arithmetic  4.9 us (3%)
  waiting for transfers between devices  3.73 us (2%)
  local copies, waits for them, and re-layouts  1.94 us (1%)
    pallas_call x1, Pallas kernels, gather_all(): pl.pallas_call(functools.partial(gather_kernel, n_group, n_expert, q_in.s...  72.2 us
    pallas_call x1, Pallas kernels, combine_and_scatter(): pl.pallas_call(functools.partial(combine_scatter_kernel, blocks), out_sha...  45 us
    pallas_call x2, Pallas kernels, scatter_blocks(): pl.pallas_call(functools.partial(scatter_kernel, n_expert), out_shape=jax...  21.5 us
    pallas_call x2, Pallas kernels, prep(): pl.pallas_call(functools.partial(prep_kernel, query_width, for_queries),...  11.8 us
    pallas_call x1, Pallas kernels, attention(): pl.pallas_call(functools.partial(attention_kernel, scale, width // depth)...  9.9 us
    dot_general x1, matrix products, per_device(): jnp.einsum('jcd,df->jcf', slot_items, gateup_here, preferred_element_type...  4.15 us
    ppermute x1, waiting for transfers between devices, from_partner(): return lax.ppermute(block, axis, route)  3.73 us
  transfers between devices with their start and end apart: 1, of which 1 were waited for; matrix products, arithmetic and copies ran while one was open for 1% of the time, Pallas kernels for 3%

profile of v16, /device:TPU:1, one launch (start us, length us, event | category | flops | bytes accessed | tf_op | source)
XLA Modules:
  0.0 181.0 jit_solution(13879803929135808655)
XLA Ops:
  0.6 0.0 copy-start
  0.6 72.2 %shard_map.149 = (bf16[16,128,512]{2,1,0:T(8,128)(2,1)}, bf16[256,2048]{1,0:T(8,128)(2,1)}, bf16[16,64,2048]{2,1,0:T(8,128)(2,1)}) custom-call(f32[128,256]{1,0:T(8,128)} %q_in.1, f32[2,128,512]{2,1,0:T(8,128)} %kv_in.1, f32[256,128]{1,0:T(8,128)} %o_in.1, bf16[64,2048]{1,0:T(8,128)(2,1)} %h_in.1, f32[1,2048]{1,0:T(1,128)} %bitcast.28), custom_call_target="tpu_custom_call" | custom-call | tf_op jit(solution)/shard_map/pallas_call | solution.py:180
  72.8 0.0 copy-start.3
  72.9 6.1 %shard_map.151.own_ref = bf16[2,1024,128]{2,1,0:T(8,128)(2,1)} custom-call(bf16[1024,2048]{1,0:T(8,128)(2,1)} %bitcast.24, bf16[2048,512]{1,0:T(8,128)(2,1)} %bitcast.26, f32[2048,128]{1,0:T(8,128)} %constant.45.clone.table_ref, f32[1,128]{1,0:T(1,128)} %bitcast.29), custom_call_target="tpu_custom_call" | custom-call | flops 1073741824 | bytes 5767168 | tf_op jit(solution)/shard_map/pallas_call | solution.py:601
  78.9 0.8 collective-permute-start
  79.7 0.0 copy-done.3
  79.7 0.1 copy.19
  79.8 0.1 select_reduce_fusion.2
  79.9 0.1 fusion.29
  80.0 0.1 fusion.20
  80.1 0.1 reduce_window_sum.11
  80.2 0.0 copy-start.4
  80.2 5.7 %shard_map.150.q_ref = bf16[1024,256]{1,0:T(8,128)(2,1)} custom-call(bf16[1024,2048]{1,0:T(8,128)(2,1)} %bitcast.25, bf16[2048,512]{1,0:T(8,128)(2,1)} %bitcast.27, f32[2048,128]{1,0:T(8,128)} %constant.45.clone.table_ref, f32[1,128]{1,0:T(1,128)} %bitcast.30), custom_call_target="tpu_custom_call" | custom-call | flops 1073741824 | bytes 5767168 | tf_op jit(solution)/shard_map/pallas_call | solution.py:601
  86.0 0.0 copy-done.4
  86.0 0.6 fusion.27
  86.6 0.2 select_reduce_fusion.1
  86.8 3.7 %collective-permute-done.far_ref = bf16[2,1024,128]{2,1,0:T(8,128)(2,1)} collective-permute-done((bf16[2,1024,128]{2,1,0:T(8,128)(2,1)}, bf16[2,1024,128]{2,1,0:T(8,128)(2,1)}, u32[]{:S(2)}, u32[]{:S(2)}) %collective-permute-start) | collective-permute-done | bytes 524320 | tf_op jit(solution)/shard_map/ppermute | solution.py:30
  90.5 9.9 %shard_map.152.attended_ref = bf16[1024,256]{1,0:T(8,128)(2,1)} custom-call(bf16[1024,256]{1,0:T(8,128)(2,1)} %shard_map.150.q_ref, bf16[2,1024,128]{2,1,0:T(8,128)(2,1)} %shard_map.151.own_ref, bf16[2,1024,128]{2,1,0:T(8,128)(2,1)} %collective-permute-done.far_ref, s32[1,1]{1,0:T(1,128)} %bitcast.5.length_ref), custom_call_target="tpu_custom_call" | custom-call | flops 2147483648 | bytes 2097152 | tf_op jit(solution)/shard_map/pallas_call | solution.py:506
  100.4 0.0 copy-start.2
  100.4 45.0 %shard_map.153 = bf16[8,64,2048]{2,1,0:T(8,128)(2,1)} custom-call(bf16[1024,256]{1,0:T(8,128)(2,1)} %shard_map.152.attended_ref, bf16[256,2048]{1,0:T(8,128)(2,1)} %get-tuple-element.7.weight_ref), custom_call_target="tpu_custom_call" | custom-call | tf_op jit(solution)/shard_map/pallas_call | solution.py:319
  145.4 2.0 %convert_reduce_fusion = f32[64,2048]{1,0:T(8,128)S(1)} fusion(bf16[8,64,2048]{2,1,0:T(8,128)(2,1)} %shard_map.153), kind=kLoop, calls=%fused_computation.2 | loop fusion | flops 1966080 | bytes 2621440 | tf_op jit(solution)/shard_map/reduce_sum | solution.py:680
  147.4 1.1 fusion.6
  148.5 0.0 copy-start.1
  148.6 0.0 copy-done.2
  148.6 0.3 fusion.9
  148.9 0.9 copy.33.part
  149.8 12.7 %shard_map.154 = bf16[16,4,2048]{2,1,0:T(4,128)(2,1)} custom-call(bf16[16,4,2048]{2,1,0:T(4,128)(2,1)} %copy.33.part), custom_call_target="tpu_custom_call" | custom-call | tf_op jit(solution)/shard_map/pallas_call | solution.py:446
  162.5 4.1 %fusion = f32[16,4,1536]{2,0,1:T(8,128)S(1)} fusion(bf16[1,2048,1536]{2,1,0:T(8,128)(2,1)} %param.24, bf16[16,4,2048]{2,1,0:T(4,128)(2,1)} %shard_map.154), kind=kOutput, calls=%fused_computation | convolution fusion | flops 402653184 | bytes 6946816 | tf_op jit(solution)/shard_map/jcd,df->jcf/dot_general | solution.py:709
  166.6 0.0 copy-done
  166.7 0.7 fusion.2
  167.3 0.9 copy.32.part
  168.2 8.9 %shard_map.155 = bf16[16,4,2048]{2,1,0:T(4,128)(2,1)} custom-call(bf16[16,4,2048]{2,1,0:T(4,128)(2,1)} %copy.32.part), custom_call_target="tpu_custom_call" | custom-call | tf_op jit(solution)/shard_map/pallas_call | solution.py:446
  177.1 0.0 copy-done.1
  177.1 1.3 fusion.17
  178.4 0.2 select_reduce_fusion
  178.7 0.1 exponential_reduce_fusion
  178.8 0.2 select_reduce_fusion.3
  179.0 2.0 %fusion.5 = bf16[64,2048]{1,0:T(8,128)(2,1)} fusion(bf16[16,4,2048]{2,1,0:T(4,128)(2,1)} %shard_map.155, f32[64]{0:T(128)S(1)} %select_reduce_fusion.3, s32[64]{0:T(128)S(1)} %add_add_fusion, s32[16,4]{0,1:T(4,128)S(1)} %multiply_add_fusion, pred[64]{0:T(512)(128)(4,1)S(1)} %fusion.29), kind=kOutput, calls=%fused_computation.7 | convolution fusion | flops 17047552 | bytes 525120 | tf_op jit(solution)/shard_map/jct,jcd->td/dot_general | solution.py:717
  (3 shorter events, 0.0 us)
Async XLA Ops:
  0.6 166.0 %copy-start = (bf16[1,768,2048]{2,1,0:T(8,128)(2,1)S(1)}, bf16[1,768,2048]{2,1,0:T(8,128)(2,1)}, u32[]{:S(2)}) copy-start(bf16[1,768,2048]{2,1,0:T(8,128)(2,1)} %param.25) | copy-start | bytes 9437188
  72.8 6.8 %copy-start.3 = (s32[64,8]{0,1:T(8,128)S(1)}, s32[64,8]{0,1:T(8,128)}, u32[]{:S(2)}) copy-start(s32[64,8]{0,1:T(8,128)} %param.26) | copy-start | bytes 6148
  78.9 11.6 %collective-permute-start = (bf16[2,1024,128]{2,1,0:T(8,128)(2,1)}, bf16[2,1024,128]{2,1,0:T(8,128)(2,1)}, u32[]{:S(2)}, u32[]{:S(2)}) collective-permute-start(bf16[2,1024,128]{2,1,0:T(8,128)(2,1)} %shard_map.151.own_ref), channel_id=1, source_target_pairs={{0,16},{16,0},{32,48},{48,32},{64,80},{80,64},{96,112},{112,96},{1... | collective-permute-start | bytes 1572872 | tf_op jit(solution)/shard_map/ppermute | solution.py:30
  80.2 5.8 %copy-start.4 = (s32[8]{0:T(128)S(1)}, s32[8]{0:T(128)}, u32[]{:S(2)}) copy-start(s32[8]{0:T(128)} %param.22) | copy-start | bytes 100
  100.4 48.2 %copy-start.2 = (f32[2048]{0:T(1024)S(1)}, f32[2048]{0:T(1024)}, u32[]{:S(2)}) copy-start(f32[2048]{0:T(1024)} %param.16) | copy-start | bytes 24580
  148.5 28.6 %copy-start.1 = (bf16[64,2048]{1,0:T(8,128)(2,1)}, bf16[64,2048]{1,0:T(8,128)(2,1)S(1)}, u32[]{:S(2)}) copy-start(bf16[64,2048]{1,0:T(8,128)(2,1)S(1)} %get-tuple-element.9) | copy-start | bytes 786436

commit v17 on v15

--- a/solution.py
+++ b/solution.py
@@ -497,7 +497,7 @@
 def attention(queries, own_kv, far_kv, length, scale):
     rows, width = queries.shape
     key_rows, depth = own_kv.shape[1:]
-    block = min(256, rows)
+    block = min(512, rows)
     pair = pl.BlockSpec((2, key_rows, depth), lambda i: (0, 0, 0))
     return pl.pallas_call(
         functools.partial(attention_kernel, scale, width // depth),
@@ -584,7 +584,7 @@
     rows, width = normed_rows.shape
     depth = table.shape[1]
     query_width = joined.shape[1] - 2 * depth
-    block = min(256, rows)
+    block = min(512, rows)
     whole = lambda shape: pl.BlockSpec(shape, lambda i: (0, 0))
     if for_queries:
         out_shape = jax.ShapeDtypeStruct((rows, query_width), jnp.bfloat16)

time: 181 us -> 180 us (level)
  no operation moved by 1% of the time
where the time goes in v17:
time: 180 us
  Pallas kernels  160 us (89%)
  matrix products  8.45 us (5%)
  other arithmetic  4.9 us (3%)
  local copies, waits for them, and re-layouts  4.31 us (2%)
    pallas_call x1, Pallas kernels, gather_all(): pl.pallas_call(functools.partial(gather_kernel, n_group, n_expert, q_in.s...  72.2 us
    pallas_call x1, Pallas kernels, combine_and_scatter(): pl.pallas_call(functools.partial(combine_scatter_kernel, blocks), out_sha...  44.9 us
    pallas_call x2, Pallas kernels, scatter_blocks(): pl.pallas_call(functools.partial(scatter_kernel, n_expert), out_shape=jax...  21.5 us
    pallas_call x2, Pallas kernels, prep(): pl.pallas_call(functools.partial(prep_kernel, query_width, for_queries),...  12.1 us
    pallas_call x1, Pallas kernels, attention(): pl.pallas_call(functools.partial(attention_kernel, scale, width // depth)...  8.83 us
    dot_general x1, matrix products, per_device(): jnp.einsum('jcd,df->jcf', slot_items, gateup_here, preferred_element_type...  4.16 us
  transfers between devices with their start and end apart: 1, of which 1 were waited for; matrix products, arithmetic and copies ran while one was open for 2% of the time, Pallas kernels for 3%

profile of v17, /device:TPU:1, one launch (start us, length us, event | category | flops | bytes accessed | tf_op | source)
XLA Modules:
  0.0 180.1 jit_solution(14985015822936147086)
XLA Ops:
  0.6 0.0 copy-start
  0.6 72.2 %shard_map.149 = (bf16[16,128,512]{2,1,0:T(8,128)(2,1)}, bf16[16,256,128]{2,1,0:T(8,128)(2,1)}, bf16[16,64,2048]{2,1,0:T(8,128)(2,1)}) custom-call(f32[128,256]{1,0:T(8,128)} %q_in.1, f32[2,128,512]{2,1,0:T(8,128)} %kv_in.1, f32[256,128]{1,0:T(8,128)} %o_in.1, bf16[64,2048]{1,0:T(8,128)(2,1)} %h_in.1, f32[1,2048]{1,0:T(1,128)} %bitcast.34), custom_call_target="tpu_custom_call" | custom-call | tf_op jit(solution)/shard_map/pallas_call | solution.py:176
  72.8 0.0 copy-start.3
  72.9 0.0 copy-start.4
  72.9 6.3 %shard_map.151.own_ref = bf16[2,1024,128]{2,1,0:T(8,128)(2,1)} custom-call(bf16[1024,2048]{1,0:T(8,128)(2,1)} %bitcast.30, bf16[2048,512]{1,0:T(8,128)(2,1)} %bitcast.32, f32[2048,128]{1,0:T(8,128)} %constant.45.clone.table_ref, f32[1,128]{1,0:T(1,128)} %bitcast.35), custom_call_target="tpu_custom_call" | custom-call | flops 1073741824 | bytes 5767168 | tf_op jit(solution)/shard_map/pallas_call | solution.py:597
  79.1 0.8 collective-permute-start
  79.9 0.0 copy-done.3
  79.9 0.1 copy.21
  80.0 0.1 select_reduce_fusion.2
  80.1 0.1 fusion.29
  80.2 0.1 fusion.20
  80.3 0.1 reduce_window_sum.11
  80.4 0.2 select_reduce_fusion.1
  80.6 0.0 copy-done.4
  80.6 0.6 fusion.27
  81.3 5.8 %shard_map.150.q_ref = bf16[1024,256]{1,0:T(8,128)(2,1)} custom-call(bf16[1024,2048]{1,0:T(8,128)(2,1)} %bitcast.31, bf16[2048,512]{1,0:T(8,128)(2,1)} %bitcast.33, f32[2048,128]{1,0:T(8,128)} %constant.45.clone.table_ref, f32[1,128]{1,0:T(1,128)} %bitcast.36), custom_call_target="tpu_custom_call" | custom-call | flops 1073741824 | bytes 5767168 | tf_op jit(solution)/shard_map/pallas_call | solution.py:597
  87.1 2.4 %copy_bitcast_fusion.weight_ref = bf16[256,2048]{1,0:T(8,128)(2,1)} fusion(bf16[16,256,128]{2,1,0:T(8,128)(2,1)} %get-tuple-element.7), kind=kLoop, calls=%fused_computation.8 | loop fusion | bytes 2097152 | tf_op jit(solution)/shard_map/reshape | solution.py:674
  89.5 1.2 collective-permute-done.far_ref
  90.7 8.8 %shard_map.152.attended_ref = bf16[1024,256]{1,0:T(8,128)(2,1)} custom-call(bf16[1024,256]{1,0:T(8,128)(2,1)} %shard_map.150.q_ref, bf16[2,1024,128]{2,1,0:T(8,128)(2,1)} %shard_map.151.own_ref, bf16[2,1024,128]{2,1,0:T(8,128)(2,1)} %collective-permute-done.far_ref, s32[1,1]{1,0:T(1,128)} %bitcast.5.length_ref), custom_call_target="tpu_custom_call" | custom-call | flops 2147483648 | bytes 2097152 | tf_op jit(solution)/shard_map/pallas_call | solution.py:502
  99.5 0.0 copy-start.2
  99.5 44.9 %shard_map.153 = bf16[8,64,2048]{2,1,0:T(8,128)(2,1)} custom-call(bf16[1024,256]{1,0:T(8,128)(2,1)} %shard_map.152.attended_ref, bf16[256,2048]{1,0:T(8,128)(2,1)} %copy_bitcast_fusion.weight_ref), custom_call_target="tpu_custom_call" | custom-call | tf_op jit(solution)/shard_map/pallas_call | solution.py:315
  144.5 2.0 %convert_reduce_fusion = f32[64,2048]{1,0:T(8,128)S(1)} fusion(bf16[8,64,2048]{2,1,0:T(8,128)(2,1)} %shard_map.153), kind=kLoop, calls=%fused_computation.2 | loop fusion | flops 1966080 | bytes 2621440 | tf_op jit(solution)/shard_map/reduce_sum | solution.py:676
  146.5 1.1 fusion.6
  147.7 0.0 copy-start.1
  147.7 0.0 copy-done.2
  147.7 0.3 fusion.9
  148.0 0.9 copy.37.part
  148.9 12.7 %shard_map.154 = bf16[16,4,2048]{2,1,0:T(4,128)(2,1)} custom-call(bf16[16,4,2048]{2,1,0:T(4,128)(2,1)} %copy.37.part), custom_call_target="tpu_custom_call" | custom-call | tf_op jit(solution)/shard_map/pallas_call | solution.py:442
  161.6 4.2 %fusion = f32[16,4,1536]{2,0,1:T(8,128)S(1)} fusion(bf16[1,2048,1536]{2,1,0:T(8,128)(2,1)} %param.24, bf16[16,4,2048]{2,1,0:T(4,128)(2,1)} %shard_map.154), kind=kOutput, calls=%fused_computation | convolution fusion | flops 402653184 | bytes 6946816 | tf_op jit(solution)/shard_map/jcd,df->jcf/dot_general | solution.py:705
  165.8 0.0 copy-done
  165.8 0.7 fusion.2
  166.4 0.9 copy.36.part
  167.4 8.8 %shard_map.155 = bf16[16,4,2048]{2,1,0:T(4,128)(2,1)} custom-call(bf16[16,4,2048]{2,1,0:T(4,128)(2,1)} %copy.36.part), custom_call_target="tpu_custom_call" | custom-call | tf_op jit(solution)/shard_map/pallas_call | solution.py:442
  176.2 0.0 copy-done.1
  176.2 1.3 fusion.17
  177.5 0.2 select_reduce_fusion
  177.8 0.1 exponential_reduce_fusion
  177.9 0.2 select_reduce_fusion.3
  178.1 2.0 %fusion.5 = bf16[64,2048]{1,0:T(8,128)(2,1)} fusion(bf16[16,4,2048]{2,1,0:T(4,128)(2,1)} %shard_map.155, f32[64]{0:T(128)S(1)} %select_reduce_fusion.3, s32[64]{0:T(128)S(1)} %add_add_fusion, s32[16,4]{0,1:T(4,128)S(1)} %multiply_add_fusion, pred[64]{0:T(512)(128)(4,1)S(1)} %fusion.29), kind=kOutput, calls=%fused_computation.7 | convolution fusion | flops 17047552 | bytes 525120 | tf_op jit(solution)/shard_map/jct,jcd->td/dot_general | solution.py:713
  (3 shorter events, 0.0 us)
Async XLA Ops:
  0.6 165.1 %copy-start = (bf16[1,768,2048]{2,1,0:T(8,128)(2,1)S(1)}, bf16[1,768,2048]{2,1,0:T(8,128)(2,1)}, u32[]{:S(2)}) copy-start(bf16[1,768,2048]{2,1,0:T(8,128)(2,1)} %param.25) | copy-start | bytes 9437188
  72.8 7.1 %copy-start.3 = (s32[64,8]{0,1:T(8,128)S(1)}, s32[64,8]{0,1:T(8,128)}, u32[]{:S(2)}) copy-start(s32[64,8]{0,1:T(8,128)} %param.26) | copy-start | bytes 6148
  72.9 7.8 %copy-start.4 = (s32[8]{0:T(128)S(1)}, s32[8]{0:T(128)}, u32[]{:S(2)}) copy-start(s32[8]{0:T(128)} %param.22) | copy-start | bytes 100
  79.1 11.6 %collective-permute-start = (bf16[2,1024,128]{2,1,0:T(8,128)(2,1)}, bf16[2,1024,128]{2,1,0:T(8,128)(2,1)}, u32[]{:S(2)}, u32[]{:S(2)}) collective-permute-start(bf16[2,1024,128]{2,1,0:T(8,128)(2,1)} %shard_map.151.own_ref), channel_id=1, source_target_pairs={{0,16},{16,0},{32,48},{48,32},{64,80},{80,64},{96,112},{112,96},{1... | collective-permute-start | bytes 1572872 | tf_op jit(solution)/shard_map/ppermute | solution.py:30
  99.5 48.1 %copy-start.2 = (f32[2048]{0:T(1024)S(1)}, f32[2048]{0:T(1024)}, u32[]{:S(2)}) copy-start(f32[2048]{0:T(1024)} %param.16) | copy-start | bytes 24580
  147.7 28.6 %copy-start.1 = (bf16[64,2048]{1,0:T(8,128)(2,1)}, bf16[64,2048]{1,0:T(8,128)(2,1)S(1)}, u32[]{:S(2)}) copy-start(bf16[64,2048]{1,0:T(8,128)(2,1)S(1)} %get-tuple-element.9) | copy-start | bytes 786436

commit v18 on v17

--- a/solution.py
+++ b/solution.py
@@ -124,12 +124,12 @@
     own += [pltpu.make_async_copy(inputs[k], slot(k, g), local.at[k]) for k in range(2)]
     for copy in own:
         copy.start()
+    for dev in (pair_dev, plus_dev, minus_dev):
+        for k in range(2):
+            push(k, g, inputs[k], dev)
     xpush(xn, e, mate_dev)
     for dev in chip_devs:
         xpush(xn, e, dev)
-    for dev in (pair_dev, plus_dev, minus_dev):
-        for k in range(2):
-            push(k, g, inputs[k], dev)
     partner = g + 1 - 2 * xh
     arrive(partner)
     forward(partner, plus_dev)

time: 180 us -> 165 us (0.917)
  Pallas kernels: 160 us -> 144 us
    pallas_call x1, Pallas kernels: 72.2 us -> 47 us  [gather_all(): pl.pallas_call(functools.partial(gather_kernel, n_group, n_expert, q_in.s...]
    pallas_call x1, Pallas kernels: 44.9 us -> 54.2 us  [combine_and_scatter(): pl.pallas_call(functools.partial(combine_scatter_kernel, blocks), out_sha...]
  transfers between devices with their start and end apart: 1 -> 1, of which waited for: 1 -> 1; matrix products, arithmetic and copies ran while one was open for 2% -> 2% of each run, Pallas kernels for 3% -> 4%
where the time goes in v18:
time: 165 us
  Pallas kernels  144 us (87%)
  matrix products  8.45 us (5%)
  other arithmetic  4.9 us (3%)
  local copies, waits for them, and re-layouts  4.31 us (3%)
  starting transfers between devices  1.89 us (1%)
    pallas_call x1, Pallas kernels, combine_and_scatter(): pl.pallas_call(functools.partial(combine_scatter_kernel, blocks), out_sha...  54.2 us
    pallas_call x1, Pallas kernels, gather_all(): pl.pallas_call(functools.partial(gather_kernel, n_group, n_expert, q_in.s...  47 us
    pallas_call x2, Pallas kernels, scatter_blocks(): pl.pallas_call(functools.partial(scatter_kernel, n_expert), out_shape=jax...  21.8 us
    pallas_call x2, Pallas kernels, prep(): pl.pallas_call(functools.partial(prep_kernel, query_width, for_queries),...  12.1 us
    pallas_call x1, Pallas kernels, attention(): pl.pallas_call(functools.partial(attention_kernel, scale, width // depth)...  8.83 us
    dot_general x1, matrix products, per_device(): jnp.einsum('jcd,df->jcf', slot_items, gateup_here, preferred_element_type...  4.15 us
  transfers between devices with their start and end apart: 1, of which 1 were waited for; matrix products, arithmetic and copies ran while one was open for 2% of the time, Pallas kernels for 4%

profile of v18, /device:TPU:1, one launch (start us, length us, event | category | flops | bytes accessed | tf_op | source)
XLA Modules:
  0.0 165.0 jit_solution(14563443897680421922)
XLA Ops:
  0.6 0.0 copy-start
  0.6 47.0 %shard_map.149 = (bf16[16,128,512]{2,1,0:T(8,128)(2,1)}, bf16[16,256,128]{2,1,0:T(8,128)(2,1)}, bf16[16,64,2048]{2,1,0:T(8,128)(2,1)}) custom-call(f32[128,256]{1,0:T(8,128)} %q_in.1, f32[2,128,512]{2,1,0:T(8,128)} %kv_in.1, f32[256,128]{1,0:T(8,128)} %o_in.1, bf16[64,2048]{1,0:T(8,128)(2,1)} %h_in.1, f32[1,2048]{1,0:T(1,128)} %bitcast.34), custom_call_target="tpu_custom_call" | custom-call | tf_op jit(solution)/shard_map/pallas_call | solution.py:176
  47.7 0.0 copy-start.3
  47.7 0.0 copy-start.4
  47.7 6.3 %shard_map.151.own_ref = bf16[2,1024,128]{2,1,0:T(8,128)(2,1)} custom-call(bf16[1024,2048]{1,0:T(8,128)(2,1)} %bitcast.30, bf16[2048,512]{1,0:T(8,128)(2,1)} %bitcast.32, f32[2048,128]{1,0:T(8,128)} %constant.45.clone.table_ref, f32[1,128]{1,0:T(1,128)} %bitcast.35), custom_call_target="tpu_custom_call" | custom-call | flops 1073741824 | bytes 5767168 | tf_op jit(solution)/shard_map/pallas_call | solution.py:597
  53.9 1.9 %collective-permute-start = (bf16[2,1024,128]{2,1,0:T(8,128)(2,1)}, bf16[2,1024,128]{2,1,0:T(8,128)(2,1)}, u32[]{:S(2)}, u32[]{:S(2)}) collective-permute-start(bf16[2,1024,128]{2,1,0:T(8,128)(2,1)} %shard_map.151.own_ref), channel_id=1, source_target_pairs={{0,16},{16,0},{32,48},{48,32},{64,80},{80,64},{96,112},{112,96},{1... | collective-permute-start | bytes 1572872 | tf_op jit(solution)/shard_map/ppermute | solution.py:30
  55.8 0.0 copy-done.3
  55.8 0.1 copy.21
  55.9 0.1 select_reduce_fusion.2
  56.0 0.1 fusion.29
  56.2 0.1 fusion.20
  56.3 0.1 reduce_window_sum.11
  56.3 0.2 select_reduce_fusion.1
  56.5 0.0 copy-done.4
  56.6 0.6 fusion.27
  57.2 5.8 %shard_map.150.q_ref = bf16[1024,256]{1,0:T(8,128)(2,1)} custom-call(bf16[1024,2048]{1,0:T(8,128)(2,1)} %bitcast.31, bf16[2048,512]{1,0:T(8,128)(2,1)} %bitcast.33, f32[2048,128]{1,0:T(8,128)} %constant.45.clone.table_ref, f32[1,128]{1,0:T(1,128)} %bitcast.36), custom_call_target="tpu_custom_call" | custom-call | flops 1073741824 | bytes 5767168 | tf_op jit(solution)/shard_map/pallas_call | solution.py:597
  63.0 2.4 %copy_bitcast_fusion.weight_ref = bf16[256,2048]{1,0:T(8,128)(2,1)} fusion(bf16[16,256,128]{2,1,0:T(8,128)(2,1)} %get-tuple-element.7), kind=kLoop, calls=%fused_computation.8 | loop fusion | bytes 2097152 | tf_op jit(solution)/shard_map/reshape | solution.py:674
  65.4 0.7 collective-permute-done.far_ref
  66.1 8.8 %shard_map.152.attended_ref = bf16[1024,256]{1,0:T(8,128)(2,1)} custom-call(bf16[1024,256]{1,0:T(8,128)(2,1)} %shard_map.150.q_ref, bf16[2,1024,128]{2,1,0:T(8,128)(2,1)} %shard_map.151.own_ref, bf16[2,1024,128]{2,1,0:T(8,128)(2,1)} %collective-permute-done.far_ref, s32[1,1]{1,0:T(1,128)} %bitcast.5.length_ref), custom_call_target="tpu_custom_call" | custom-call | flops 2147483648 | bytes 2097152 | tf_op jit(solution)/shard_map/pallas_call | solution.py:502
  74.9 0.0 copy-start.2
  74.9 54.2 %shard_map.153 = bf16[8,64,2048]{2,1,0:T(8,128)(2,1)} custom-call(bf16[1024,256]{1,0:T(8,128)(2,1)} %shard_map.152.attended_ref, bf16[256,2048]{1,0:T(8,128)(2,1)} %copy_bitcast_fusion.weight_ref), custom_call_target="tpu_custom_call" | custom-call | tf_op jit(solution)/shard_map/pallas_call | solution.py:315
  129.1 2.0 %convert_reduce_fusion = f32[64,2048]{1,0:T(8,128)S(1)} fusion(bf16[8,64,2048]{2,1,0:T(8,128)(2,1)} %shard_map.153), kind=kLoop, calls=%fused_computation.2 | loop fusion | flops 1966080 | bytes 2621440 | tf_op jit(solution)/shard_map/reduce_sum | solution.py:676
  131.1 1.1 fusion.6
  132.2 0.0 copy-start.1
  132.3 0.0 copy-done.2
  132.3 0.3 fusion.9
  132.6 0.9 copy.37.part
  133.5 13.0 %shard_map.154 = bf16[16,4,2048]{2,1,0:T(4,128)(2,1)} custom-call(bf16[16,4,2048]{2,1,0:T(4,128)(2,1)} %copy.37.part), custom_call_target="tpu_custom_call" | custom-call | tf_op jit(solution)/shard_map/pallas_call | solution.py:442
  146.5 4.2 %fusion = f32[16,4,1536]{2,0,1:T(8,128)S(1)} fusion(bf16[1,2048,1536]{2,1,0:T(8,128)(2,1)} %param.24, bf16[16,4,2048]{2,1,0:T(4,128)(2,1)} %shard_map.154), kind=kOutput, calls=%fused_computation | convolution fusion | flops 402653184 | bytes 6946816 | tf_op jit(solution)/shard_map/jcd,df->jcf/dot_general | solution.py:705
  150.7 0.0 copy-done
  150.7 0.7 fusion.2
  151.4 0.9 copy.36.part
  152.3 8.8 %shard_map.155 = bf16[16,4,2048]{2,1,0:T(4,128)(2,1)} custom-call(bf16[16,4,2048]{2,1,0:T(4,128)(2,1)} %copy.36.part), custom_call_target="tpu_custom_call" | custom-call | tf_op jit(solution)/shard_map/pallas_call | solution.py:442
  161.1 0.0 copy-done.1
  161.1 1.3 fusion.17
  162.4 0.2 select_reduce_fusion
  162.7 0.1 exponential_reduce_fusion
  162.8 0.2 select_reduce_fusion.3
  163.0 2.0 %fusion.5 = bf16[64,2048]{1,0:T(8,128)(2,1)} fusion(bf16[16,4,2048]{2,1,0:T(4,128)(2,1)} %shard_map.155, f32[64]{0:T(128)S(1)} %select_reduce_fusion.3, s32[64]{0:T(128)S(1)} %add_add_fusion, s32[16,4]{0,1:T(4,128)S(1)} %multiply_add_fusion, pred[64]{0:T(512)(128)(4,1)S(1)} %fusion.29), kind=kOutput, calls=%fused_computation.7 | convolution fusion | flops 17047552 | bytes 525120 | tf_op jit(solution)/shard_map/jct,jcd->td/dot_general | solution.py:713
  (3 shorter events, 0.0 us)
Async XLA Ops:
  0.6 150.0 %copy-start = (bf16[1,768,2048]{2,1,0:T(8,128)(2,1)S(1)}, bf16[1,768,2048]{2,1,0:T(8,128)(2,1)}, u32[]{:S(2)}) copy-start(bf16[1,768,2048]{2,1,0:T(8,128)(2,1)} %param.25) | copy-start | bytes 9437188
  47.7 8.2 %copy-start.3 = (s32[64,8]{0,1:T(8,128)S(1)}, s32[64,8]{0,1:T(8,128)}, u32[]{:S(2)}) copy-start(s32[64,8]{0,1:T(8,128)} %param.26) | copy-start | bytes 6148
  47.7 8.9 %copy-start.4 = (s32[8]{0:T(128)S(1)}, s32[8]{0:T(128)}, u32[]{:S(2)}) copy-start(s32[8]{0:T(128)} %param.22) | copy-start | bytes 100
  53.9 12.1 %collective-permute-start = (bf16[2,1024,128]{2,1,0:T(8,128)(2,1)}, bf16[2,1024,128]{2,1,0:T(8,128)(2,1)}, u32[]{:S(2)}, u32[]{:S(2)}) collective-permute-start(bf16[2,1024,128]{2,1,0:T(8,128)(2,1)} %shard_map.151.own_ref), channel_id=1, source_target_pairs={{0,16},{16,0},{32,48},{48,32},{64,80},{80,64},{96,112},{112,96},{1... | collective-permute-start | bytes 1572872 | tf_op jit(solution)/shard_map/ppermute | solution.py:30
  74.9 57.4 %copy-start.2 = (f32[2048]{0:T(1024)S(1)}, f32[2048]{0:T(1024)}, u32[]{:S(2)}) copy-start(f32[2048]{0:T(1024)} %param.16) | copy-start | bytes 24580
  132.2 28.9 %copy-start.1 = (bf16[64,2048]{1,0:T(8,128)(2,1)}, bf16[64,2048]{1,0:T(8,128)(2,1)S(1)}, u32[]{:S(2)}) copy-start(bf16[64,2048]{1,0:T(8,128)(2,1)S(1)} %get-tuple-element.9) | copy-start | bytes 786436

commit v19 on v18

--- a/solution.py
+++ b/solution.py
@@ -127,13 +127,13 @@
     for dev in (pair_dev, plus_dev, minus_dev):
         for k in range(2):
             push(k, g, inputs[k], dev)
-    xpush(xn, e, mate_dev)
-    for dev in chip_devs:
-        xpush(xn, e, dev)
     partner = g + 1 - 2 * xh
     arrive(partner)
     forward(partner, plus_dev)
     forward(partner, minus_dev)
+    xpush(xn, e, mate_dev)
+    for dev in chip_devs:
+        xpush(xn, e, dev)
     chip_origins = [2 * lax.rem(chip + j, chips) + core for j in range(1, chips)]
     normed_order = [chip_origins[0:2], chip_origins[2:5], chip_origins[5:]]
     for step in range(1, 4):

time: 165 us -> 166 us (level)
  waiting for transfers between devices: 0.65 us -> 3.95 us
  starting transfers between devices: 1.89 us -> 0.01 us
    pallas_call x1, Pallas kernels: 54.2 us -> 47.4 us  [combine_and_scatter(): pl.pallas_call(functools.partial(combine_scatter_kernel, blocks), out_sha...]
    pallas_call x1, Pallas kernels: 47 us -> 53.3 us  [gather_all(): pl.pallas_call(functools.partial(gather_kernel, n_group, n_expert, q_in.s...]
    ppermute x1, waiting for transfers between devices: 0.65 us -> 3.95 us  [from_partner(): return lax.ppermute(block, axis, route)]
    ppermute x1, starting transfers between devices: 1.89 us -> 0.01 us  [from_partner(): return lax.ppermute(block, axis, route)]
where the time goes in v19:
time: 166 us
  Pallas kernels  143 us (86%)
  matrix products  8.45 us (5%)
  other arithmetic  4.9 us (3%)
  local copies, waits for them, and re-layouts  4.31 us (3%)
  waiting for transfers between devices  3.95 us (2%)
    pallas_call x1, Pallas kernels, gather_all(): pl.pallas_call(functools.partial(gather_kernel, n_group, n_expert, q_in.s...  53.3 us
    pallas_call x1, Pallas kernels, combine_and_scatter(): pl.pallas_call(functools.partial(combine_scatter_kernel, blocks), out_sha...  47.4 us
    pallas_call x2, Pallas kernels, scatter_blocks(): pl.pallas_call(functools.partial(scatter_kernel, n_expert), out_shape=jax...  21.9 us
    pallas_call x2, Pallas kernels, prep(): pl.pallas_call(functools.partial(prep_kernel, query_width, for_queries),...  12.1 us
    pallas_call x1, Pallas kernels, attention(): pl.pallas_call(functools.partial(attention_kernel, scale, width // depth)...  8.83 us
    dot_general x1, matrix products, per_device(): jnp.einsum('jcd,df->jcf', slot_items, gateup_here, preferred_element_type...  4.15 us
    ppermute x1, waiting for transfers between devices, from_partner(): return lax.ppermute(block, axis, route)  3.95 us
  transfers between devices with their start and end apart: 1, of which 1 were waited for; matrix products, arithmetic and copies ran while one was open for 2% of the time, Pallas kernels for 4%

profile of v19, /device:TPU:1, one launch (start us, length us, event | category | flops | bytes accessed | tf_op | source)
XLA Modules:
  0.0 165.9 jit_solution(18382368380544074848)
XLA Ops:
  0.6 0.0 copy-start
  0.6 53.3 %shard_map.149 = (bf16[16,128,512]{2,1,0:T(8,128)(2,1)}, bf16[16,256,128]{2,1,0:T(8,128)(2,1)}, bf16[16,64,2048]{2,1,0:T(8,128)(2,1)}) custom-call(f32[128,256]{1,0:T(8,128)} %q_in.1, f32[2,128,512]{2,1,0:T(8,128)} %kv_in.1, f32[256,128]{1,0:T(8,128)} %o_in.1, bf16[64,2048]{1,0:T(8,128)(2,1)} %h_in.1, f32[1,2048]{1,0:T(1,128)} %bitcast.34), custom_call_target="tpu_custom_call" | custom-call | tf_op jit(solution)/shard_map/pallas_call | solution.py:176
  53.9 0.0 copy-start.3
  53.9 0.0 copy-start.4
  54.0 6.3 %shard_map.151.own_ref = bf16[2,1024,128]{2,1,0:T(8,128)(2,1)} custom-call(bf16[1024,2048]{1,0:T(8,128)(2,1)} %bitcast.30, bf16[2048,512]{1,0:T(8,128)(2,1)} %bitcast.32, f32[2048,128]{1,0:T(8,128)} %constant.45.clone.table_ref, f32[1,128]{1,0:T(1,128)} %bitcast.35), custom_call_target="tpu_custom_call" | custom-call | flops 1073741824 | bytes 5767168 | tf_op jit(solution)/shard_map/pallas_call | solution.py:597
  60.2 0.0 collective-permute-start
  60.2 0.0 copy-done.3
  60.2 0.1 copy.21
  60.3 0.1 select_reduce_fusion.2
  60.4 0.1 fusion.29
  60.5 0.1 fusion.20
  60.6 0.1 reduce_window_sum.11
  60.7 0.2 select_reduce_fusion.1
  60.9 0.0 copy-done.4
  60.9 0.6 fusion.27
  61.6 5.8 %shard_map.150.q_ref = bf16[1024,256]{1,0:T(8,128)(2,1)} custom-call(bf16[1024,2048]{1,0:T(8,128)(2,1)} %bitcast.31, bf16[2048,512]{1,0:T(8,128)(2,1)} %bitcast.33, f32[2048,128]{1,0:T(8,128)} %constant.45.clone.table_ref, f32[1,128]{1,0:T(1,128)} %bitcast.36), custom_call_target="tpu_custom_call" | custom-call | flops 1073741824 | bytes 5767168 | tf_op jit(solution)/shard_map/pallas_call | solution.py:597
  67.4 2.4 %copy_bitcast_fusion.weight_ref = bf16[256,2048]{1,0:T(8,128)(2,1)} fusion(bf16[16,256,128]{2,1,0:T(8,128)(2,1)} %get-tuple-element.7), kind=kLoop, calls=%fused_computation.8 | loop fusion | bytes 2097152 | tf_op jit(solution)/shard_map/reshape | solution.py:674
  69.8 3.9 %collective-permute-done.far_ref = bf16[2,1024,128]{2,1,0:T(8,128)(2,1)} collective-permute-done((bf16[2,1024,128]{2,1,0:T(8,128)(2,1)}, bf16[2,1024,128]{2,1,0:T(8,128)(2,1)}, u32[]{:S(2)}, u32[]{:S(2)}) %collective-permute-start) | collective-permute-done | bytes 524320 | tf_op jit(solution)/shard_map/ppermute | solution.py:30
  73.7 8.8 %shard_map.152.attended_ref = bf16[1024,256]{1,0:T(8,128)(2,1)} custom-call(bf16[1024,256]{1,0:T(8,128)(2,1)} %shard_map.150.q_ref, bf16[2,1024,128]{2,1,0:T(8,128)(2,1)} %shard_map.151.own_ref, bf16[2,1024,128]{2,1,0:T(8,128)(2,1)} %collective-permute-done.far_ref, s32[1,1]{1,0:T(1,128)} %bitcast.5.length_ref), custom_call_target="tpu_custom_call" | custom-call | flops 2147483648 | bytes 2097152 | tf_op jit(solution)/shard_map/pallas_call | solution.py:502
  82.6 0.0 copy-start.2
  82.6 47.4 %shard_map.153 = bf16[8,64,2048]{2,1,0:T(8,128)(2,1)} custom-call(bf16[1024,256]{1,0:T(8,128)(2,1)} %shard_map.152.attended_ref, bf16[256,2048]{1,0:T(8,128)(2,1)} %copy_bitcast_fusion.weight_ref), custom_call_target="tpu_custom_call" | custom-call | tf_op jit(solution)/shard_map/pallas_call | solution.py:315
  129.9 2.0 %convert_reduce_fusion = f32[64,2048]{1,0:T(8,128)S(1)} fusion(bf16[8,64,2048]{2,1,0:T(8,128)(2,1)} %shard_map.153), kind=kLoop, calls=%fused_computation.2 | loop fusion | flops 1966080 | bytes 2621440 | tf_op jit(solution)/shard_map/reduce_sum | solution.py:676
  132.0 1.1 fusion.6
  133.1 0.0 copy-start.1
  133.1 0.0 copy-done.2
  133.1 0.3 fusion.9
  133.4 0.9 copy.37.part
  134.3 13.0 %shard_map.154 = bf16[16,4,2048]{2,1,0:T(4,128)(2,1)} custom-call(bf16[16,4,2048]{2,1,0:T(4,128)(2,1)} %copy.37.part), custom_call_target="tpu_custom_call" | custom-call | tf_op jit(solution)/shard_map/pallas_call | solution.py:442
  147.4 4.2 %fusion = f32[16,4,1536]{2,0,1:T(8,128)S(1)} fusion(bf16[1,2048,1536]{2,1,0:T(8,128)(2,1)} %param.24, bf16[16,4,2048]{2,1,0:T(4,128)(2,1)} %shard_map.154), kind=kOutput, calls=%fused_computation | convolution fusion | flops 402653184 | bytes 6946816 | tf_op jit(solution)/shard_map/jcd,df->jcf/dot_general | solution.py:705
  151.5 0.0 copy-done
  151.6 0.7 fusion.2
  152.2 0.9 copy.36.part
  153.1 8.8 %shard_map.155 = bf16[16,4,2048]{2,1,0:T(4,128)(2,1)} custom-call(bf16[16,4,2048]{2,1,0:T(4,128)(2,1)} %copy.36.part), custom_call_target="tpu_custom_call" | custom-call | tf_op jit(solution)/shard_map/pallas_call | solution.py:442
  162.0 0.0 copy-done.1
  162.0 1.3 fusion.17
  163.3 0.2 select_reduce_fusion
  163.6 0.1 exponential_reduce_fusion
  163.7 0.2 select_reduce_fusion.3
  163.9 2.0 %fusion.5 = bf16[64,2048]{1,0:T(8,128)(2,1)} fusion(bf16[16,4,2048]{2,1,0:T(4,128)(2,1)} %shard_map.155, f32[64]{0:T(128)S(1)} %select_reduce_fusion.3, s32[64]{0:T(128)S(1)} %add_add_fusion, s32[16,4]{0,1:T(4,128)S(1)} %multiply_add_fusion, pred[64]{0:T(512)(128)(4,1)S(1)} %fusion.29), kind=kOutput, calls=%fused_computation.7 | convolution fusion | flops 17047552 | bytes 525120 | tf_op jit(solution)/shard_map/jct,jcd->td/dot_general | solution.py:713
  (3 shorter events, 0.0 us)
Async XLA Ops:
  0.6 150.9 %copy-start = (bf16[1,768,2048]{2,1,0:T(8,128)(2,1)S(1)}, bf16[1,768,2048]{2,1,0:T(8,128)(2,1)}, u32[]{:S(2)}) copy-start(bf16[1,768,2048]{2,1,0:T(8,128)(2,1)} %param.25) | copy-start | bytes 9437188
  53.9 6.3 %copy-start.3 = (s32[64,8]{0,1:T(8,128)S(1)}, s32[64,8]{0,1:T(8,128)}, u32[]{:S(2)}) copy-start(s32[64,8]{0,1:T(8,128)} %param.26) | copy-start | bytes 6148
  53.9 7.0 %copy-start.4 = (s32[8]{0:T(128)S(1)}, s32[8]{0:T(128)}, u32[]{:S(2)}) copy-start(s32[8]{0:T(128)} %param.22) | copy-start | bytes 100
  60.2 13.5 %collective-permute-start = (bf16[2,1024,128]{2,1,0:T(8,128)(2,1)}, bf16[2,1024,128]{2,1,0:T(8,128)(2,1)}, u32[]{:S(2)}, u32[]{:S(2)}) collective-permute-start(bf16[2,1024,128]{2,1,0:T(8,128)(2,1)} %shard_map.151.own_ref), channel_id=1, source_target_pairs={{0,16},{16,0},{32,48},{48,32},{64,80},{80,64},{96,112},{112,96},{1... | collective-permute-start | bytes 1572872 | tf_op jit(solution)/shard_map/ppermute | solution.py:30
  82.6 50.6 %copy-start.2 = (f32[2048]{0:T(1024)S(1)}, f32[2048]{0:T(1024)}, u32[]{:S(2)}) copy-start(f32[2048]{0:T(1024)} %param.16) | copy-start | bytes 24580
  133.1 28.9 %copy-start.1 = (bf16[64,2048]{1,0:T(8,128)(2,1)}, bf16[64,2048]{1,0:T(8,128)(2,1)S(1)}, u32[]{:S(2)}) copy-start(bf16[64,2048]{1,0:T(8,128)(2,1)S(1)} %get-tuple-element.9) | copy-start | bytes 786436

commit v20 on v18

--- a/solution.py
+++ b/solution.py
@@ -497,7 +497,7 @@
 def attention(queries, own_kv, far_kv, length, scale):
     rows, width = queries.shape
     key_rows, depth = own_kv.shape[1:]
-    block = min(512, rows)
+    block = rows
     pair = pl.BlockSpec((2, key_rows, depth), lambda i: (0, 0, 0))
     return pl.pallas_call(
         functools.partial(attention_kernel, scale, width // depth),

time: 165 us -> 165 us (level)
  no operation moved by 1% of the time
where the time goes in v20:
time: 165 us
  Pallas kernels  144 us (87%)
  matrix products  8.44 us (5%)
  other arithmetic  4.9 us (3%)
  local copies, waits for them, and re-layouts  4.31 us (3%)
  starting transfers between devices  1.89 us (1%)
    pallas_call x1, Pallas kernels, combine_and_scatter(): pl.pallas_call(functools.partial(combine_scatter_kernel, blocks), out_sha...  54.2 us
    pallas_call x1, Pallas kernels, gather_all(): pl.pallas_call(functools.partial(gather_kernel, n_group, n_expert, q_in.s...  47 us
    pallas_call x2, Pallas kernels, scatter_blocks(): pl.pallas_call(functools.partial(scatter_kernel, n_expert), out_shape=jax...  21.8 us
    pallas_call x2, Pallas kernels, prep(): pl.pallas_call(functools.partial(prep_kernel, query_width, for_queries),...  12.1 us
    pallas_call x1, Pallas kernels, attention(): pl.pallas_call(functools.partial(attention_kernel, scale, width // depth)...  8.6 us
    dot_general x1, matrix products, per_device(): jnp.einsum('jcd,df->jcf', slot_items, gateup_here, preferred_element_type...  4.15 us
  transfers between devices with their start and end apart: 1, of which 1 were waited for; matrix products, arithmetic and copies ran while one was open for 2% of the time, Pallas kernels for 4%

profile of v20, /device:TPU:1, one launch (start us, length us, event | category | flops | bytes accessed | tf_op | source)
XLA Modules:
  0.0 164.8 jit_solution(17090848509219958747)
XLA Ops:
  0.6 0.0 copy-start
  0.6 47.0 %shard_map.149 = (bf16[16,128,512]{2,1,0:T(8,128)(2,1)}, bf16[16,256,128]{2,1,0:T(8,128)(2,1)}, bf16[16,64,2048]{2,1,0:T(8,128)(2,1)}) custom-call(f32[128,256]{1,0:T(8,128)} %q_in.1, f32[2,128,512]{2,1,0:T(8,128)} %kv_in.1, f32[256,128]{1,0:T(8,128)} %o_in.1, bf16[64,2048]{1,0:T(8,128)(2,1)} %h_in.1, f32[1,2048]{1,0:T(1,128)} %bitcast.34), custom_call_target="tpu_custom_call" | custom-call | tf_op jit(solution)/shard_map/pallas_call | solution.py:176
  47.7 0.0 copy-start.3
  47.7 0.0 copy-start.4
  47.7 6.3 %shard_map.151.own_ref = bf16[2,1024,128]{2,1,0:T(8,128)(2,1)} custom-call(bf16[1024,2048]{1,0:T(8,128)(2,1)} %bitcast.30, bf16[2048,512]{1,0:T(8,128)(2,1)} %bitcast.32, f32[2048,128]{1,0:T(8,128)} %constant.45.clone.table_ref, f32[1,128]{1,0:T(1,128)} %bitcast.35), custom_call_target="tpu_custom_call" | custom-call | flops 1073741824 | bytes 5767168 | tf_op jit(solution)/shard_map/pallas_call | solution.py:597
  53.9 1.9 %collective-permute-start = (bf16[2,1024,128]{2,1,0:T(8,128)(2,1)}, bf16[2,1024,128]{2,1,0:T(8,128)(2,1)}, u32[]{:S(2)}, u32[]{:S(2)}) collective-permute-start(bf16[2,1024,128]{2,1,0:T(8,128)(2,1)} %shard_map.151.own_ref), channel_id=1, source_target_pairs={{0,16},{16,0},{32,48},{48,32},{64,80},{80,64},{96,112},{112,96},{1... | collective-permute-start | bytes 1572872 | tf_op jit(solution)/shard_map/ppermute | solution.py:30
  55.8 0.0 copy-done.3
  55.8 0.1 copy.21
  55.9 0.1 select_reduce_fusion.2
  56.0 0.1 fusion.29
  56.2 0.1 fusion.20
  56.3 0.1 reduce_window_sum.11
  56.3 0.2 select_reduce_fusion.1
  56.5 0.0 copy-done.4
  56.6 0.6 fusion.27
  57.2 5.8 %shard_map.150.q_ref = bf16[1024,256]{1,0:T(8,128)(2,1)} custom-call(bf16[1024,2048]{1,0:T(8,128)(2,1)} %bitcast.31, bf16[2048,512]{1,0:T(8,128)(2,1)} %bitcast.33, f32[2048,128]{1,0:T(8,128)} %constant.45.clone.table_ref, f32[1,128]{1,0:T(1,128)} %bitcast.36), custom_call_target="tpu_custom_call" | custom-call | flops 1073741824 | bytes 5767168 | tf_op jit(solution)/shard_map/pallas_call | solution.py:597
  63.0 2.4 %copy_bitcast_fusion.weight_ref = bf16[256,2048]{1,0:T(8,128)(2,1)} fusion(bf16[16,256,128]{2,1,0:T(8,128)(2,1)} %get-tuple-element.7), kind=kLoop, calls=%fused_computation.8 | loop fusion | bytes 2097152 | tf_op jit(solution)/shard_map/reshape | solution.py:674
  65.4 0.7 collective-permute-done.far_ref
  66.1 8.6 %shard_map.152.attended_ref = bf16[1024,256]{1,0:T(8,128)(2,1)} custom-call(bf16[1024,256]{1,0:T(8,128)(2,1)} %shard_map.150.q_ref, bf16[2,1024,128]{2,1,0:T(8,128)(2,1)} %shard_map.151.own_ref, bf16[2,1024,128]{2,1,0:T(8,128)(2,1)} %collective-permute-done.far_ref, s32[1,1]{1,0:T(1,128)} %bitcast.5.length_ref), custom_call_target="tpu_custom_call" | custom-call | flops 2147483648 | bytes 2097152 | tf_op jit(solution)/shard_map/pallas_call | solution.py:502
  74.7 0.0 copy-start.2
  74.7 54.2 %shard_map.153 = bf16[8,64,2048]{2,1,0:T(8,128)(2,1)} custom-call(bf16[1024,256]{1,0:T(8,128)(2,1)} %shard_map.152.attended_ref, bf16[256,2048]{1,0:T(8,128)(2,1)} %copy_bitcast_fusion.weight_ref), custom_call_target="tpu_custom_call" | custom-call | tf_op jit(solution)/shard_map/pallas_call | solution.py:315
  128.9 2.0 %convert_reduce_fusion = f32[64,2048]{1,0:T(8,128)S(1)} fusion(bf16[8,64,2048]{2,1,0:T(8,128)(2,1)} %shard_map.153), kind=kLoop, calls=%fused_computation.2 | loop fusion | flops 1966080 | bytes 2621440 | tf_op jit(solution)/shard_map/reduce_sum | solution.py:676
  130.9 1.1 fusion.6
  132.0 0.0 copy-start.1
  132.0 0.0 copy-done.2
  132.1 0.3 fusion.9
  132.4 0.9 copy.37.part
  133.3 13.0 %shard_map.154 = bf16[16,4,2048]{2,1,0:T(4,128)(2,1)} custom-call(bf16[16,4,2048]{2,1,0:T(4,128)(2,1)} %copy.37.part), custom_call_target="tpu_custom_call" | custom-call | tf_op jit(solution)/shard_map/pallas_call | solution.py:442
  146.3 4.1 %fusion = f32[16,4,1536]{2,0,1:T(8,128)S(1)} fusion(bf16[1,2048,1536]{2,1,0:T(8,128)(2,1)} %param.24, bf16[16,4,2048]{2,1,0:T(4,128)(2,1)} %shard_map.154), kind=kOutput, calls=%fused_computation | convolution fusion | flops 402653184 | bytes 6946816 | tf_op jit(solution)/shard_map/jcd,df->jcf/dot_general | solution.py:705
  150.4 0.0 copy-done
  150.5 0.7 fusion.2
  151.1 0.9 copy.36.part
  152.0 8.8 %shard_map.155 = bf16[16,4,2048]{2,1,0:T(4,128)(2,1)} custom-call(bf16[16,4,2048]{2,1,0:T(4,128)(2,1)} %copy.36.part), custom_call_target="tpu_custom_call" | custom-call | tf_op jit(solution)/shard_map/pallas_call | solution.py:442
  160.9 0.0 copy-done.1
  160.9 1.3 fusion.17
  162.2 0.2 select_reduce_fusion
  162.4 0.1 exponential_reduce_fusion
  162.6 0.2 select_reduce_fusion.3
  162.7 2.0 %fusion.5 = bf16[64,2048]{1,0:T(8,128)(2,1)} fusion(bf16[16,4,2048]{2,1,0:T(4,128)(2,1)} %shard_map.155, f32[64]{0:T(128)S(1)} %select_reduce_fusion.3, s32[64]{0:T(128)S(1)} %add_add_fusion, s32[16,4]{0,1:T(4,128)S(1)} %multiply_add_fusion, pred[64]{0:T(512)(128)(4,1)S(1)} %fusion.29), kind=kOutput, calls=%fused_computation.7 | convolution fusion | flops 17047552 | bytes 525120 | tf_op jit(solution)/shard_map/jct,jcd->td/dot_general | solution.py:713
  (3 shorter events, 0.0 us)
Async XLA Ops:
  0.6 149.8 %copy-start = (bf16[1,768,2048]{2,1,0:T(8,128)(2,1)S(1)}, bf16[1,768,2048]{2,1,0:T(8,128)(2,1)}, u32[]{:S(2)}) copy-start(bf16[1,768,2048]{2,1,0:T(8,128)(2,1)} %param.25) | copy-start | bytes 9437188
  47.7 8.2 %copy-start.3 = (s32[64,8]{0,1:T(8,128)S(1)}, s32[64,8]{0,1:T(8,128)}, u32[]{:S(2)}) copy-start(s32[64,8]{0,1:T(8,128)} %param.26) | copy-start | bytes 6148
  47.7 8.9 %copy-start.4 = (s32[8]{0:T(128)S(1)}, s32[8]{0:T(128)}, u32[]{:S(2)}) copy-start(s32[8]{0:T(128)} %param.22) | copy-start | bytes 100
  53.9 12.1 %collective-permute-start = (bf16[2,1024,128]{2,1,0:T(8,128)(2,1)}, bf16[2,1024,128]{2,1,0:T(8,128)(2,1)}, u32[]{:S(2)}, u32[]{:S(2)}) collective-permute-start(bf16[2,1024,128]{2,1,0:T(8,128)(2,1)} %shard_map.151.own_ref), channel_id=1, source_target_pairs={{0,16},{16,0},{32,48},{48,32},{64,80},{80,64},{96,112},{112,96},{1... | collective-permute-start | bytes 1572872 | tf_op jit(solution)/shard_map/ppermute | solution.py:30
  74.7 57.4 %copy-start.2 = (f32[2048]{0:T(1024)S(1)}, f32[2048]{0:T(1024)}, u32[]{:S(2)}) copy-start(f32[2048]{0:T(1024)} %param.16) | copy-start | bytes 24580
  132.0 28.9 %copy-start.1 = (bf16[64,2048]{1,0:T(8,128)(2,1)}, bf16[64,2048]{1,0:T(8,128)(2,1)S(1)}, u32[]{:S(2)}) copy-start(bf16[64,2048]{1,0:T(8,128)(2,1)S(1)} %get-tuple-element.9) | copy-start | bytes 786436
